TPU v7x, 32 devices: a whole 2x2x4 slice. The times are simulated.
32 devices in a mesh: grp: 8 (over y, x, core), seq: 4 (over z).
Axes of the slice: x: 2, y: 2, z: 4, core: 2. Of those that a mesh axis runs over, the one named last changes fastest.
Arguments:
- tokens: bfloat16 [8192, 512], P(('grp', 'seq')), parts along dimension 0, may hold values from -6 to 6
- group_pos: int32 [2048], P('grp'), parts along dimension 0, may hold values from 0 to 1023, as said below
- log_decay: float32 [8192, 16], P(('grp', 'seq')), parts along dimension 0, may hold values from -1 to 0, as said below
- in_weight: bfloat16 [512, 2176], replicated, may hold values from -0.25 to 0.25
- norm_gain: float32 [1024], replicated, may hold values from 0.1 to 1.9
- out_weight: bfloat16 [1024, 512], replicated, may hold values from -0.1875 to 0.1875
- inner_gain: float32 [512], replicated, may hold values from 0.1 to 1.9
- qkv_weight: bfloat16 [4, 512, 192], P('seq'), may hold values from -1 to 1
- attn_out: bfloat16 [4, 64, 512], P('seq'), may hold values from -0.375 to 0.375
Outputs:
- result: bfloat16 [8192, 512], P(('grp', 'seq')), parts along dimension 0
There are 8 independent parts, one for each index of `grp`. A program takes and returns all parts, laid end to end along the dimension named above; an argument that names none is the same for every part. Nothing has to cross between parts.
Inputs may be any that keep to these rules, and one draw needn't show every extreme that they name: `group_pos`: strictly increasing. Each device's 256 positions hold at least one group start and at most 128; some device holds exactly 128. `log_decay`: negative at every position.
All inputs are finite; a program needn't handle non-finite values.
Results may differ from a plain program's by a relative error of at most 0.0061.
Values may be sent and summed in bfloat16 or wider, within the bound.
No kernel may reach another device: no remote copies, remote signals or barrier semaphores. Data moves between devices by JAX's collectives and lax.ppermute only.
A program may use at most 64 MiB of HBM per device.

v0:
```python
import jax
import jax.numpy as jnp
from jax import lax
from jax.sharding import PartitionSpec as P


def entering(value, axis, join, neutral):
    count, mine = (lax.axis_size(axis), lax.axis_index(axis))
    pieces = jax.tree.map(lambda part: lax.all_gather(part, axis), value)
    subtotal = jax.tree.map(
        lambda part, zero: jnp.full_like(part, 0) + jnp.asarray(zero, part.dtype), value, neutral
    )

    def turn(position, subtotal):
        longer = join(subtotal, jax.tree.map(lambda part: part[position], pieces))
        return jax.tree.map(lambda new, old: jnp.where(position < mine, new, old), longer, subtotal)

    return lax.fori_loop(0, count - 1, turn, subtotal)


def rms_norm(values, gain):
    return values * lax.rsqrt(jnp.mean(values * values, axis=-1, keepdims=True) + 1e-05) * gain


def attend(rows, w_qkv, index, valid):
    head_dim = w_qkv.shape[1] // 3
    qkv = jnp.dot(rows, w_qkv, preferred_element_type=jnp.float32).astype(jnp.bfloat16)
    query = qkv[:, :head_dim]
    keys = qkv[:, head_dim : 2 * head_dim]
    values = qkv[:, 2 * head_dim :]
    count = rows.shape[0]
    block = min(512, count)

    def one_block(start):
        query_block = lax.dynamic_slice_in_dim(query, start, block, 0)
        index_block = lax.dynamic_slice_in_dim(index, start, block, 0)
        scores = jnp.dot(query_block, keys.T, preferred_element_type=jnp.float32) * head_dim ** (
            -0.5
        )
        allowed = (index[None, :] <= index_block[:, None]) & valid[None, :]
        scores = jnp.where(allowed, scores, -jnp.inf)
        top = jnp.max(scores, axis=1, keepdims=True)
        expo = jnp.exp(scores - top)
        probs = (expo / jnp.sum(expo, axis=1, keepdims=True)).astype(jnp.bfloat16)
        return jnp.dot(probs, values, preferred_element_type=jnp.float32).astype(jnp.bfloat16)

    starts = jnp.arange(count // block, dtype=jnp.int32) * block
    return lax.map(one_block, starts).reshape(count, head_dim)


def shards(
    tokens, group_pos, log_decay, in_weight, norm_gain, out_weight, inner_gain, qkv_weight, attn_out
):
    highest = lax.Precision.HIGHEST
    length = tokens.shape[0]
    heads = log_decay.shape[1]
    width = out_weight.shape[0]
    model_width = out_weight.shape[1]
    head_size = width // heads
    state_dim = (in_weight.shape[1] - 2 * width) // 2
    proj = jnp.dot(tokens, in_weight, preferred_element_type=jnp.float32).astype(jnp.bfloat16)
    xs = proj[:, :width].astype(jnp.float32).reshape(length, heads, head_size)
    gate = proj[:, width : 2 * width].astype(jnp.float32)
    bmat = proj[:, 2 * width : 2 * width + state_dim].astype(jnp.float32)
    cmat = proj[:, 2 * width + state_dim :].astype(jnp.float32)
    cumul = jnp.cumsum(log_decay, axis=0)
    differ = cumul.T[:, :, None] - cumul.T[:, None, :]
    lower = jnp.arange(length)[:, None] >= jnp.arange(length)[None, :]
    decays = jnp.exp(jnp.where(lower[None], differ, -jnp.inf))
    intersections = jnp.dot(cmat, bmat.T, precision=highest)
    within = jnp.einsum("hij,jhp->ihp", decays * intersections[None], xs, precision=highest)
    tails = jnp.exp(cumul[-1][None, :] - cumul)
    local_state = jnp.einsum("jh,jhp,jn->hpn", tails, xs, bmat, precision=highest)
    total_decay = jnp.exp(cumul[-1])

    def link(earlier, later):
        return (earlier[0] * later[0], later[0][:, None, None] * earlier[1] + later[1])

    identity = (jnp.ones_like(total_decay), jnp.zeros_like(local_state))
    _, state_in = entering((total_decay, local_state), "seq", link, identity)
    carried = jnp.einsum("ih,in,hpn->ihp", jnp.exp(cumul), cmat, state_in, precision=highest)
    gated = (within + carried).reshape(length, width) * jax.nn.silu(gate)
    normed = rms_norm(gated, norm_gain).astype(jnp.bfloat16)
    hidden = (
        tokens.astype(jnp.float32) + jnp.dot(normed, out_weight, preferred_element_type=jnp.float32)
    ).astype(jnp.bfloat16)
    position = lax.axis_index("seq")
    devices = lax.axis_size("seq")
    most = length // 2
    groups = group_pos.shape[0]
    starts = jnp.arange(devices, dtype=jnp.int32) * length
    before = jnp.sum((group_pos[None, :] < starts[:, None]).astype(jnp.int32), axis=1)
    upto = jnp.sum((group_pos[None, :] < (starts + length)[:, None]).astype(jnp.int32), axis=1)
    counts = upto - before
    slots = jnp.arange(most, dtype=jnp.int32)
    picks = jnp.clip(before[position] + slots, 0, groups - 1)
    valid_here = slots < counts[position]
    local_pos = group_pos[picks] - position * length
    placing = (
        (local_pos[:, None] == jnp.arange(length, dtype=jnp.int32)[None, :]) & valid_here[:, None]
    ).astype(jnp.float32)
    rows = jnp.dot(placing.astype(jnp.bfloat16), hidden, preferred_element_type=jnp.float32)
    rows_n = rms_norm(rows, inner_gain).astype(jnp.bfloat16)
    gathered = lax.all_gather(rows_n, "seq", axis=0, tiled=True)
    slot_group = (before[:, None] + slots[None, :]).reshape(-1)
    slot_valid = (slots[None, :] < counts[:, None]).reshape(-1)
    w_qkv = qkv_weight[0]
    heads_out = attend(gathered, w_qkv, slot_group, slot_valid)
    full_out = lax.all_gather(attn_out, "seq", axis=0, tiled=True)
    mine = lax.all_to_all(heads_out[:, None, :], "seq", split_axis=0, concat_axis=1, tiled=True)
    back = jnp.dot(
        mine.reshape(most, -1),
        full_out.reshape(-1, model_width),
        preferred_element_type=jnp.float32,
    )
    placed = jnp.dot(placing.T, back, precision=highest)
    return (hidden.astype(jnp.float32) + placed).astype(jnp.bfloat16)


def solution(mesh):
    in_specs = (
        P(("grp", "seq"), None),
        P("grp"),
        P(("grp", "seq"), None),
        P(),
        P(),
        P(),
        P(),
        P("seq", None, None),
        P("seq", None, None),
    )
    out_specs = P(("grp", "seq"), None)
    return jax.shard_map(shards, mesh=mesh, in_specs=in_specs, out_specs=out_specs, check_vma=False)
```

profile of v0, /device:TPU:0, one launch (start us, length us, event | category | flops | bytes accessed | tf_op | source)
XLA Modules:
  0.0 115.9 jit_solution(2016591434502746078)
XLA Ops:
  6.5 0.9 copy_bitcast_fusion.1
  8.6 1.9 %convolution_convert_fusion = bf16[256,2176]{0,1:T(8,128)(2,1)S(1)} fusion(bf16[256,512]{1,0:T(8,128)(2,1)} %param.11, bf16[512,2176]{1,0:T(8,128)(2,1)S(1)} %copy-done), kind=kOutput, calls=%fused_computation.9 | convolution fusion | flops 570982400 | bytes 3604480 | tf_op jit(solution)/shard_map/dot_general | solution.py:61
  10.6 1.0 copy-done.2
  11.5 1.5 %fusion.23 = f32[16,64,64]{2,1,0:T(8,128)} fusion(bf16[256,16,64]{0,2,1:T(8,128)(2,1)S(1)} %bitcast.77, f32[256,16]{0,1:T(8,128)S(1)} %get-tuple-element.159, bf16[256,2176]{0,1:T(8,128)(2,1)S(1)} %convolution_convert_fusion), kind=kOutput, calls=%fused_computation.37 | convolution fusion | flops 201850880 | bytes 835584 | tf_op jit(solution)/shard_map/jh,jhp,jn->hpn/dot_general | solution.py:73
  13.8 0.7 fusion.50
  15.8 1.3 %gather_fusion = s32[128]{0:T(128)S(1)} fusion(s32[256]{0:T(256)S(1)} %copy-done.1, s32[1024]{0:T(1024)S(1)} %pad_clamp_fusion), kind=kCustom, calls=%fused_computation | custom fusion | bytes 1536 | tf_op jit(solution)/shard_map/gather | solution.py:98
  17.1 12.7 %all-gather.1 = f32[4,1,16]{2,1,0:T(1,128)S(1)} all-gather(f32[1,1,16]{2,1,0:T(1,128)S(1)} %bitcast.82), channel_id=1, replica_groups=mesh['grp'=8,'seq'=4] {'seq'}, dimensions={0}, use_global_device_ids=true | all-gather | bytes 320 | tf_op jit(solution)/shard_map/all_gather | solution.py:9
  29.9 0.8 slice_convert_fusion
  30.7 1.0 fusion.46
  31.7 4.1 %fusion.11 = f32[256,16,64]{0,2,1:T(8,128)} fusion(bf16[256,16,64]{0,2,1:T(8,128)(2,1)S(1)} %bitcast.78, f32[256,256]{1,0:T(8,128)S(1)} %fusion.46, f32[16,256]{1,0:T(8,128)S(1)} %get-tuple-element.161, pred[256,256]{1,0:T(8,128)(4,1)S(1)} %iota_compare_fusion), kind=kOutput, calls=%fused_computation.15 | convolution fusion | flops 808452096 | bytes 1916928 | tf_op jit(solution)/shard_map/hij,jhp->ihp/dot_general | solution.py:71
  35.7 25.8 %all-gather.4.cloned.1.call-done = f32[64,64,64]{2,1,0:T(8,128)} async-done(((f32[16,64,64]{2,1,0:T(8,128)}), f32[64,64,64]{2,1,0:T(8,128)}) %all-gather.4.cloned.1.call-update) | async-done | bytes 1048592 | tf_op jit(solution)/shard_map/all_gather | solution.py:9
  61.6 3.6 %while.18 = (s32[]{:T(128)}, f32[16,64,64]{2,1,0:T(8,128)S(1)}, s32[]{:T(128)}, f32[4,16]{1,0:T(4,128)S(1)}, f32[4,16,64,64]{3,2,1,0:T(8,128)}, /*index=5*/s32[]{:T(128)}, s32[]{:T(128)}) while((s32[]{:T(128)}, f32[16,64,64]{2,1,0:T(8,128)S(1)}, s32[]{:T(128)}, f32[4,16]{1,0:T(4,128)S(1)}, f32[4,16,64,64]{3,2,1,0:T(8,128)}, ...), condition=%wide.region_3.4_spmd.clone, body=%wide.region_2.3_spmd.clone.sunk | while | flops 262148 | bytes 786729 | solution.py:18
  61.6 1.2 %fusion.68 = f32[16,64,64]{2,1,0:T(8,128)S(1)} fusion(f32[4,16,64,64]{3,2,1,0:T(8,128)} %get-tuple-element.217, s32[]{:T(128)} %get-tuple-element.206, f32[16,64,64]{2,1,0:T(8,128)S(1)} %get-tuple-element.207, f32[16]{0:T(128)S(1)} %dynamic-slice_bitcast_fusion.2, pred[]{:T(512)S(6)} %compare.3, pred[]{:T(512)S(6)} %lt.120), kind=kLoop, calls=%fused_computation.2.clone.1 | loop fusion | flops 262144 | bytes 786502 | tf_op jit(solution)/shard_map/while/body/eval_jaxpr/jit(_where)/select_n | solution.py:16
  62.8 1.2 %fusion.68 = f32[16,64,64]{2,1,0:T(8,128)S(1)} fusion(f32[4,16,64,64]{3,2,1,0:T(8,128)} %get-tuple-element.217, s32[]{:T(128)} %get-tuple-element.206, f32[16,64,64]{2,1,0:T(8,128)S(1)} %get-tuple-element.207, f32[16]{0:T(128)S(1)} %dynamic-slice_bitcast_fusion.2, pred[]{:T(512)S(6)} %compare.3, pred[]{:T(512)S(6)} %lt.120), kind=kLoop, calls=%fused_computation.2.clone.1 | loop fusion | flops 262144 | bytes 786502 | tf_op jit(solution)/shard_map/while/body/eval_jaxpr/jit(_where)/select_n | solution.py:16
  64.0 1.2 %fusion.68 = f32[16,64,64]{2,1,0:T(8,128)S(1)} fusion(f32[4,16,64,64]{3,2,1,0:T(8,128)} %get-tuple-element.217, s32[]{:T(128)} %get-tuple-element.206, f32[16,64,64]{2,1,0:T(8,128)S(1)} %get-tuple-element.207, f32[16]{0:T(128)S(1)} %dynamic-slice_bitcast_fusion.2, pred[]{:T(512)S(6)} %compare.3, pred[]{:T(512)S(6)} %lt.120), kind=kLoop, calls=%fused_computation.2.clone.1 | loop fusion | flops 262144 | bytes 786502 | tf_op jit(solution)/shard_map/while/body/eval_jaxpr/jit(_where)/select_n | solution.py:16
  65.2 2.4 %fusion.15 = f32[256,16,64]{0,2,1:T(8,128)S(1)} fusion(f32[256,16,64]{0,2,1:T(8,128)} %fusion.11, f32[16,64,64]{2,1,0:T(8,128)S(1)} %get-tuple-element.123, f32[256,16]{0,1:T(8,128)S(1)} %get-tuple-element.158, f32[256,64]{0,1:T(8,128)S(1)} %slice_convert_fusion), kind=kOutput, calls=%fused_computation.19 | convolution fusion | flops 201850880 | bytes 2441216 | tf_op jit(solution)/shard_map/ih,in,hpn->ihp/dot_general | solution.py:81
  67.6 1.4 %multiply_reduce_fusion = (f32[256]{0:T(256)S(1)}, f32[256,1024]{0,1:T(8,128)S(1)}) fusion(bf16[256,2176]{0,1:T(8,128)(2,1)} %copy-done.2, f32[256,16,64]{0,2,1:T(8,128)S(1)} %fusion.15), kind=kLoop, calls=%fused_computation.36 | loop fusion | flops 2096896 | bytes 2622464 | tf_op jit(solution)/shard_map/reduce_sum | solution.py:22
  69.1 0.8 fusion.16
  70.3 15.6 %all_gather.19 = bf16[512,512]{1,0:T(8,128)(2,1)S(1)} all-gather(bf16[128,512]{1,0:T(8,128)(2,1)S(1)} %multiply_convert_fusion.2), channel_id=1, replica_groups=mesh['grp'=8,'seq'=4] {'seq'}, dimensions={0}, use_global_device_ids=true | all-gather | bytes 655360 | tf_op jit(solution)/shard_map/all_gather | solution.py:104
  87.8 0.7 reduce.6
  88.6 0.8 reshape.183
  89.4 3.3 %all-to-all-start = ((bf16[4,2,4096]{2,1,0:T(2,128)(2,1)}), bf16[4,2,4096]{2,1,0:T(2,128)(2,1)S(1)}, u32[]{:S(2)}, u32[]{:S(2)}) async-start(bf16[4,2,4096]{2,1,0:T(2,128)(2,1)} %reshape.183), calls=%async_computation | async-start | bytes 131072 | tf_op jit(solution)/shard_map/all_to_all | solution.py:110
  92.7 14.6 %all_gather.20 = bf16[4,64,512]{2,1,0:T(8,128)(2,1)S(1)} all-gather(bf16[1,64,512]{2,1,0:T(8,128)(2,1)S(1)} %copy-done.6), channel_id=1, replica_groups=mesh['grp'=8,'seq'=4] {'seq'}, dimensions={0}, use_global_device_ids=true | all-gather | bytes 327680 | tf_op jit(solution)/shard_map/all_gather | solution.py:109
  107.8 1.2 %fusion.17 = bf16[256,512]{1,0:T(8,128)(2,1)} fusion(f32[128,512]{1,0:T(8,128)S(1)} %fusion.55, bf16[256,512]{1,0:T(8,128)(2,1)S(1)} %fusion.16, s32[128]{0:T(128)S(1)} %broadcast_subtract_fusion, pred[128]{0:T(512)(128)(4,1)S(1)} %iota_compare_fusion.3), kind=kOutput, calls=%fused_computation.25 | convolution fusion | flops 201785344 | bytes 787072 | tf_op jit(solution)/shard_map/dot_general | solution.py:116
  (58 shorter events, 6.3 us)
Async XLA Ops:
  6.5 2.0 %copy-start = (bf16[512,2176]{1,0:T(8,128)(2,1)S(1)}, bf16[512,2176]{1,0:T(8,128)(2,1)}, u32[]{:S(2)}) copy-start(bf16[512,2176]{1,0:T(8,128)(2,1)} %param.14) | copy-start | bytes 6684676
  6.5 55.0 %all-gather.4.cloned.1.call-start = ((), (), s32[]{:S(2)}) async-start(), calls=%async_computation.1 | async-start | bytes 2621440 | tf_op jit(solution)/shard_map/all_gather | solution.py:9
  10.5 1.0 copy-start.2
  10.5 2.5 %copy-start.1 = (s32[256]{0:T(256)S(1)}, s32[256]{0:T(256)}, u32[]{:S(2)}) copy-start(s32[256]{0:T(256)} %param.12) | copy-start | bytes 3076
  65.2 3.9 %copy-start.3 = (bf16[256,512]{1,0:T(8,128)(2,1)S(1)}, bf16[256,512]{1,0:T(8,128)(2,1)}, u32[]{:S(2)}) copy-start(bf16[256,512]{1,0:T(8,128)(2,1)} %param.11) | copy-start | bytes 786436
  65.2 3.9 %copy-start.4 = (bf16[1024,512]{1,0:T(8,128)(2,1)S(1)}, bf16[1024,512]{1,0:T(8,128)(2,1)}, u32[]{:S(2)}) copy-start(bf16[1024,512]{1,0:T(8,128)(2,1)} %param.16) | copy-start | bytes 3145732
  65.2 3.9 %copy-start.7 = (f32[1024]{0:T(1024)S(1)}, f32[1024]{0:T(1024)}, u32[]{:S(2)}) copy-start(f32[1024]{0:T(1024)} %param.15) | copy-start | bytes 12292
  69.0 1.2 %copy-start.8 = (f32[512]{0:T(512)S(1)}, f32[512]{0:T(512)}, u32[]{:S(2)}) copy-start(f32[512]{0:T(512)} %param.17) | copy-start | bytes 6148
  69.0 16.9 %copy-start.5 = (bf16[1,512,192]{1,2,0:T(8,128)(2,1)S(1)}, bf16[1,512,192]{1,2,0:T(8,128)(2,1)}, u32[]{:S(2)}) copy-start(bf16[1,512,192]{1,2,0:T(8,128)(2,1)} %param.18) | copy-start | bytes 589828
  86.9 5.7 %copy-start.6 = (bf16[1,64,512]{2,1,0:T(8,128)(2,1)S(1)}, bf16[1,64,512]{2,1,0:T(8,128)(2,1)}, u32[]{:S(2)}) copy-start(bf16[1,64,512]{2,1,0:T(8,128)(2,1)} %param.19) | copy-start | bytes 196612
  89.4 17.9 %all-to-all-start = ((bf16[4,2,4096]{2,1,0:T(2,128)(2,1)}), bf16[4,2,4096]{2,1,0:T(2,128)(2,1)S(1)}, u32[]{:S(2)}, u32[]{:S(2)}) async-start(bf16[4,2,4096]{2,1,0:T(2,128)(2,1)} %reshape.183), calls=%async_computation | async-start | bytes 131072 | tf_op jit(solution)/shard_map/all_to_all | solution.py:110
Sparse Core Ops, SparseCore 0:
  13.1 48.3 all-gather.3
where the time goes:
time: 117 us; the launch traced here: 116 us
  blocking collectives  42.9 us (37%)
  waiting for transfers between devices  25.9 us (22%)
  matrix products  14.4 us (12%)
  between operations  13.7 us (12%)
  other arithmetic  9.12 us (8%)
  local copies, waits for them, and re-layouts  6.46 us (6%)
  starting transfers between devices  3.29 us (3%)
    all_gather x1, waiting for transfers between devices, entering(): pieces = jax.tree.map(lambda part: lax.all_gather(part, axis), value)  25.8 us
    all_gather x1, blocking collectives, shards(): gathered = lax.all_gather(rows_n, 'seq', axis=0, tiled=True)  15.6 us
    all_gather x1, blocking collectives, shards(): full_out = lax.all_gather(attn_out, 'seq', axis=0, tiled=True)  14.6 us
    all_gather x1, blocking collectives, entering(): pieces = jax.tree.map(lambda part: lax.all_gather(part, axis), value)  12.7 us
    dot_general x1, matrix products, shards(): jnp.einsum('hij,jhp->ihp', decays * intersections[None], xs, precision=hi...  4.07 us
    select_n x3, other arithmetic, turn(): jnp.where(position < mine, new, old)  3.51 us
    all_to_all x1, starting transfers between devices, shards(): lax.all_to_all(heads_out[:, None, :], 'seq', split_axis=0, concat_axis=1,...  3.28 us
    dot_general x1, matrix products, shards(): jnp.einsum('ih,in,hpn->ihp', jnp.exp(cumul), cmat, state_in, precision=hi...  2.42 us
  transfers between devices with their start and end apart: 2, of which 1 were waited for; matrix products, arithmetic and copies ran while one was open for 9% of the time, Pallas kernels for 0%

commit v1 on v0

v1 whole, which is shorter than its diff:
```python
import functools

import jax
import jax.numpy as jnp
from jax import lax
from jax.experimental import pallas as pl
from jax.experimental.pallas import tpu as pltpu
from jax.sharding import PartitionSpec as P

F32 = jnp.float32
BF16 = jnp.bfloat16
EPS = 1e-05
VMEM = pl.BlockSpec(memory_space=pltpu.VMEM)
ANY = pl.BlockSpec(memory_space=pl.ANY)


def dot(a, b):
    return jnp.dot(a, b, preferred_element_type=F32)


def dot_rows(a, b):
    return lax.dot_general(a, b, (((0,), (0,)), ((), ())), preferred_element_type=F32)


def dot_lanes(a, b):
    return lax.dot_general(a, b, (((1,), (1,)), ((), ())), preferred_element_type=F32)


def iota(shape, axis):
    return lax.broadcasted_iota(jnp.int32, shape, axis)


def terms(value, count):
    out = []
    for _ in range(count):
        term = value.astype(BF16)
        out.append(term)
        value = value - term.astype(F32)
    return out


def spread(value, heads, width, count):
    size = width // heads
    row = iota((heads, width), 0)
    lane = iota((heads, width), 1)
    pick = ((lane >= row * size) & (lane < (row + 1) * size)).astype(BF16)
    return sum(dot(term, pick) for term in terms(value, count))


def weight_copies(weight, buffer, sems, start, step):
    count = buffer.shape[0]
    return [
        pltpu.make_async_copy(
            weight.at[:, pl.ds(start + i * step, step)], buffer.at[i], sems.at[i]
        )
        for i in range(count)
    ]


def front_kernel(
    split, tokens, decay, weight, qkv, attn_out,
    xs, bc, local, first, total, cumul, piece,
    xs_buffer, bc_buffer, xs_sems, bc_sems,
):
    length, heads = decay.shape
    width = xs.shape[1]
    states = local.shape[0]
    step = xs_buffer.shape[2]
    bc_copy = weight_copies(weight, bc_buffer, bc_sems, 2 * width, 2 * states)
    xs_copy = weight_copies(weight, xs_buffer, xs_sems, 0, step)
    for copy in bc_copy + xs_copy:
        copy.start()

    lower = (iota((length, length), 0) >= iota((length, length), 1)).astype(BF16)
    cum = sum(dot(lower, term) for term in terms(decay[...], 3))
    cumul[...] = cum
    last = cum[length - 1 :, :]
    tails = jnp.exp(last - cum)
    total[...] = spread(jnp.broadcast_to(jnp.exp(last), (8, heads)), heads, width, 3)
    tails_wide = spread(tails, heads, width, 2)

    mine = lax.rem(lax.axis_index("grp"), split)
    rows = qkv.shape[1] // split
    part = qkv[0, pl.ds(pl.multiple_of(mine * rows, rows), rows), :]
    two = 2 * part.shape[1] // 3
    value = part[:, two:]
    half = rows // 2
    piece[:rows, :] = part[:, :two]
    piece[rows : rows + half, :] = jnp.concatenate([value[:half], value[half:]], axis=1)
    few = attn_out.shape[1] // split
    back = attn_out[0, pl.ds(pl.multiple_of(mine * few, few), few), :]
    for i in range(back.shape[1] // two):
        at = rows + half + i * few
        piece[at : at + few, :] = back[:, i * two : (i + 1) * two]

    bc_copy[0].wait()
    ins = tokens[...]
    both = dot(ins, bc_buffer[0]).astype(BF16)
    bc[...] = both
    for i, copy in enumerate(xs_copy):
        lanes = slice(i * step, (i + 1) * step)
        copy.wait()
        block = dot(ins, xs_buffer[i]).astype(BF16)
        xs[:, lanes] = block
        scaled = (block.astype(F32) * tails_wide[:, lanes]).astype(BF16)
        state = dot_rows(both, scaled)[:states]
        local[:, lanes] = state
        first[:, lanes] = state.astype(BF16)


def middle_kernel(
    tokens, decay, weight, cumul, xs, bc, groups,
    within, silu, grown, placing, cmat,
    gate_buffer, gate_sems,
):
    length, heads = decay.shape
    width = xs.shape[1]
    states = bc.shape[1] // 2
    step = gate_buffer.shape[2]
    most = placing.shape[1]
    copies = weight_copies(weight, gate_buffer, gate_sems, width, step)
    for copy in copies:
        copy.start()

    here = lax.axis_index("seq") * length
    count = groups.shape[1]
    position = here + iota((length, count), 0)
    group = jnp.broadcast_to(groups[...], (length, count))
    starts = jnp.sum((group == position).astype(F32), axis=1, keepdims=True)
    ahead = (group < position) & (group >= here)
    rank = jnp.sum(ahead.astype(F32), axis=1, keepdims=True).astype(jnp.int32)
    slot = iota((length, most), 1)
    placing[...] = jnp.where(slot == rank, starts, 0.0).astype(BF16)

    cum = cumul[...]
    upper = (iota((length, length), 0) <= iota((length, length), 1)).astype(BF16)
    cum_t = sum(dot_rows(term, upper) for term in terms(decay[...], 3))
    grown[...] = spread(jnp.exp(cum), heads, width, 2)
    both = bc[...]
    cmat[...] = both[:, states:]
    mixed = dot_lanes(both[:, states:], both[:, :states])

    half = length // 2
    lower = iota((half, half), 0) >= iota((half, half), 1)
    size = width // heads
    pair = 2 * size
    left = iota((half, pair), 1) < size
    for at in range(0, heads, 2):
        lanes = slice(at * size, at * size + pair)
        early, late = xs[:half, lanes], xs[half:, lanes]
        tops, lows = [], []
        for head in (at, at + 1):
            column = cum[:, head : head + 1]
            row = cum_t[head : head + 1, :]
            apart = jnp.where(lower, column[:half] - row[:, :half], -jnp.inf)
            top = (jnp.exp(apart) * mixed[:half, :half]).astype(BF16)
            apart = jnp.where(lower, column[half:] - row[:, half:], -jnp.inf)
            low = (jnp.exp(apart) * mixed[half:, half:]).astype(BF16)
            across = jnp.exp(column[half:] - row[:, :half])
            across = (across * mixed[half:, :half]).astype(BF16)
            tops.append(dot(top, early))
            lows.append(dot(low, late) + dot(across, early))
        within[:half, lanes] = jnp.where(left, tops[0], tops[1])
        within[half:, lanes] = jnp.where(left, lows[0], lows[1])

    ins = tokens[...]
    for i, copy in enumerate(copies):
        copy.wait()
        gate = dot(ins, gate_buffer[i]).astype(BF16).astype(F32)
        silu[:, i * step : (i + 1) * step] = gate / (1.0 + jnp.exp(-gate))


def post_kernel(
    state, within, silu, grown, placing, cmat, gain, out_weight, tokens, inner_gain,
    hidden, rows,
):
    carried = dot(cmat[...], state[...])
    gated = (within[...] + grown[...] * carried) * silu[...]
    scale = lax.rsqrt(jnp.mean(gated * gated, axis=1, keepdims=True) + EPS)
    normed = (gated * scale * gain[...]).astype(BF16)
    mixed = dot(normed, out_weight[...])
    out = (tokens[...].astype(F32) + mixed).astype(BF16)
    hidden[...] = out
    picked = dot_rows(placing[...], out)
    scale = lax.rsqrt(jnp.mean(picked * picked, axis=1, keepdims=True) + EPS)
    rows[...] = (picked * scale * inner_gain[...]).astype(BF16)


def weight_kernel(masks, split, model, head_dim, *refs):
    count = len(masks)
    bundles, (wq, wk, wv, wo) = refs[:count], refs[count:]
    heads = wq.shape[1] // head_dim
    rows = model // split
    half = rows // 2
    few = head_dim // split
    two = 2 * head_dim
    tall = rows + half + few * (model // two)
    mine = lax.rem(lax.axis_index("grp"), split)
    for bundle, mask in zip(bundles, masks):
        for j, bits in enumerate(mask):
            quarter = mine ^ bits
            down = pl.ds(pl.multiple_of(quarter * rows, rows), rows)
            for h in range(heads):
                at = (j * heads + h) * tall
                lanes = slice(h * head_dim, (h + 1) * head_dim)
                both = bundle[at : at + rows, :]
                wq[down, lanes] = both[:, :head_dim]
                wk[down, lanes] = both[:, head_dim:]
                value = bundle[at + rows : at + rows + half, :]
                wv[down, lanes] = jnp.concatenate([value[:, :head_dim], value[:, head_dim:]], axis=0)
                at += rows + half
                start = pl.multiple_of(h * head_dim + quarter * few, few)
                for i in range(model // two):
                    wo[pl.ds(start, few), i * two : (i + 1) * two] = bundle[
                        at + i * few : at + (i + 1) * few, :
                    ]


def attend_kernel(devices, length, *refs):
    rows = refs[:devices]
    wq, wk, wv, wo, hidden, placing, groups, result = refs[devices:]
    most = rows[0].shape[0]
    heads = devices
    head_dim = wq.shape[1] // heads
    me = lax.axis_index("seq")
    own = rows[0][...]
    known = jnp.concatenate([own] + [row[...] for row in rows[1:]], axis=0)
    query = dot(own, wq[...]).astype(BF16)
    keys = dot(known, wk[...]).astype(BF16)
    values = dot(known, wv[...]).astype(BF16)

    slot = iota((most, most), 1)
    allowed = [slot <= iota((most, most), 0)]
    for back in range(1, devices):
        start = (me - back) * length
        inside = (groups[...] >= start) & (groups[...] < start + length)
        count = jnp.sum(inside.astype(F32), axis=1, keepdims=True).astype(jnp.int32)
        allowed.append(slot < count)
    allowed = jnp.concatenate(allowed, axis=1)

    outs = []
    for head in range(heads):
        lanes = slice(head * head_dim, (head + 1) * head_dim)
        scores = dot_lanes(query[:, lanes], keys[:, lanes]) * head_dim ** (-0.5)
        scores = jnp.where(allowed, scores, -jnp.inf)
        top = jnp.max(scores, axis=1, keepdims=True)
        expo = jnp.exp(scores - top)
        probs = (expo / jnp.sum(expo, axis=1, keepdims=True)).astype(BF16)
        outs.append(dot(probs, values[:, lanes]).astype(BF16))
    joined = jnp.concatenate(outs, axis=1)
    back = dot(joined, wo[...])
    place = placing[...]
    placed = sum(dot(place, term) for term in terms(back, 2))
    result[...] = (hidden[...].astype(F32) + placed).astype(BF16)


def call(kernel, outs, ins, scratch=(), specs=None):
    return pl.pallas_call(
        kernel,
        out_shape=[jax.ShapeDtypeStruct(shape, dtype) for shape, dtype in outs],
        in_specs=specs or [VMEM] * len(ins),
        out_specs=[VMEM] * len(outs),
        scratch_shapes=list(scratch),
    )(*ins)


def shards(
    tokens, group_pos, log_decay, in_weight, norm_gain, out_weight, inner_gain, qkv_weight, attn_out
):
    devices = lax.axis_size("seq")
    grps = lax.axis_size("grp")
    length, model = tokens.shape
    heads = log_decay.shape[1]
    width = out_weight.shape[0]
    states = (in_weight.shape[1] - 2 * width) // 2
    head_dim = attn_out.shape[1]
    most = length // 2
    split = next(s for s in (4, 2, 1) if grps % s == 0)
    step = min(256, width)
    chunks = width // step
    groups = group_pos.reshape(1, -1)
    tall = model // split * 3 // 2 + head_dim // split * (model // (2 * head_dim))

    xs, bc, local, first, total, cumul, piece = call(
        functools.partial(front_kernel, split),
        [
            ((length, width), BF16),
            ((length, 2 * states), BF16),
            ((states, width), F32),
            ((states, width), BF16),
            ((8, width), F32),
            ((length, heads), F32),
            ((tall, 2 * head_dim), BF16),
        ],
        [tokens, log_decay, in_weight, qkv_weight, attn_out],
        [
            pltpu.VMEM((chunks, model, step), BF16),
            pltpu.VMEM((1, model, 2 * states), BF16),
            pltpu.SemaphoreType.DMA((chunks,)),
            pltpu.SemaphoreType.DMA((1,)),
        ],
        [VMEM, VMEM, ANY, VMEM, VMEM],
    )

    state = jnp.zeros((states, width), BF16)
    for s in range(devices - 1):
        sent = first
        if s:
            sent = (total[:1] * state.astype(F32) + local).astype(BF16)
        state = state + lax.ppermute(sent, "seq", [(s, s + 1)])

    within, silu, grown, placing, cmat = call(
        middle_kernel,
        [
            ((length, width), F32),
            ((length, width), F32),
            ((length, width), F32),
            ((length, most), BF16),
            ((length, states), BF16),
        ],
        [tokens, log_decay, in_weight, cumul, xs, bc, groups],
        [pltpu.VMEM((chunks, model, step), BF16), pltpu.SemaphoreType.DMA((chunks,))],
        [VMEM, VMEM, ANY, VMEM, VMEM, VMEM, VMEM],
    )

    pieces = [piece]
    for s in range(1, devices):
        around = [(i, (i + s) % devices) for i in range(devices)]
        pieces.append(lax.ppermute(piece, "seq", around))
    bundles, masks, bit = [jnp.concatenate(pieces, axis=0)], [(0,)], split // 2
    while bit:
        whole = bundles[0] if len(bundles) == 1 else jnp.concatenate(bundles, axis=0)
        other = lax.ppermute(whole, "grp", [(i, i ^ bit) for i in range(grps)])
        bundles.append(other)
        masks.append(tuple(m ^ bit for mask in masks for m in mask))
        bit //= 2
    weights = call(
        functools.partial(weight_kernel, masks, split, model, head_dim),
        [((model, devices * head_dim), BF16)] * 3 + [((devices * head_dim, model), BF16)],
        bundles,
    )

    hidden, rows = call(
        post_kernel,
        [((length, model), BF16), ((most, model), BF16)],
        [
            state, within, silu, grown, placing, cmat, norm_gain.reshape(1, -1), out_weight,
            tokens, inner_gain.reshape(1, -1),
        ],
    )
    known = [rows]
    for s in range(1, devices):
        known.append(lax.ppermute(rows, "seq", [(i, i + s) for i in range(devices - s)]))

    (result,) = call(
        functools.partial(attend_kernel, devices, length),
        [((length, model), BF16)],
        known + list(weights) + [hidden, placing, groups],
    )
    return result


def solution(mesh):
    in_specs = (
        P(("grp", "seq"), None),
        P("grp"),
        P(("grp", "seq"), None),
        P(),
        P(),
        P(),
        P(),
        P("seq", None, None),
        P("seq", None, None),
    )
    out_specs = P(("grp", "seq"), None)
    return jax.shard_map(shards, mesh=mesh, in_specs=in_specs, out_specs=out_specs, check_vma=False)
```

time: 117 us -> 59.9 us (0.51)
  the two profiles are of different devices: /device:TPU:0 before, /device:TPU:28 now
where the time goes in v1:
time: 59.9 us; the launch traced here: 59.3 us
  Pallas kernels  22 us (37%)
  waiting for transfers between devices  17.5 us (29%)
  starting transfers between devices  10.5 us (18%)
  local copies, waits for them, and re-layouts  6.44 us (11%)
  other arithmetic  2.69 us (4%)
    pallas_call x5, Pallas kernels, call(): pl.pallas_call(kernel, out_shape=[jax.ShapeDtypeStruct(shape, dtype) for...  22 us
    ppermute x3, waiting for transfers between devices, shards(): lax.ppermute(rows, 'seq', [(i, i + s) for i in range(devices - s)])  9.16 us
    unnamed x18, local copies, waits for them, and re-layouts  5.64 us
    ppermute x3, waiting for transfers between devices, shards(): pieces.append(lax.ppermute(piece, 'seq', around))  4.61 us
    ppermute x3, starting transfers between devices, shards(): lax.ppermute(rows, 'seq', [(i, i + s) for i in range(devices - s)])  3.86 us
    ppermute x3, starting transfers between devices, shards(): state = state + lax.ppermute(sent, 'seq', [(s, s + 1)])  2.62 us
    ppermute x2, waiting for transfers between devices, shards(): other = lax.ppermute(whole, 'grp', [(i, i ^ bit) for i in range(grps)])  2.44 us
    ppermute x3, starting transfers between devices, shards(): pieces.append(lax.ppermute(piece, 'seq', around))  2.42 us
  transfers between devices with their start and end apart: 11, of which 5 were waited for; matrix products, arithmetic and copies ran while one was open for 7% of the time, Pallas kernels for 21%

profile of v1, /device:TPU:28, one launch (start us, length us, event | category | flops | bytes accessed | tf_op | source)
XLA Modules:
  0.0 59.3 jit_solution(15065200367289164968)
XLA Ops:
  0.0 1.5 %copy.10.decay = f32[256,16]{1,0:T(8,128)} copy(f32[256,16]{0,1:T(8,128)} %param.11) | data formatting | bytes 32768 | tf_op args[2]
  1.5 1.8 %copy.11.qkv = bf16[1,512,192]{2,1,0:T(8,128)(2,1)} copy(bf16[1,512,192]{1,2,0:T(8,128)(2,1)} %param.16) | data formatting | bytes 393216 | tf_op args[7]
  3.2 5.1 %shard_map.91 = (bf16[256,1024]{1,0:T(8,128)(2,1)}, bf16[256,128]{1,0:T(8,128)(2,1)}, f32[64,1024]{1,0:T(8,128)}, bf16[64,1024]{1,0:T(8,128)(2,1)}, f32[8,1024]{...) custom-call(bf16[256,512]{1,0:T(8,128)(2,1)} %tokens.5, f32[256,16]{1,0:T(8,128)} %copy.10.decay, ...), custom_call_target="tpu_custom_call" | custom-call | tf_op jit(solution)/shard_map/pallas_call | solution.py:258
  8.6 1.7 %collective-permute-start.7 = (bf16[256,128]{1,0:T(8,128)(2,1)}, bf16[256,128]{1,0:T(8,128)(2,1)S(1)}, u32[]{:S(2)}, u32[]{:S(2)}) collective-permute-start(bf16[256,128]{1,0:T(8,128)(2,1)} %get-tuple-element.35), channel_id=1, source_target_pairs={{0,2},{1,3},{2,0},{3,1},{4,6},{5,7},{6,4},{7,5},{8,10},{9,11},{10,... | collective-permute-start | bytes 196616 | tf_op jit(solution)/shard_map/ppermute | solution.py:329
  11.4 0.9 %constant_dynamic-update-slice_fusion.8 = (bf16[2048,128]{1,0:T(8,128)(2,1)S(1)}, bf16[1024,128]{1,0:T(8,128)(2,1)S(1)}) fusion(bf16[256,128]{1,0:T(8,128)(2,1)} %get-tuple-element.35), kind=kLoop, calls=%fused_computation.10 | loop fusion | bytes 196608
  12.3 1.1 %collective-permute-done.6 = bf16[256,128]{1,0:T(8,128)(2,1)S(1)} collective-permute-done((bf16[256,128]{1,0:T(8,128)(2,1)}, bf16[256,128]{1,0:T(8,128)(2,1)S(1)}, u32[]{:S(2)}, u32[]{:S(2)}) %collective-permute-start.6) | collective-permute-done | bytes 65568 | tf_op jit(solution)/shard_map/ppermute | solution.py:329
  13.4 3.5 %collective-permute-done.7 = bf16[256,128]{1,0:T(8,128)(2,1)S(1)} collective-permute-done((bf16[256,128]{1,0:T(8,128)(2,1)}, bf16[256,128]{1,0:T(8,128)(2,1)S(1)}, u32[]{:S(2)}, u32[]{:S(2)}) %collective-permute-start.7) | collective-permute-done | bytes 65568 | tf_op jit(solution)/shard_map/ppermute | solution.py:329
  17.0 1.6 %collective-permute-start.9 = (bf16[1024,128]{1,0:T(8,128)(2,1)S(1)}, bf16[1024,128]{1,0:T(8,128)(2,1)S(1)}, u32[]{:S(2)}, u32[]{:S(2)}) collective-permute-start(bf16[1024,128]{1,0:T(8,128)(2,1)S(1)} %get-tuple-element.44.refs_0_), channel_id=1, source_target_pairs={{0,8},{4,12},{8,0},{12,4},{16,24},{20,28},{24,16},{28,20},{1,9},{5... | collective-permute-start | bytes 786440 | tf_op jit(solution)/shard_map/ppermute | solution.py:333
  18.5 0.8 %slice.4 = f32[1,1024]{1,0:T(1,128)S(1)} slice(f32[8,1024]{1,0:T(8,128)} %get-tuple-element.24), slice={[0:1], [0:1024]} | slice | bytes 8192 | tf_op jit(solution)/shard_map/slice | solution.py:309
  19.3 1.0 %add_convert_fusion.1 = bf16[64,1024]{1,0:T(8,128)(2,1)S(1)} fusion(f32[64,1024]{1,0:T(8,128)} %get-tuple-element.25, bf16[64,1024]{1,0:T(8,128)(2,1)S(1)} %collective-permute-done, f32[1024]{0:T(1024)S(1)} %bitcast.4), kind=kLoop, calls=%fused_computation.1 | loop fusion | flops 262144 | bytes 528384 | tf_op jit(solution)/shard_map/convert_element_type | solution.py:309
  21.0 2.4 %collective-permute-done.9.refs_1_ = bf16[1024,128]{1,0:T(8,128)(2,1)S(1)} collective-permute-done((bf16[1024,128]{1,0:T(8,128)(2,1)S(1)}, bf16[1024,128]{1,0:T(8,128)(2,1)S(1)}, u32[]{:S(2)}, u32[]{:S(2)}) %collective-permute-start.9) | collective-permute-done | bytes 262176 | tf_op jit(solution)/shard_map/ppermute | solution.py:333
  23.5 1.0 %add_convert_fusion = (bf16[64,1024]{1,0:T(8,128)(2,1)S(1)}, bf16[64,1024]{1,0:T(8,128)(2,1)S(1)}) fusion(f32[64,1024]{1,0:T(8,128)} %get-tuple-element.25, f32[1024]{0:T(1024)S(1)} %bitcast.5, bf16[64,1024]{1,0:T(8,128)(2,1)S(1)} %collective-permute-done, bf16[64,1024]{1,0:T(8,128)(2,1)S(1)} %collective-permute-done.1), kind=kLoop, calls=%fused_computation | loop fusion | flops 327680 | bytes 790528 | tf_op jit(solution)/shard_map/convert_element_type | solution.py:309
  24.6 1.3 %collective-permute-start.2 = (bf16[64,1024]{1,0:T(8,128)(2,1)S(1)}, bf16[64,1024]{1,0:T(8,128)(2,1)S(1)}, u32[]{:S(2)}, u32[]{:S(2)}) collective-permute-start(bf16[64,1024]{1,0:T(8,128)(2,1)S(1)} %get-tuple-element.41), channel_id=1, source_target_pairs={{2,3},{6,7},{10,11},{14,15},{18,19},{22,23},{26,27},{30,31}} | collective-permute-start | bytes 393224 | tf_op jit(solution)/shard_map/ppermute | solution.py:310
  25.9 5.2 %shard_map.92 = (f32[256,1024]{1,0:T(8,128)}, f32[256,1024]{1,0:T(8,128)}, f32[256,1024]{1,0:T(8,128)}, bf16[256,128]{1,0:T(8,128)(2,1)}, bf16[256,64]{1,0:T(8,128)(2,1)}) custom-call(bf16[256,512]{1,0:T(8,128)(2,1)} %tokens.5, f32[256,16]{1,0:T(8,128)} %copy.10.decay, bf16[512,2176]{1,0:T(8,128)(2,1)} %weight.3, f32[256,16]{1,0:T(8,128)} %get-tuple-element.26.cumul, ...), custom_call_target="tpu_custom_call" | custom-call | tf_op jit(solution)/shard_map/pallas_call | solution.py:258
  31.1 1.3 %collective-permute-done.2 = bf16[64,1024]{1,0:T(8,128)(2,1)S(1)} collective-permute-done((bf16[64,1024]{1,0:T(8,128)(2,1)S(1)}, bf16[64,1024]{1,0:T(8,128)(2,1)S(1)}, u32[]{:S(2)}, u32[]{:S(2)}) %collective-permute-start.2) | collective-permute-done | bytes 131104 | tf_op jit(solution)/shard_map/ppermute | solution.py:310
  32.3 0.7 %add.15.state = bf16[64,1024]{1,0:T(8,128)(2,1)} add(bf16[64,1024]{1,0:T(8,128)(2,1)S(1)} %get-tuple-element.42, bf16[64,1024]{1,0:T(8,128)(2,1)S(1)} %collective-permute-done.2) | non-fusion elementwise | flops 65536 | bytes 393216 | tf_op jit(solution)/shard_map/add | solution.py:310
  33.0 4.0 %shard_map.93 = (bf16[256,512]{1,0:T(8,128)(2,1)}, bf16[128,512]{1,0:T(8,128)(2,1)}) custom-call(bf16[64,1024]{1,0:T(8,128)(2,1)} %add.15.state, f32[256,1024]{1,0:T(8,128)} %get-tuple-element.29.within, f32[256,1024]{1,0:T(8,128)} %get-tuple-element.30.silu, f32[256,1024]{1,0:T(8,128)} %get-tuple-element.31.grown, ...), custom_call_target="tpu_custom_call" | custom-call | tf_op jit(solution)/shard_map/pallas_call | solution.py:258
  37.0 1.3 %collective-permute-start.3 = (bf16[128,512]{1,0:T(8,128)(2,1)}, bf16[128,512]{1,0:T(8,128)(2,1)S(1)}, u32[]{:S(2)}, u32[]{:S(2)}) collective-permute-start(bf16[128,512]{1,0:T(8,128)(2,1)} %get-tuple-element.34.refs_0_), channel_id=1, source_target_pairs={{0,1},{1,2},{2,3},{4,5},{5,6},{6,7},{8,9},{9,10},{10,11},{12,13},{... | collective-permute-start | bytes 393224 | tf_op jit(solution)/shard_map/ppermute | solution.py:353
  38.3 1.3 %collective-permute-start.4 = (bf16[128,512]{1,0:T(8,128)(2,1)}, bf16[128,512]{1,0:T(8,128)(2,1)S(1)}, u32[]{:S(2)}, u32[]{:S(2)}) collective-permute-start(bf16[128,512]{1,0:T(8,128)(2,1)} %get-tuple-element.34.refs_0_), channel_id=1, source_target_pairs={{0,2},{1,3},{4,6},{5,7},{8,10},{9,11},{12,14},{13,15},{16,18},{17,... | collective-permute-start | bytes 393224 | tf_op jit(solution)/shard_map/ppermute | solution.py:353
  39.6 1.3 %collective-permute-start.5 = (bf16[128,512]{1,0:T(8,128)(2,1)}, bf16[128,512]{1,0:T(8,128)(2,1)S(1)}, u32[]{:S(2)}, u32[]{:S(2)}) collective-permute-start(bf16[128,512]{1,0:T(8,128)(2,1)} %get-tuple-element.34.refs_0_), channel_id=1, source_target_pairs={{0,3},{4,7},{8,11},{12,15},{16,19},{20,23},{24,27},{28,31}} | collective-permute-start | bytes 393224 | tf_op jit(solution)/shard_map/ppermute | solution.py:353
  40.9 0.8 %copy-done.1 = bf16[2048,128]{1,0:T(8,128)(2,1)} copy-done((bf16[2048,128]{1,0:T(8,128)(2,1)}, bf16[2048,128]{1,0:T(8,128)(2,1)S(1)}, u32[]{:S(2)}) %copy-start.1) | copy-done | bytes 524312
  41.7 3.1 %shard_map.94 = (bf16[512,256]{1,0:T(8,128)(2,1)}, bf16[512,256]{1,0:T(8,128)(2,1)}, bf16[512,256]{1,0:T(8,128)(2,1)}, bf16[256,512]{1,0:T(8,128)(2,1)}) custom-call(bf16[1024,128]{1,0:T(8,128)(2,1)} %copy-done.2, bf16[1024,128]{1,0:T(8,128)(2,1)} %copy-done, bf16[2048,128]{1,0:T(8,128)(2,1)} %copy-done.1), custom_call_target="tpu_custom_call" | custom-call | tf_op jit(solution)/shard_map/pallas_call | solution.py:258
  44.8 9.2 %collective-permute-done.4.refs_2_ = bf16[128,512]{1,0:T(8,128)(2,1)S(1)} collective-permute-done((bf16[128,512]{1,0:T(8,128)(2,1)}, bf16[128,512]{1,0:T(8,128)(2,1)S(1)}, u32[]{:S(2)}, u32[]{:S(2)}) %collective-permute-start.4) | collective-permute-done | bytes 131104 | tf_op jit(solution)/shard_map/ppermute | solution.py:353
  54.6 4.7 %shard_map.95 = bf16[256,512]{1,0:T(8,128)(2,1)} custom-call(bf16[128,512]{1,0:T(8,128)(2,1)} %get-tuple-element.34.refs_0_, bf16[128,512]{1,0:T(8,128)(2,1)} %copy-done.3, bf16[128,512]{1,0:T(8,128)(2,1)} %copy-done.4, bf16[128,512]{1,0:T(8,128)(2,1)} %copy-done.5, bf16[512,256]{1,0:T(8,128)(2,1)} %get-tuple-element.36.refs_4_, ...), custom_call_target="tpu_custom_call" | custom-call | tf_op jit(solution)/shard_map/pallas_call | solution.py:258
  (26 shorter events, 2.9 us)
Async XLA Ops:
  8.3 5.1 %collective-permute-start.6 = (bf16[256,128]{1,0:T(8,128)(2,1)}, bf16[256,128]{1,0:T(8,128)(2,1)S(1)}, u32[]{:S(2)}, u32[]{:S(2)}) collective-permute-start(bf16[256,128]{1,0:T(8,128)(2,1)} %get-tuple-element.35), channel_id=1, source_target_pairs={{0,1},{1,2},{2,3},{3,0},{4,5},{5,6},{6,7},{7,4},{8,9},{9,10},{10,1... | collective-permute-start | bytes 196616 | tf_op jit(solution)/shard_map/ppermute | solution.py:329
  8.6 8.3 %collective-permute-start.7 = (bf16[256,128]{1,0:T(8,128)(2,1)}, bf16[256,128]{1,0:T(8,128)(2,1)S(1)}, u32[]{:S(2)}, u32[]{:S(2)}) collective-permute-start(bf16[256,128]{1,0:T(8,128)(2,1)} %get-tuple-element.35), channel_id=1, source_target_pairs={{0,2},{1,3},{2,0},{3,1},{4,6},{5,7},{6,4},{7,5},{8,10},{9,11},{10,... | collective-permute-start | bytes 196616 | tf_op jit(solution)/shard_map/ppermute | solution.py:329
  10.3 6.6 %collective-permute-start.8 = (bf16[256,128]{1,0:T(8,128)(2,1)}, bf16[256,128]{1,0:T(8,128)(2,1)S(1)}, u32[]{:S(2)}, u32[]{:S(2)}) collective-permute-start(bf16[256,128]{1,0:T(8,128)(2,1)} %get-tuple-element.35), channel_id=1, source_target_pairs={{0,3},{1,0},{2,1},{3,2},{4,7},{5,4},{6,5},{7,6},{8,11},{9,8},{10,9... | collective-permute-start | bytes 196616 | tf_op jit(solution)/shard_map/ppermute | solution.py:329
  10.7 8.6 %collective-permute-start = (bf16[64,1024]{1,0:T(8,128)(2,1)}, bf16[64,1024]{1,0:T(8,128)(2,1)S(1)}, u32[]{:S(2)}, u32[]{:S(2)}) collective-permute-start(bf16[64,1024]{1,0:T(8,128)(2,1)} %get-tuple-element.23), channel_id=1, source_target_pairs={{0,1},{4,5},{8,9},{12,13},{16,17},{20,21},{24,25},{28,29}} | collective-permute-start | bytes 393224 | tf_op jit(solution)/shard_map/ppermute | solution.py:310
  17.0 14.1 %copy-start.2 = (bf16[1024,128]{1,0:T(8,128)(2,1)}, bf16[1024,128]{1,0:T(8,128)(2,1)S(1)}, u32[]{:S(2)}) copy-start(bf16[1024,128]{1,0:T(8,128)(2,1)S(1)} %get-tuple-element.44.refs_0_) | copy-start | bytes 786436
  17.0 6.4 %collective-permute-start.9 = (bf16[1024,128]{1,0:T(8,128)(2,1)S(1)}, bf16[1024,128]{1,0:T(8,128)(2,1)S(1)}, u32[]{:S(2)}, u32[]{:S(2)}) collective-permute-start(bf16[1024,128]{1,0:T(8,128)(2,1)S(1)} %get-tuple-element.44.refs_0_), channel_id=1, source_target_pairs={{0,8},{4,12},{8,0},{12,4},{16,24},{20,28},{24,16},{28,20},{1,9},{5... | collective-permute-start | bytes 786440 | tf_op jit(solution)/shard_map/ppermute | solution.py:333
  20.3 3.2 %collective-permute-start.1 = (bf16[64,1024]{1,0:T(8,128)(2,1)S(1)}, bf16[64,1024]{1,0:T(8,128)(2,1)S(1)}, u32[]{:S(2)}, u32[]{:S(2)}) collective-permute-start(bf16[64,1024]{1,0:T(8,128)(2,1)S(1)} %add_convert_fusion.1), channel_id=1, source_target_pairs={{1,2},{5,6},{9,10},{13,14},{17,18},{21,22},{25,26},{29,30}} | collective-permute-start | bytes 393224 | tf_op jit(solution)/shard_map/ppermute | solution.py:310
  23.4 7.6 %copy-start = (bf16[1024,128]{1,0:T(8,128)(2,1)}, bf16[1024,128]{1,0:T(8,128)(2,1)S(1)}, u32[]{:S(2)}) copy-start(bf16[1024,128]{1,0:T(8,128)(2,1)S(1)} %collective-permute-done.9.refs_1_) | copy-start | bytes 786436
  23.4 17.4 %collective-permute-start.10 = (bf16[2048,128]{1,0:T(8,128)(2,1)S(1)}, bf16[2048,128]{1,0:T(8,128)(2,1)S(1)}, u32[]{:S(2)}, u32[]{:S(2)}) collective-permute-start(bf16[2048,128]{1,0:T(8,128)(2,1)S(1)} %constant_dynamic-update-slice_fusion.4), channel_id=1, source_target_pairs={{0,4},{4,0},{8,12},{12,8},{16,20},{20,16},{24,28},{28,24},{1,5},{5... | collective-permute-start | bytes 1572872 | tf_op jit(solution)/shard_map/ppermute | solution.py:333
  24.6 7.8 %collective-permute-start.2 = (bf16[64,1024]{1,0:T(8,128)(2,1)S(1)}, bf16[64,1024]{1,0:T(8,128)(2,1)S(1)}, u32[]{:S(2)}, u32[]{:S(2)}) collective-permute-start(bf16[64,1024]{1,0:T(8,128)(2,1)S(1)} %get-tuple-element.41), channel_id=1, source_target_pairs={{2,3},{6,7},{10,11},{14,15},{18,19},{22,23},{26,27},{30,31}} | collective-permute-start | bytes 393224 | tf_op jit(solution)/shard_map/ppermute | solution.py:310
  37.0 7.8 %collective-permute-start.3 = (bf16[128,512]{1,0:T(8,128)(2,1)}, bf16[128,512]{1,0:T(8,128)(2,1)S(1)}, u32[]{:S(2)}, u32[]{:S(2)}) collective-permute-start(bf16[128,512]{1,0:T(8,128)(2,1)} %get-tuple-element.34.refs_0_), channel_id=1, source_target_pairs={{0,1},{1,2},{2,3},{4,5},{5,6},{6,7},{8,9},{9,10},{10,11},{12,13},{... | collective-permute-start | bytes 393224 | tf_op jit(solution)/shard_map/ppermute | solution.py:353
  38.3 15.6 %collective-permute-start.4 = (bf16[128,512]{1,0:T(8,128)(2,1)}, bf16[128,512]{1,0:T(8,128)(2,1)S(1)}, u32[]{:S(2)}, u32[]{:S(2)}) collective-permute-start(bf16[128,512]{1,0:T(8,128)(2,1)} %get-tuple-element.34.refs_0_), channel_id=1, source_target_pairs={{0,2},{1,3},{4,6},{5,7},{8,10},{9,11},{12,14},{13,15},{16,18},{17,... | collective-permute-start | bytes 393224 | tf_op jit(solution)/shard_map/ppermute | solution.py:353
  39.6 14.3 %collective-permute-start.5 = (bf16[128,512]{1,0:T(8,128)(2,1)}, bf16[128,512]{1,0:T(8,128)(2,1)S(1)}, u32[]{:S(2)}, u32[]{:S(2)}) collective-permute-start(bf16[128,512]{1,0:T(8,128)(2,1)} %get-tuple-element.34.refs_0_), channel_id=1, source_target_pairs={{0,3},{4,7},{8,11},{12,15},{16,19},{20,23},{24,27},{28,31}} | collective-permute-start | bytes 393224 | tf_op jit(solution)/shard_map/ppermute | solution.py:353
  40.9 0.8 %copy-start.1 = (bf16[2048,128]{1,0:T(8,128)(2,1)}, bf16[2048,128]{1,0:T(8,128)(2,1)S(1)}, u32[]{:S(2)}) copy-start(bf16[2048,128]{1,0:T(8,128)(2,1)S(1)} %collective-permute-done.10.refs_2_) | copy-start | bytes 1572868
  44.8 9.2 %copy-start.3 = (bf16[128,512]{1,0:T(8,128)(2,1)}, bf16[128,512]{1,0:T(8,128)(2,1)S(1)}, u32[]{:S(2)}) copy-start(bf16[128,512]{1,0:T(8,128)(2,1)S(1)} %collective-permute-done.3.refs_1_) | copy-start | bytes 393220
  53.9 0.6 %copy-start.4 = (bf16[128,512]{1,0:T(8,128)(2,1)}, bf16[128,512]{1,0:T(8,128)(2,1)S(1)}, u32[]{:S(2)}) copy-start(bf16[128,512]{1,0:T(8,128)(2,1)S(1)} %collective-permute-done.4.refs_2_) | copy-start | bytes 393220
  53.9 0.7 %copy-start.5 = (bf16[128,512]{1,0:T(8,128)(2,1)}, bf16[128,512]{1,0:T(8,128)(2,1)S(1)}, u32[]{:S(2)}) copy-start(bf16[128,512]{1,0:T(8,128)(2,1)S(1)} %collective-permute-done.5.refs_3_) | copy-start | bytes 393220

commit v2 on v1

v2 whole, which is shorter than its diff:
```python
import functools

import jax
import jax.numpy as jnp
from jax import lax
from jax.experimental import pallas as pl
from jax.experimental.pallas import tpu as pltpu
from jax.sharding import PartitionSpec as P


F32 = jnp.float32
BF16 = jnp.bfloat16
EPS = 1e-05
VMEM = pl.BlockSpec(memory_space=pltpu.VMEM)
HBM = pl.BlockSpec(memory_space=pltpu.HBM)


def dot(a, b):
    return jnp.dot(a, b, preferred_element_type=F32)


def dot_rows(a, b):
    return lax.dot_general(a, b, (((0,), (0,)), ((), ())), preferred_element_type=F32)


def dot_lanes(a, b):
    return lax.dot_general(a, b, (((1,), (1,)), ((), ())), preferred_element_type=F32)


def iota(shape, axis):
    return lax.broadcasted_iota(jnp.int32, shape, axis)


def terms(value, count):
    out = []
    for _ in range(count):
        term = value.astype(BF16)
        out.append(term)
        value = value - term.astype(F32)
    return out


def spread(value, heads, width, count):
    size = width // heads
    row = iota((heads, width), 0)
    lane = iota((heads, width), 1)
    pick = ((lane >= row * size) & (lane < (row + 1) * size)).astype(BF16)
    return sum(dot(term, pick) for term in terms(value, count))


def weight_copies(weight, buffer, sems, start, step):
    count = buffer.shape[0]
    return [
        pltpu.make_async_copy(
            weight.at[:, pl.ds(start + i * step, step)], buffer.at[i], sems.at[i]
        )
        for i in range(count)
    ]


def front_kernel(
    tokens_hbm, decay_hbm, weight,
    xs, bc, local, first, total, cumul,
    tokens, decay, xs_buffer, bc_buffer, small_sems, xs_sems, bc_sems,
):
    heads, length = decay.shape
    width = xs.shape[1]
    states = local.shape[0]
    step = xs_buffer.shape[2]
    bc_copy = weight_copies(weight, bc_buffer, bc_sems, 2 * width, 2 * states)
    xs_copy = weight_copies(weight, xs_buffer, xs_sems, 0, step)
    decay_copy = pltpu.make_async_copy(decay_hbm, decay, small_sems.at[0])
    token_copy = pltpu.make_async_copy(tokens_hbm, tokens, small_sems.at[1])
    for copy in [decay_copy, token_copy] + bc_copy + xs_copy:
        copy.start()

    decay_copy.wait()
    lower = (iota((length, length), 0) >= iota((length, length), 1)).astype(BF16)
    cum = sum(dot_lanes(lower, term) for term in terms(decay[...], 3))
    cumul[...] = cum
    last = cum[length - 1 :, :]
    tails = jnp.exp(last - cum)
    total[...] = spread(jnp.broadcast_to(jnp.exp(last), (8, heads)), heads, width, 3)
    tails_wide = spread(tails, heads, width, 2)

    token_copy.wait()
    bc_copy[0].wait()
    ins = tokens[...]
    both = dot(ins, bc_buffer[0]).astype(BF16)
    bc[...] = both
    for i, copy in enumerate(xs_copy):
        lanes = slice(i * step, (i + 1) * step)
        copy.wait()
        block = dot(ins, xs_buffer[i]).astype(BF16)
        xs[:, lanes] = block
        scaled = (block.astype(F32) * tails_wide[:, lanes]).astype(BF16)
        state = dot_rows(both, scaled)[:states]
        local[:, lanes] = state
        first[:, lanes] = state.astype(BF16)


def middle_kernel(
    split, tokens, decay, weight, cumul, xs, bc, groups, qkv, attn_out,
    within, silu, grown, placing, cmat, piece,
    gate_buffer, gate_sems,
):
    heads, length = decay.shape
    width = xs.shape[1]
    states = bc.shape[1] // 2
    step = gate_buffer.shape[2]
    most = placing.shape[1]
    copies = weight_copies(weight, gate_buffer, gate_sems, width, step)
    for copy in copies:
        copy.start()

    mine = lax.rem(lax.axis_index("grp"), split[0] * split[1])
    lanes = piece.shape[1]
    column = pl.ds(pl.multiple_of(lax.rem(mine, split[0]) * lanes, lanes), lanes)
    stack = jnp.concatenate([qkv[0, :, column], attn_out[0, :, column]], axis=0)
    tall = piece.shape[0]
    part = lax.div(mine, split[0])
    chosen = stack[:tall]
    for i in range(1, split[1]):
        chosen = jnp.where(part == i, stack[i * tall : (i + 1) * tall], chosen)
    piece[...] = chosen

    here = lax.axis_index("seq") * length
    count = groups.shape[1]
    position = here + iota((length, count), 0)
    group = jnp.broadcast_to(groups[...], (length, count))
    starts = jnp.sum((group == position).astype(F32), axis=1, keepdims=True)
    ahead = (group < position) & (group >= here)
    rank = jnp.sum(ahead.astype(F32), axis=1, keepdims=True).astype(jnp.int32)
    slot = iota((length, most), 1)
    placing[...] = jnp.where(slot == rank, starts, 0.0).astype(BF16)

    cum = cumul[...]
    upper = (iota((length, length), 0) <= iota((length, length), 1)).astype(BF16)
    cum_t = sum(dot(term, upper) for term in terms(decay[...], 3))
    grown[...] = spread(jnp.exp(cum), heads, width, 2)
    both = bc[...]
    cmat[...] = both[:, states:]
    mixed = dot_lanes(both[:, states:], both[:, :states])

    half = length // 2
    lower = iota((half, half), 0) >= iota((half, half), 1)
    size = width // heads
    pair = 2 * size
    left = iota((half, pair), 1) < size
    for at in range(0, heads, 2):
        lanes = slice(at * size, at * size + pair)
        early, late = xs[:half, lanes], xs[half:, lanes]
        tops, lows = [], []
        for head in (at, at + 1):
            column = cum[:, head : head + 1]
            row = cum_t[head : head + 1, :]
            apart = jnp.where(lower, column[:half] - row[:, :half], -jnp.inf)
            top = (jnp.exp(apart) * mixed[:half, :half]).astype(BF16)
            apart = jnp.where(lower, column[half:] - row[:, half:], -jnp.inf)
            low = (jnp.exp(apart) * mixed[half:, half:]).astype(BF16)
            across = jnp.exp(column[half:] - row[:, :half])
            across = (across * mixed[half:, :half]).astype(BF16)
            tops.append(dot(top, early))
            lows.append(dot(low, late) + dot(across, early))
        within[:half, lanes] = jnp.where(left, tops[0], tops[1])
        within[half:, lanes] = jnp.where(left, lows[0], lows[1])

    ins = tokens[...]
    for i, copy in enumerate(copies):
        copy.wait()
        gate = dot(ins, gate_buffer[i]).astype(BF16).astype(F32)
        silu[:, i * step : (i + 1) * step] = gate / (1.0 + jnp.exp(-gate))


def merge_kernel(step, came, before, total, local, state, sent):
    taken = lax.axis_index("seq") == step + 1
    value = jnp.where(taken, came[...].astype(F32), before[...].astype(F32))
    state[...] = value.astype(BF16)
    sent[...] = (total[0:1, :] * value + local[...]).astype(BF16)


def first_merge_kernel(step, came, total, local, state, sent):
    taken = lax.axis_index("seq") == step + 1
    value = jnp.where(taken, came[...].astype(F32), 0.0)
    state[...] = value.astype(BF16)
    sent[...] = (total[0:1, :] * value + local[...]).astype(BF16)


def post_kernel(
    low, high, state, within, silu, grown, placing, cmat, gain, out_weight, tokens, inner_gain,
    *refs,
):
    earlier, (hidden, rows) = refs[:-2], refs[-2:]
    me = lax.axis_index("seq")
    active = (me >= low) & (me < high)

    @pl.when(active)
    def _():
        carried = dot(cmat[...], state[...])
        gated = (within[...] + grown[...] * carried) * silu[...]
        scale = lax.rsqrt(jnp.mean(gated * gated, axis=1, keepdims=True) + EPS)
        normed = (gated * scale * gain[...]).astype(BF16)
        mixed = dot(normed, out_weight[...])
        out = (tokens[...].astype(F32) + mixed).astype(BF16)
        hidden[...] = out
        picked = dot_rows(placing[...], out)
        scale = lax.rsqrt(jnp.mean(picked * picked, axis=1, keepdims=True) + EPS)
        rows[...] = (picked * scale * inner_gain[...]).astype(BF16)

    @pl.when(jnp.logical_not(active))
    def _():
        hidden[...] = earlier[0][...] if earlier else jnp.zeros_like(hidden)
        rows[...] = earlier[1][...] if earlier else jnp.zeros_like(rows)


def weight_kernel(masks, split, *refs):
    bundles, out = refs[:-1], refs[-1]
    parts = out.shape[0] // split[1]
    lanes = bundles[0].shape[1]
    mine = lax.rem(lax.axis_index("grp"), split[0] * split[1])
    tall = out.shape[1]
    for bundle, mask in zip(bundles, masks):
        source = mine ^ mask
        column = pl.ds(pl.multiple_of(lax.rem(source, split[0]) * lanes, lanes), lanes)
        part = lax.div(source, split[0]) * parts
        for j in range(parts):
            out[part + j, :, column] = bundle[j * tall : (j + 1) * tall, :]


def attend_kernel(devices, length, *refs):
    known, (hidden, weights, placing, groups, result) = refs[:devices], refs[devices:]
    most = known[0].shape[0]
    heads = devices
    head_dim = weights.shape[1] // heads
    me = lax.axis_index("seq")
    own = known[0][...]
    known = jnp.concatenate([block[...] for block in known], axis=0)
    query = dot_lanes(own, weights[0]).astype(BF16)
    keys = dot_lanes(weights[1], known).astype(BF16)
    values = dot_lanes(known, weights[2]).astype(BF16)

    slot = iota((most, most), 1)
    allowed = [slot <= iota((most, most), 0)]
    for back in range(1, devices):
        other = me ^ back
        start = other * length
        inside = (groups[...] >= start) & (groups[...] < start + length)
        count = jnp.sum(inside.astype(F32), axis=1, keepdims=True).astype(jnp.int32)
        allowed.append(slot < jnp.where(other < me, count, 0))
    allowed = jnp.concatenate(allowed, axis=1)

    outs = []
    for head in range(heads):
        lanes = slice(head * head_dim, (head + 1) * head_dim)
        scores = dot(query[:, lanes], keys[lanes, :]) * head_dim ** (-0.5)
        scores = jnp.where(allowed, scores, -jnp.inf)
        top = jnp.max(scores, axis=1, keepdims=True)
        expo = jnp.exp(scores - top)
        probs = (expo / jnp.sum(expo, axis=1, keepdims=True)).astype(BF16)
        outs.append(dot(probs, values[:, lanes]).astype(BF16))
    joined = jnp.concatenate(outs, axis=1)
    back = dot(joined, weights[3])
    place = placing[...]
    placed = sum(dot(place, term) for term in terms(back, 2))
    result[...] = (hidden[...].astype(F32) + placed).astype(BF16)


def swap(value, axis, mask):
    pairs = [(i, i ^ mask) for i in range(lax.axis_size(axis))]
    return lax.ppermute(value, axis, pairs)


def in_hbm(value):
    return pltpu.with_memory_space_constraint(value, pltpu.HBM)


def call(kernel, outs, ins, cost, scratch=(), specs=None):
    kernel = pl.pallas_call(
        kernel,
        out_shape=[jax.ShapeDtypeStruct(shape, dtype) for shape, dtype in outs],
        in_specs=specs or [VMEM] * len(ins),
        out_specs=[VMEM] * len(outs),
        scratch_shapes=list(scratch),
        cost_estimate=pl.CostEstimate(flops=cost, transcendentals=0, bytes_accessed=0),
        compiler_params=pltpu.CompilerParams(vmem_limit_bytes=24 << 20),
    )
    return kernel(*ins)


def shards(
    tokens, group_pos, log_decay, in_weight, norm_gain, out_weight, inner_gain, qkv_weight, attn_out
):
    devices = lax.axis_size("seq")
    grps = lax.axis_size("grp")
    length, model = tokens.shape
    heads = log_decay.shape[1]
    width = out_weight.shape[0]
    states = (in_weight.shape[1] - 2 * width) // 2
    head_dim = attn_out.shape[1]
    most = length // 2
    lane_split = next(s for s in (4, 2, 1) if grps % s == 0 and model % (128 * s) == 0)
    row_split = 2 if grps % (2 * lane_split) == 0 else 1
    split = (lane_split, row_split)
    tall = 4 * head_dim // row_split
    step = min(256, width)
    chunks = width // step
    groups = group_pos.reshape(1, -1)
    decay = log_decay.T
    qkv = jnp.transpose(qkv_weight, (0, 2, 1))
    gain, inner = norm_gain.reshape(1, -1), inner_gain.reshape(1, -1)
    buffers = [pltpu.VMEM((chunks, model, step), BF16), pltpu.SemaphoreType.DMA((chunks,))]

    xs, bc, local, first, total, cumul = call(
        front_kernel,
        [
            ((length, width), BF16),
            ((length, 2 * states), BF16),
            ((states, width), F32),
            ((states, width), BF16),
            ((8, width), F32),
            ((length, heads), F32),
        ],
        [in_hbm(tokens), in_hbm(decay), in_hbm(in_weight)],
        3 * 10**9,
        [
            pltpu.VMEM(tokens.shape, BF16),
            pltpu.VMEM(decay.shape, F32),
            buffers[0],
            pltpu.VMEM((1, model, 2 * states), BF16),
            pltpu.SemaphoreType.DMA((2,)),
            buffers[1],
            pltpu.SemaphoreType.DMA((1,)),
        ],
        [HBM, HBM, HBM],
    )

    def link(sent, step):
        pairs = [(step, step + 1), (step + 1, step)]
        return lax.ppermute(sent, "seq", pairs)

    came = link(first, 0)

    within, silu, grown, placing, cmat, piece = call(
        functools.partial(middle_kernel, split),
        [
            ((length, width), F32),
            ((length, width), F32),
            ((length, width), F32),
            ((length, most), BF16),
            ((length, states), BF16),
            ((tall, model // lane_split), BF16),
        ],
        [tokens, decay, in_hbm(in_weight), cumul, xs, bc, groups, qkv, attn_out],
        3 * 10**9,
        buffers,
        [VMEM, VMEM, HBM] + [VMEM] * 6,
    )

    pieces = [piece]
    for mask in range(1, devices):
        pieces.append(swap(piece, "seq", mask))
    bundle = jnp.concatenate(
        [p[i * head_dim : (i + 1) * head_dim] for i in range(tall // head_dim) for p in pieces], axis=0
    )
    bundles, masks = [bundle], [0]
    for mask in range(2, lane_split * row_split, 2):
        bundles.append(swap(bundle, "grp", mask))
        masks.append(mask)
    if lane_split > 1:
        for i in range(len(bundles)):
            bundles.append(swap(bundles[i], "grp", 1))
            masks.append(masks[i] ^ 1)
    (weights,) = call(
        functools.partial(weight_kernel, masks, split),
        [((4, devices * head_dim, model), BF16)],
        bundles,
        10**9,
    )

    state, kept, blocks, done = None, [], {}, 0
    bounds = stages(devices)
    for low, high in zip(bounds[:-1], bounds[1:]):
        while done < high - 1 and done < devices - 2:
            ins = [came] + ([] if state is None else [state]) + [total, local]
            kernel = functools.partial(first_merge_kernel if state is None else merge_kernel, done)
            state, sent = call(kernel, [((states, width), BF16)] * 2, ins, 10**8)
            done += 1
            came = link(sent, done)
        kept = call(
            functools.partial(post_kernel, low, high),
            [((length, model), BF16), ((most, model), BF16)],
            [came if high == devices else state, within, silu, grown, placing, cmat, gain]
            + [out_weight, tokens, inner]
            + list(kept),
            2 * 10**9,
        )
        if high < devices:
            for mask in range(devices // 2 if low == 0 else 1, devices):
                if mask not in blocks:
                    blocks[mask] = swap(kept[1], "seq", mask)

    known = [kept[1]] + [blocks[mask] for mask in range(1, devices)]
    (result,) = call(
        functools.partial(attend_kernel, devices, length),
        [((length, model), BF16)],
        known + [kept[0], weights, placing, groups],
        3 * 10**9,
    )
    return result


def stages(devices):
    return sorted({0, devices // 2, devices - 1, devices})


def solution(mesh):
    in_specs = (
        P(("grp", "seq"), None),
        P("grp"),
        P(("grp", "seq"), None),
        P(),
        P(),
        P(),
        P(),
        P("seq", None, None),
        P("seq", None, None),
    )
    out_specs = P(("grp", "seq"), None)
    return jax.shard_map(shards, mesh=mesh, in_specs=in_specs, out_specs=out_specs, check_vma=False)
```

time: 59.9 us -> 46.1 us (0.77)
  the two profiles are of different devices: /device:TPU:28 before, /device:TPU:0 now
where the time goes in v2:
time: 46.1 us; the launch traced here: 45.9 us
  starting transfers between devices  18.3 us (40%)
  waiting for transfers between devices  15.4 us (33%)
  Pallas kernels  11.8 us (26%)
    ppermute x13, waiting for transfers between devices, swap(): return lax.ppermute(value, axis, pairs)  15.4 us
    ppermute x13, starting transfers between devices, swap(): return lax.ppermute(value, axis, pairs)  14.2 us
    pallas_call x9, Pallas kernels, call(): return kernel(*ins)  11.8 us
    ppermute x3, starting transfers between devices, link(): return lax.ppermute(sent, 'seq', pairs)  4.13 us
  transfers between devices with their start and end apart: 16, of which 6 were waited for; matrix products, arithmetic and copies ran while one was open for 0% of the time, Pallas kernels for 3%

profile of v2, /device:TPU:0, one launch (start us, length us, event | category | flops | bytes accessed | tf_op | source)
XLA Modules:
  0.0 45.9 jit_solution(15257854738908046324)
XLA Ops:
  0.0 3.9 %shard_map.91 = (bf16[256,1024]{1,0:T(8,128)(2,1)S(1)}, bf16[256,128]{1,0:T(8,128)(2,1)S(1)}, f32[64,1024]{1,0:T(8,128)S(1)}, bf16[64,1024]{1,0:T(8,128)(2,1)S(1...) custom-call(bf16[256,512]{1,0:T(8,128)(2,1)} %tokens.7, f32[16,256]{1,0:T(8,128)} %bitcast.6, bf16[512,2176]{1,0:T(8,128)(2,1)} %weight.3), custom_call_target="tpu_custom_call" | custom-call | flops 3000000000 | tf_op jit(solution)/shard_map/pallas_call | solution.py:287
  4.0 3.2 %shard_map.94 = (f32[256,1024]{1,0:T(8,128)S(1)}, f32[256,1024]{1,0:T(8,128)S(1)}, f32[256,1024]{1,0:T(8,128)S(1)}, bf16[256,128]{1,0:T(8,128)(2,1)S(1)}, bf16[2...) custom-call(bf16[256,512]{1,0:T(8,128)(2,1)S(1)} %copy-done.1, f32[16,256]{1,0:T(8,128)S(1)} %bitcast.7, ...), custom_call_target="tpu_custom_call" | custom-call | flops 3000000000 | tf_op jit(solution)/shard_map/pallas_call | solution.py:287
  7.3 3.1 %collective-permute-start.6 = (bf16[128,128]{1,0:T(8,128)(2,1)S(1)}, bf16[128,128]{1,0:T(8,128)(2,1)S(1)}, u32[]{:S(2)}, u32[]{:S(2)}) collective-permute-start(bf16[128,128]{1,0:T(8,128)(2,1)S(1)} %get-tuple-element.48), channel_id=1, source_target_pairs={{0,1},{1,0},{2,3},{3,2},{4,5},{5,4},{6,7},{7,6},{8,9},{9,8},{10,11... | collective-permute-start | bytes 98312 | tf_op jit(solution)/shard_map/ppermute | solution.py:270
  10.4 2.6 %collective-permute-start.7 = (bf16[128,128]{1,0:T(8,128)(2,1)S(1)}, bf16[128,128]{1,0:T(8,128)(2,1)S(1)}, u32[]{:S(2)}, u32[]{:S(2)}) collective-permute-start(bf16[128,128]{1,0:T(8,128)(2,1)S(1)} %get-tuple-element.48), channel_id=1, source_target_pairs={{0,2},{1,3},{2,0},{3,1},{4,6},{5,7},{6,4},{7,5},{8,10},{9,11},{10,... | collective-permute-start | bytes 98312 | tf_op jit(solution)/shard_map/ppermute | solution.py:270
  13.0 2.8 %collective-permute-start = (bf16[64,1024]{1,0:T(8,128)(2,1)S(1)}, bf16[64,1024]{1,0:T(8,128)(2,1)S(1)}, u32[]{:S(2)}, u32[]{:S(2)}) collective-permute-start(bf16[64,1024]{1,0:T(8,128)(2,1)S(1)} %get-tuple-element.27), channel_id=1, source_target_pairs={{0,1},{1,0},{4,5},{5,4},{8,9},{9,8},{12,13},{13,12},{16,17},{17,16... | collective-permute-start | bytes 393224 | tf_op jit(solution)/shard_map/ppermute | solution.py:339
  15.9 3.0 %collective-permute-done.8 = bf16[128,128]{1,0:T(8,128)(2,1)S(1)} collective-permute-done((bf16[128,128]{1,0:T(8,128)(2,1)S(1)}, bf16[128,128]{1,0:T(8,128)(2,1)S(1)}, u32[]{:S(2)}, u32[]{:S(2)}) %collective-permute-start.8) | collective-permute-done | bytes 32800 | tf_op jit(solution)/shard_map/ppermute | solution.py:270
  18.9 1.6 %collective-permute-start.9 = (bf16[512,128]{1,0:T(8,128)(2,1)S(1)}, bf16[512,128]{1,0:T(8,128)(2,1)S(1)}, u32[]{:S(2)}, u32[]{:S(2)}) collective-permute-start(bf16[512,128]{1,0:T(8,128)(2,1)S(1)} %constant_dynamic-update-slice_fusion.refs_0_), channel_id=1, source_target_pairs={{0,8},{4,12},{8,0},{12,4},{16,24},{20,28},{24,16},{28,20},{1,9},{5... | collective-permute-start | bytes 393224 | tf_op jit(solution)/shard_map/ppermute | solution.py:270
  20.4 1.5 %collective-permute-start.10 = (bf16[512,128]{1,0:T(8,128)(2,1)S(1)}, bf16[512,128]{1,0:T(8,128)(2,1)S(1)}, u32[]{:S(2)}, u32[]{:S(2)}) collective-permute-start(bf16[512,128]{1,0:T(8,128)(2,1)S(1)} %constant_dynamic-update-slice_fusion.refs_0_), channel_id=1, source_target_pairs={{0,16},{4,20},{8,24},{12,28},{16,0},{20,4},{24,8},{28,12},{1,17},{... | collective-permute-start | bytes 393224 | tf_op jit(solution)/shard_map/ppermute | solution.py:270
  21.9 0.5 %collective-permute-start.11 = (bf16[512,128]{1,0:T(8,128)(2,1)S(1)}, bf16[512,128]{1,0:T(8,128)(2,1)S(1)}, u32[]{:S(2)}, u32[]{:S(2)}) collective-permute-start(bf16[512,128]{1,0:T(8,128)(2,1)S(1)} %constant_dynamic-update-slice_fusion.refs_0_), channel_id=1, source_target_pairs={{0,24},{4,28},{8,16},{12,20},{16,8},{20,12},{24,0},{28,4},{1,25},{... | collective-permute-start | bytes 393224 | tf_op jit(solution)/shard_map/ppermute | solution.py:270
  22.4 0.1 shard_map.92
  22.5 0.7 %collective-permute-start.1 = (bf16[64,1024]{1,0:T(8,128)(2,1)S(1)}, bf16[64,1024]{1,0:T(8,128)(2,1)S(1)}, u32[]{:S(2)}, u32[]{:S(2)}) collective-permute-start(bf16[64,1024]{1,0:T(8,128)(2,1)S(1)} %get-tuple-element.30), channel_id=1, source_target_pairs={{1,2},{2,1},{5,6},{6,5},{9,10},{10,9},{13,14},{14,13},{17,18},{18,... | collective-permute-start | bytes 393224 | tf_op jit(solution)/shard_map/ppermute | solution.py:339
  23.2 1.1 %shard_map.95 = (bf16[256,512]{1,0:T(8,128)(2,1)S(1)}, bf16[128,512]{1,0:T(8,128)(2,1)S(1)}) custom-call(bf16[64,1024]{1,0:T(8,128)(2,1)S(1)} %get-tuple-element.31.before.state, f32[256,1024]{1,0:T(8,128)S(1)} %get-tuple-element.36.within, f32[256,1024]{1,0:T(8,128)S(1)} %get-tuple-element.37.silu, f32[256,1024]{1,0:T(8,128)S(1)} %get-tuple-element.38.grown, ...), custom_call_target="tpu_custom_call" | custom-call | flops 2000000000 | tf_op jit(solution)/shard_map/pallas_call | solution.py:287
  24.3 0.6 %collective-permute-done.9.refs_1_ = bf16[512,128]{1,0:T(8,128)(2,1)S(1)} collective-permute-done((bf16[512,128]{1,0:T(8,128)(2,1)S(1)}, bf16[512,128]{1,0:T(8,128)(2,1)S(1)}, u32[]{:S(2)}, u32[]{:S(2)}) %collective-permute-start.9) | collective-permute-done | bytes 131104 | tf_op jit(solution)/shard_map/ppermute | solution.py:270
  24.9 1.2 %collective-permute-done.10.refs_2_ = bf16[512,128]{1,0:T(8,128)(2,1)S(1)} collective-permute-done((bf16[512,128]{1,0:T(8,128)(2,1)S(1)}, bf16[512,128]{1,0:T(8,128)(2,1)S(1)}, u32[]{:S(2)}, u32[]{:S(2)}) %collective-permute-start.10) | collective-permute-done | bytes 131104 | tf_op jit(solution)/shard_map/ppermute | solution.py:270
  26.2 1.6 %collective-permute-done.11.refs_3_ = bf16[512,128]{1,0:T(8,128)(2,1)S(1)} collective-permute-done((bf16[512,128]{1,0:T(8,128)(2,1)S(1)}, bf16[512,128]{1,0:T(8,128)(2,1)S(1)}, u32[]{:S(2)}, u32[]{:S(2)}) %collective-permute-start.11) | collective-permute-done | bytes 131104 | tf_op jit(solution)/shard_map/ppermute | solution.py:270
  27.8 0.1 shard_map.93
  27.9 0.7 %collective-permute-start.2 = (bf16[64,1024]{1,0:T(8,128)(2,1)S(1)}, bf16[64,1024]{1,0:T(8,128)(2,1)S(1)}, u32[]{:S(2)}, u32[]{:S(2)}) collective-permute-start(bf16[64,1024]{1,0:T(8,128)(2,1)S(1)} %get-tuple-element.32), channel_id=1, source_target_pairs={{2,3},{3,2},{6,7},{7,6},{10,11},{11,10},{14,15},{15,14},{18,19},{1... | collective-permute-start | bytes 393224 | tf_op jit(solution)/shard_map/ppermute | solution.py:339
  28.6 3.9 %collective-permute-start.4 = (bf16[128,512]{1,0:T(8,128)(2,1)S(1)}, bf16[128,512]{1,0:T(8,128)(2,1)S(1)}, u32[]{:S(2)}, u32[]{:S(2)}) collective-permute-start(bf16[128,512]{1,0:T(8,128)(2,1)S(1)} %get-tuple-element.43.refs_1_), channel_id=1, source_target_pairs={{0,2},{1,3},{2,0},{3,1},{4,6},{5,7},{6,4},{7,5},{8,10},{9,11},{10,... | collective-permute-start | bytes 393224 | tf_op jit(solution)/shard_map/ppermute | solution.py:270
  32.5 0.5 %collective-permute-start.5 = (bf16[128,512]{1,0:T(8,128)(2,1)S(1)}, bf16[128,512]{1,0:T(8,128)(2,1)S(1)}, u32[]{:S(2)}, u32[]{:S(2)}) collective-permute-start(bf16[128,512]{1,0:T(8,128)(2,1)S(1)} %get-tuple-element.43.refs_1_), channel_id=1, source_target_pairs={{0,3},{1,2},{2,1},{3,0},{4,7},{5,6},{6,5},{7,4},{8,11},{9,10},{10,... | collective-permute-start | bytes 393224 | tf_op jit(solution)/shard_map/ppermute | solution.py:270
  33.0 0.5 %collective-permute-start.3 = (bf16[128,512]{1,0:T(8,128)(2,1)S(1)}, bf16[128,512]{1,0:T(8,128)(2,1)S(1)}, u32[]{:S(2)}, u32[]{:S(2)}) collective-permute-start(bf16[128,512]{1,0:T(8,128)(2,1)S(1)} %get-tuple-element.45.refs_1_), channel_id=1, source_target_pairs={{0,1},{1,0},{2,3},{3,2},{4,5},{5,4},{6,7},{7,6},{8,9},{9,8},{10,11... | collective-permute-start | bytes 393224 | tf_op jit(solution)/shard_map/ppermute | solution.py:270
  33.5 0.2 shard_map.98.refs_5_
  33.8 8.4 %collective-permute-done.4.refs_2_ = bf16[128,512]{1,0:T(8,128)(2,1)S(1)} collective-permute-done((bf16[128,512]{1,0:T(8,128)(2,1)S(1)}, bf16[128,512]{1,0:T(8,128)(2,1)S(1)}, u32[]{:S(2)}, u32[]{:S(2)}) %collective-permute-start.4) | collective-permute-done | bytes 131104 | tf_op jit(solution)/shard_map/ppermute | solution.py:270
  42.1 0.6 %collective-permute-done.5.refs_3_ = bf16[128,512]{1,0:T(8,128)(2,1)S(1)} collective-permute-done((bf16[128,512]{1,0:T(8,128)(2,1)S(1)}, bf16[128,512]{1,0:T(8,128)(2,1)S(1)}, u32[]{:S(2)}, u32[]{:S(2)}) %collective-permute-start.5) | collective-permute-done | bytes 131104 | tf_op jit(solution)/shard_map/ppermute | solution.py:270
  42.7 3.1 %shard_map.99 = bf16[256,512]{1,0:T(8,128)(2,1)} custom-call(bf16[128,512]{1,0:T(8,128)(2,1)S(1)} %get-tuple-element.46.refs_0_, bf16[128,512]{1,0:T(8,128)(2,1)S(1)} %collective-permute-done.3.refs_1_, bf16[128,512]{1,0:T(8,128)(2,1)S(1)} %collective-permute-done.4.refs_2_, bf16[128,512]{1,0:T(8,128)(2,1)S(1)} %collective-permute-done.5.refs_3_, ...), custom_call_target="tpu_custom_call" | custom-call | flops 3000000000 | tf_op jit(solution)/shard_map/pallas_call | solution.py:287
  (41 shorter events, 0.2 us)
Async XLA Ops:
  0.0 4.0 %copy-start.1 = (bf16[256,512]{1,0:T(8,128)(2,1)S(1)}, bf16[256,512]{1,0:T(8,128)(2,1)}, u32[]{:S(2)}) copy-start(bf16[256,512]{1,0:T(8,128)(2,1)} %tokens.7) | copy-start | bytes 786436
  0.0 4.0 %copy-start.2 = (bf16[1,512,192]{1,2,0:T(8,128)(2,1)S(1)}, bf16[1,512,192]{1,2,0:T(8,128)(2,1)}, u32[]{:S(2)}) copy-start(bf16[1,512,192]{1,2,0:T(8,128)(2,1)} %param.16) | copy-start | bytes 589828
  0.0 4.0 %copy-start.3 = (bf16[1,64,512]{2,1,0:T(8,128)(2,1)S(1)}, bf16[1,64,512]{2,1,0:T(8,128)(2,1)}, u32[]{:S(2)}) copy-start(bf16[1,64,512]{2,1,0:T(8,128)(2,1)} %attn_out.1) | copy-start | bytes 196612
  0.0 4.0 %copy-start.4 = (f32[256,16]{0,1:T(8,128)S(1)}, f32[256,16]{0,1:T(8,128)}, u32[]{:S(2)}) copy-start(f32[256,16]{0,1:T(8,128)} %param.11) | copy-start | bytes 49156
  0.0 4.0 %copy-start.7 = (s32[256]{0:T(256)S(1)}, s32[256]{0:T(256)}, u32[]{:S(2)}) copy-start(s32[256]{0:T(256)} %param.10) | copy-start | bytes 3076
  4.0 19.1 %copy-start = (bf16[1024,512]{1,0:T(8,128)(2,1)S(1)}, bf16[1024,512]{1,0:T(8,128)(2,1)}, u32[]{:S(2)}) copy-start(bf16[1024,512]{1,0:T(8,128)(2,1)} %out_weight.5) | copy-start | bytes 3145732
  4.0 19.1 %copy-start.5 = (f32[1024]{0:T(1024)S(1)}, f32[1024]{0:T(1024)}, u32[]{:S(2)}) copy-start(f32[1024]{0:T(1024)} %param.13) | copy-start | bytes 12292
  4.0 19.1 %copy-start.6 = (f32[512]{0:T(512)S(1)}, f32[512]{0:T(512)}, u32[]{:S(2)}) copy-start(f32[512]{0:T(512)} %param.15) | copy-start | bytes 6148
  7.3 8.5 %collective-permute-start.6 = (bf16[128,128]{1,0:T(8,128)(2,1)S(1)}, bf16[128,128]{1,0:T(8,128)(2,1)S(1)}, u32[]{:S(2)}, u32[]{:S(2)}) collective-permute-start(bf16[128,128]{1,0:T(8,128)(2,1)S(1)} %get-tuple-element.48), channel_id=1, source_target_pairs={{0,1},{1,0},{2,3},{3,2},{4,5},{5,4},{6,7},{7,6},{8,9},{9,8},{10,11... | collective-permute-start | bytes 98312 | tf_op jit(solution)/shard_map/ppermute | solution.py:270
  10.4 5.4 %collective-permute-start.7 = (bf16[128,128]{1,0:T(8,128)(2,1)S(1)}, bf16[128,128]{1,0:T(8,128)(2,1)S(1)}, u32[]{:S(2)}, u32[]{:S(2)}) collective-permute-start(bf16[128,128]{1,0:T(8,128)(2,1)S(1)} %get-tuple-element.48), channel_id=1, source_target_pairs={{0,2},{1,3},{2,0},{3,1},{4,6},{5,7},{6,4},{7,5},{8,10},{9,11},{10,... | collective-permute-start | bytes 98312 | tf_op jit(solution)/shard_map/ppermute | solution.py:270
  13.0 5.8 %collective-permute-start.8 = (bf16[128,128]{1,0:T(8,128)(2,1)S(1)}, bf16[128,128]{1,0:T(8,128)(2,1)S(1)}, u32[]{:S(2)}, u32[]{:S(2)}) collective-permute-start(bf16[128,128]{1,0:T(8,128)(2,1)S(1)} %get-tuple-element.48), channel_id=1, source_target_pairs={{0,3},{1,2},{2,1},{3,0},{4,7},{5,6},{6,5},{7,4},{8,11},{9,10},{10,... | collective-permute-start | bytes 98312 | tf_op jit(solution)/shard_map/ppermute | solution.py:270
  13.0 9.4 %collective-permute-start = (bf16[64,1024]{1,0:T(8,128)(2,1)S(1)}, bf16[64,1024]{1,0:T(8,128)(2,1)S(1)}, u32[]{:S(2)}, u32[]{:S(2)}) collective-permute-start(bf16[64,1024]{1,0:T(8,128)(2,1)S(1)} %get-tuple-element.27), channel_id=1, source_target_pairs={{0,1},{1,0},{4,5},{5,4},{8,9},{9,8},{12,13},{13,12},{16,17},{17,16... | collective-permute-start | bytes 393224 | tf_op jit(solution)/shard_map/ppermute | solution.py:339
  18.9 6.1 %collective-permute-start.9 = (bf16[512,128]{1,0:T(8,128)(2,1)S(1)}, bf16[512,128]{1,0:T(8,128)(2,1)S(1)}, u32[]{:S(2)}, u32[]{:S(2)}) collective-permute-start(bf16[512,128]{1,0:T(8,128)(2,1)S(1)} %constant_dynamic-update-slice_fusion.refs_0_), channel_id=1, source_target_pairs={{0,8},{4,12},{8,0},{12,4},{16,24},{20,28},{24,16},{28,20},{1,9},{5... | collective-permute-start | bytes 393224 | tf_op jit(solution)/shard_map/ppermute | solution.py:270
  20.4 5.8 %collective-permute-start.10 = (bf16[512,128]{1,0:T(8,128)(2,1)S(1)}, bf16[512,128]{1,0:T(8,128)(2,1)S(1)}, u32[]{:S(2)}, u32[]{:S(2)}) collective-permute-start(bf16[512,128]{1,0:T(8,128)(2,1)S(1)} %constant_dynamic-update-slice_fusion.refs_0_), channel_id=1, source_target_pairs={{0,16},{4,20},{8,24},{12,28},{16,0},{20,4},{24,8},{28,12},{1,17},{... | collective-permute-start | bytes 393224 | tf_op jit(solution)/shard_map/ppermute | solution.py:270
  21.9 5.9 %collective-permute-start.11 = (bf16[512,128]{1,0:T(8,128)(2,1)S(1)}, bf16[512,128]{1,0:T(8,128)(2,1)S(1)}, u32[]{:S(2)}, u32[]{:S(2)}) collective-permute-start(bf16[512,128]{1,0:T(8,128)(2,1)S(1)} %constant_dynamic-update-slice_fusion.refs_0_), channel_id=1, source_target_pairs={{0,24},{4,28},{8,16},{12,20},{16,8},{20,12},{24,0},{28,4},{1,25},{... | collective-permute-start | bytes 393224 | tf_op jit(solution)/shard_map/ppermute | solution.py:270
  22.4 6.2 %collective-permute-start.12 = (bf16[512,128]{1,0:T(8,128)(2,1)S(1)}, bf16[512,128]{1,0:T(8,128)(2,1)S(1)}, u32[]{:S(2)}, u32[]{:S(2)}) collective-permute-start(bf16[512,128]{1,0:T(8,128)(2,1)S(1)} %constant_dynamic-update-slice_fusion.refs_0_), channel_id=1, source_target_pairs={{0,4},{4,0},{8,12},{12,8},{16,20},{20,16},{24,28},{28,24},{1,5},{5... | collective-permute-start | bytes 393224 | tf_op jit(solution)/shard_map/ppermute | solution.py:270
  22.5 5.3 %collective-permute-start.1 = (bf16[64,1024]{1,0:T(8,128)(2,1)S(1)}, bf16[64,1024]{1,0:T(8,128)(2,1)S(1)}, u32[]{:S(2)}, u32[]{:S(2)}) collective-permute-start(bf16[64,1024]{1,0:T(8,128)(2,1)S(1)} %get-tuple-element.30), channel_id=1, source_target_pairs={{1,2},{2,1},{5,6},{6,5},{9,10},{10,9},{13,14},{14,13},{17,18},{18,... | collective-permute-start | bytes 393224 | tf_op jit(solution)/shard_map/ppermute | solution.py:339
  24.9 7.5 %collective-permute-start.13 = (bf16[512,128]{1,0:T(8,128)(2,1)S(1)}, bf16[512,128]{1,0:T(8,128)(2,1)S(1)}, u32[]{:S(2)}, u32[]{:S(2)}) collective-permute-start(bf16[512,128]{1,0:T(8,128)(2,1)S(1)} %collective-permute-done.9.refs_1_), channel_id=1, source_target_pairs={{0,4},{4,0},{8,12},{12,8},{16,20},{20,16},{24,28},{28,24},{1,5},{5... | collective-permute-start | bytes 393224 | tf_op jit(solution)/shard_map/ppermute | solution.py:270
  26.2 6.8 %collective-permute-start.14 = (bf16[512,128]{1,0:T(8,128)(2,1)S(1)}, bf16[512,128]{1,0:T(8,128)(2,1)S(1)}, u32[]{:S(2)}, u32[]{:S(2)}) collective-permute-start(bf16[512,128]{1,0:T(8,128)(2,1)S(1)} %collective-permute-done.10.refs_2_), channel_id=1, source_target_pairs={{0,4},{4,0},{8,12},{12,8},{16,20},{20,16},{24,28},{28,24},{1,5},{5... | collective-permute-start | bytes 393224 | tf_op jit(solution)/shard_map/ppermute | solution.py:270
  27.8 5.7 %collective-permute-start.15 = (bf16[512,128]{1,0:T(8,128)(2,1)S(1)}, bf16[512,128]{1,0:T(8,128)(2,1)S(1)}, u32[]{:S(2)}, u32[]{:S(2)}) collective-permute-start(bf16[512,128]{1,0:T(8,128)(2,1)S(1)} %collective-permute-done.11.refs_3_), channel_id=1, source_target_pairs={{0,4},{4,0},{8,12},{12,8},{16,20},{20,16},{24,28},{28,24},{1,5},{5... | collective-permute-start | bytes 393224 | tf_op jit(solution)/shard_map/ppermute | solution.py:270
  27.9 5.8 %collective-permute-start.2 = (bf16[64,1024]{1,0:T(8,128)(2,1)S(1)}, bf16[64,1024]{1,0:T(8,128)(2,1)S(1)}, u32[]{:S(2)}, u32[]{:S(2)}) collective-permute-start(bf16[64,1024]{1,0:T(8,128)(2,1)S(1)} %get-tuple-element.32), channel_id=1, source_target_pairs={{2,3},{3,2},{6,7},{7,6},{10,11},{11,10},{14,15},{15,14},{18,19},{1... | collective-permute-start | bytes 393224 | tf_op jit(solution)/shard_map/ppermute | solution.py:339
  28.6 13.5 %collective-permute-start.4 = (bf16[128,512]{1,0:T(8,128)(2,1)S(1)}, bf16[128,512]{1,0:T(8,128)(2,1)S(1)}, u32[]{:S(2)}, u32[]{:S(2)}) collective-permute-start(bf16[128,512]{1,0:T(8,128)(2,1)S(1)} %get-tuple-element.43.refs_1_), channel_id=1, source_target_pairs={{0,2},{1,3},{2,0},{3,1},{4,6},{5,7},{6,4},{7,5},{8,10},{9,11},{10,... | collective-permute-start | bytes 393224 | tf_op jit(solution)/shard_map/ppermute | solution.py:270
  32.5 10.3 %collective-permute-start.5 = (bf16[128,512]{1,0:T(8,128)(2,1)S(1)}, bf16[128,512]{1,0:T(8,128)(2,1)S(1)}, u32[]{:S(2)}, u32[]{:S(2)}) collective-permute-start(bf16[128,512]{1,0:T(8,128)(2,1)S(1)} %get-tuple-element.43.refs_1_), channel_id=1, source_target_pairs={{0,3},{1,2},{2,1},{3,0},{4,7},{5,6},{6,5},{7,4},{8,11},{9,10},{10,... | collective-permute-start | bytes 393224 | tf_op jit(solution)/shard_map/ppermute | solution.py:270
  33.0 9.8 %collective-permute-start.3 = (bf16[128,512]{1,0:T(8,128)(2,1)S(1)}, bf16[128,512]{1,0:T(8,128)(2,1)S(1)}, u32[]{:S(2)}, u32[]{:S(2)}) collective-permute-start(bf16[128,512]{1,0:T(8,128)(2,1)S(1)} %get-tuple-element.45.refs_1_), channel_id=1, source_target_pairs={{0,1},{1,0},{2,3},{3,2},{4,5},{5,4},{6,7},{7,6},{8,9},{9,8},{10,11... | collective-permute-start | bytes 393224 | tf_op jit(solution)/shard_map/ppermute | solution.py:270

commit v3 on v2

--- a/solution.py
+++ b/solution.py
@@ -42,10 +42,10 @@
 
 def spread(value, heads, width, count):
     size = width // heads
-    row = iota((heads, width), 0)
-    lane = iota((heads, width), 1)
+    row = lax.rem(iota((count * heads, width), 0), heads)
+    lane = iota((count * heads, width), 1)
     pick = ((lane >= row * size) & (lane < (row + 1) * size)).astype(BF16)
-    return sum(dot(term, pick) for term in terms(value, count))
+    return dot(jnp.concatenate(terms(value, count), axis=1), pick)
 
 
 def weight_copies(weight, buffer, sems, start, step):
@@ -59,9 +59,9 @@
 
 
 def front_kernel(
-    tokens_hbm, decay_hbm, weight,
+    split, tokens_hbm, decay_hbm, weight, qkv, attn_out,
     xs, bc, local, first, total, cumul,
-    tokens, decay, xs_buffer, bc_buffer, small_sems, xs_sems, bc_sems,
+    tokens, decay, stack, xs_buffer, bc_buffer, small_sems, xs_sems, bc_sems,
 ):
     heads, length = decay.shape
     width = xs.shape[1]
@@ -71,7 +71,19 @@
     xs_copy = weight_copies(weight, xs_buffer, xs_sems, 0, step)
     decay_copy = pltpu.make_async_copy(decay_hbm, decay, small_sems.at[0])
     token_copy = pltpu.make_async_copy(tokens_hbm, tokens, small_sems.at[1])
-    for copy in [decay_copy, token_copy] + bc_copy + xs_copy:
+    mine = lax.rem(lax.axis_index("grp"), split[0] * split[1])
+    lanes = stack.shape[1]
+    column = pl.ds(pl.multiple_of(lax.rem(mine, split[0]) * lanes, lanes), lanes)
+    upper_rows = qkv.shape[1]
+    qkv_copy = pltpu.make_async_copy(
+        qkv.at[0, :, column], stack.at[pl.ds(0, upper_rows)], small_sems.at[2]
+    )
+    out_copy = pltpu.make_async_copy(
+        attn_out.at[0, :, column],
+        stack.at[pl.ds(upper_rows, attn_out.shape[1])],
+        small_sems.at[3],
+    )
+    for copy in [decay_copy, token_copy] + bc_copy + xs_copy + [qkv_copy, out_copy]:
         copy.start()
 
     decay_copy.wait()
@@ -89,19 +101,29 @@
     both = dot(ins, bc_buffer[0]).astype(BF16)
     bc[...] = both
     for i, copy in enumerate(xs_copy):
-        lanes = slice(i * step, (i + 1) * step)
+        at = slice(i * step, (i + 1) * step)
         copy.wait()
         block = dot(ins, xs_buffer[i]).astype(BF16)
-        xs[:, lanes] = block
-        scaled = (block.astype(F32) * tails_wide[:, lanes]).astype(BF16)
+        xs[:, at] = block
+        scaled = (block.astype(F32) * tails_wide[:, at]).astype(BF16)
         state = dot_rows(both, scaled)[:states]
-        local[:, lanes] = state
-        first[:, lanes] = state.astype(BF16)
+        local[:, at] = state
+        first[:states, at] = state.astype(BF16)
+
+    qkv_copy.wait()
+    out_copy.wait()
+    tall = stack.shape[0] // split[1]
+    part = lax.div(mine, split[0])
+    piece = stack[pl.ds(pl.multiple_of(part * tall, tall), tall), :]
+    few = first.shape[0] - states
+    wide = stack.shape[1]
+    for i in range(width // wide):
+        first[states:, i * wide : (i + 1) * wide] = piece[i * few : (i + 1) * few]
 
 
 def middle_kernel(
-    split, tokens, decay, weight, cumul, xs, bc, groups, qkv, attn_out,
-    within, silu, grown, placing, cmat, piece,
+    tokens, decay, weight, cumul, xs, bc, groups,
+    within, silu, grown, placing, cmat,
     gate_buffer, gate_sems,
 ):
     heads, length = decay.shape
@@ -112,17 +134,6 @@
     copies = weight_copies(weight, gate_buffer, gate_sems, width, step)
     for copy in copies:
         copy.start()
-
-    mine = lax.rem(lax.axis_index("grp"), split[0] * split[1])
-    lanes = piece.shape[1]
-    column = pl.ds(pl.multiple_of(lax.rem(mine, split[0]) * lanes, lanes), lanes)
-    stack = jnp.concatenate([qkv[0, :, column], attn_out[0, :, column]], axis=0)
-    tall = piece.shape[0]
-    part = lax.div(mine, split[0])
-    chosen = stack[:tall]
-    for i in range(1, split[1]):
-        chosen = jnp.where(part == i, stack[i * tall : (i + 1) * tall], chosen)
-    piece[...] = chosen
 
     here = lax.axis_index("seq") * length
     count = groups.shape[1]
@@ -179,11 +190,19 @@
     sent[...] = (total[0:1, :] * value + local[...]).astype(BF16)
 
 
-def first_merge_kernel(step, came, total, local, state, sent):
+def first_merge_kernel(step, came, first, total, local, state, sent, bundle):
     taken = lax.axis_index("seq") == step + 1
-    value = jnp.where(taken, came[...].astype(F32), 0.0)
+    states = local.shape[0]
+    value = jnp.where(taken, came[:states, :].astype(F32), 0.0)
     state[...] = value.astype(BF16)
     sent[...] = (total[0:1, :] * value + local[...]).astype(BF16)
+    few = came.shape[0] - states
+    wide = bundle.shape[1]
+    count = local.shape[1] // wide
+    for j, source in enumerate((first, came)):
+        for i in range(count):
+            at = (j * count + i) * few
+            bundle[at : at + few, :] = source[states:, i * wide : (i + 1) * wide]
 
 
 def post_kernel(
@@ -213,55 +232,70 @@
         rows[...] = earlier[1][...] if earlier else jnp.zeros_like(rows)
 
 
-def weight_kernel(masks, split, *refs):
+def weight_kernel(masks, split, head_dim, *refs):
     bundles, out = refs[:-1], refs[-1]
     parts = out.shape[0] // split[1]
     lanes = bundles[0].shape[1]
     mine = lax.rem(lax.axis_index("grp"), split[0] * split[1])
-    tall = out.shape[1]
+    heads = out.shape[1] // head_dim
     for bundle, mask in zip(bundles, masks):
         source = mine ^ mask
         column = pl.ds(pl.multiple_of(lax.rem(source, split[0]) * lanes, lanes), lanes)
         part = lax.div(source, split[0]) * parts
-        for j in range(parts):
-            out[part + j, :, column] = bundle[j * tall : (j + 1) * tall, :]
-
-
-def attend_kernel(devices, length, *refs):
-    known, (hidden, weights, placing, groups, result) = refs[:devices], refs[devices:]
-    most = known[0].shape[0]
-    heads = devices
-    head_dim = weights.shape[1] // heads
+        for head in range(heads):
+            for j in range(parts):
+                at = (head * parts + j) * head_dim
+                out[part + j, head * head_dim : (head + 1) * head_dim, column] = bundle[
+                    at : at + head_dim, :
+                ]
+
+
+def own_kernel(devices, length, rows, weights, groups, query, keys, values, bias):
+    most = rows.shape[0]
+    own = rows[...]
+    query[...] = dot_lanes(own, weights[0]).astype(BF16)
+    keys[...] = dot_lanes(weights[1], own).astype(BF16)
+    values[...] = dot_lanes(own, weights[2]).astype(BF16)
     me = lax.axis_index("seq")
-    own = known[0][...]
-    known = jnp.concatenate([block[...] for block in known], axis=0)
-    query = dot_lanes(own, weights[0]).astype(BF16)
-    keys = dot_lanes(weights[1], known).astype(BF16)
-    values = dot_lanes(known, weights[2]).astype(BF16)
-
     slot = iota((most, most), 1)
-    allowed = [slot <= iota((most, most), 0)]
+    bias[:, :most] = jnp.where(slot <= iota((most, most), 0), 0.0, -jnp.inf)
     for back in range(1, devices):
         other = me ^ back
         start = other * length
         inside = (groups[...] >= start) & (groups[...] < start + length)
         count = jnp.sum(inside.astype(F32), axis=1, keepdims=True).astype(jnp.int32)
-        allowed.append(slot < jnp.where(other < me, count, 0))
-    allowed = jnp.concatenate(allowed, axis=1)
-
+        seen = slot < jnp.where(other < me, count, 0)
+        bias[:, back * most : (back + 1) * most] = jnp.where(seen, 0.0, -jnp.inf)
+
+
+def project_kernel(*refs):
+    rows, (weights, keys, values) = refs[:-3], refs[-3:]
+    block = sum(some[...] for some in rows)
+    keys[...] = dot_lanes(weights[1], block).astype(BF16)
+    values[...] = dot_lanes(block, weights[2]).astype(BF16)
+
+
+def attend_kernel(devices, *refs):
+    keys, refs = refs[:devices], refs[devices:]
+    values, refs = refs[:devices], refs[devices:]
+    query, bias, weights, hidden, placing, result = refs
+    heads = devices
+    head_dim = query.shape[1] // heads
+    known = jnp.concatenate([block[...] for block in keys], axis=1)
+    worth = jnp.concatenate([block[...] for block in values], axis=0)
+    hide = bias[...]
     outs = []
     for head in range(heads):
         lanes = slice(head * head_dim, (head + 1) * head_dim)
-        scores = dot(query[:, lanes], keys[lanes, :]) * head_dim ** (-0.5)
-        scores = jnp.where(allowed, scores, -jnp.inf)
+        scores = dot(query[:, lanes], known[lanes, :]) * head_dim ** (-0.5) + hide
         top = jnp.max(scores, axis=1, keepdims=True)
         expo = jnp.exp(scores - top)
-        probs = (expo / jnp.sum(expo, axis=1, keepdims=True)).astype(BF16)
-        outs.append(dot(probs, values[:, lanes]).astype(BF16))
+        share = 1.0 / jnp.sum(expo, axis=1, keepdims=True)
+        outs.append(dot((expo * share).astype(BF16), worth[:, lanes]).astype(BF16))
     joined = jnp.concatenate(outs, axis=1)
-    back = dot(joined, weights[3])
+    back = jnp.concatenate(terms(dot(joined, weights[3]), 2), axis=0)
     place = placing[...]
-    placed = sum(dot(place, term) for term in terms(back, 2))
+    placed = dot(jnp.concatenate([place, place], axis=1), back)
     result[...] = (hidden[...].astype(F32) + placed).astype(BF16)
 
 
@@ -302,8 +336,11 @@
     row_split = 2 if grps % (2 * lane_split) == 0 else 1
     split = (lane_split, row_split)
     tall = 4 * head_dim // row_split
+    lane_count = model // lane_split
+    extra = tall * lane_count // width
     step = min(256, width)
     chunks = width // step
+    wide = min(512, width)
     groups = group_pos.reshape(1, -1)
     decay = log_decay.T
     qkv = jnp.transpose(qkv_weight, (0, 2, 1))
@@ -311,57 +348,60 @@
     buffers = [pltpu.VMEM((chunks, model, step), BF16), pltpu.SemaphoreType.DMA((chunks,))]
 
     xs, bc, local, first, total, cumul = call(
-        front_kernel,
+        functools.partial(front_kernel, split),
         [
             ((length, width), BF16),
             ((length, 2 * states), BF16),
             ((states, width), F32),
-            ((states, width), BF16),
+            ((states + extra, width), BF16),
             ((8, width), F32),
             ((length, heads), F32),
         ],
-        [in_hbm(tokens), in_hbm(decay), in_hbm(in_weight)],
+        [in_hbm(tokens), in_hbm(decay), in_hbm(in_weight), in_hbm(qkv), in_hbm(attn_out)],
         3 * 10**9,
         [
             pltpu.VMEM(tokens.shape, BF16),
             pltpu.VMEM(decay.shape, F32),
-            buffers[0],
+            pltpu.VMEM((tall * row_split, lane_count), BF16),
+            pltpu.VMEM((width // wide, model, wide), BF16),
             pltpu.VMEM((1, model, 2 * states), BF16),
-            pltpu.SemaphoreType.DMA((2,)),
-            buffers[1],
+            pltpu.SemaphoreType.DMA((4,)),
+            pltpu.SemaphoreType.DMA((width // wide,)),
             pltpu.SemaphoreType.DMA((1,)),
         ],
-        [HBM, HBM, HBM],
+        [HBM] * 5,
     )
 
     def link(sent, step):
-        pairs = [(step, step + 1), (step + 1, step)]
+        pairs = [(step, step + 1)]
         return lax.ppermute(sent, "seq", pairs)
 
-    came = link(first, 0)
-
-    within, silu, grown, placing, cmat, piece = call(
-        functools.partial(middle_kernel, split),
+    came = swap(first, "seq", 1)
+
+    within, silu, grown, placing, cmat = call(
+        middle_kernel,
         [
             ((length, width), F32),
             ((length, width), F32),
             ((length, width), F32),
             ((length, most), BF16),
             ((length, states), BF16),
-            ((tall, model // lane_split), BF16),
         ],
-        [tokens, decay, in_hbm(in_weight), cumul, xs, bc, groups, qkv, attn_out],
+        [tokens, decay, in_hbm(in_weight), cumul, xs, bc, groups],
         3 * 10**9,
         buffers,
-        [VMEM, VMEM, HBM] + [VMEM] * 6,
-    )
-
-    pieces = [piece]
-    for mask in range(1, devices):
-        pieces.append(swap(piece, "seq", mask))
-    bundle = jnp.concatenate(
-        [p[i * head_dim : (i + 1) * head_dim] for i in range(tall // head_dim) for p in pieces], axis=0
-    )
+        [VMEM, VMEM, HBM] + [VMEM] * 4,
+    )
+
+    kernel = functools.partial(first_merge_kernel, 0)
+    outs = [((states, width), BF16)] * 2 + [((2 * tall, lane_count), BF16)]
+    state, sent, bundle = call(kernel, outs, [came, first, total, local], 10**8)
+    came = link(sent, 1)
+    mask = 2
+    while mask < devices:
+        other = swap(bundle, "seq", mask)
+        bundle = jnp.concatenate([bundle, other], axis=0)
+        mask *= 2
     bundles, masks = [bundle], [0]
     for mask in range(2, lane_split * row_split, 2):
         bundles.append(swap(bundle, "grp", mask))
@@ -371,18 +411,18 @@
             bundles.append(swap(bundles[i], "grp", 1))
             masks.append(masks[i] ^ 1)
     (weights,) = call(
-        functools.partial(weight_kernel, masks, split),
+        functools.partial(weight_kernel, masks, split, head_dim),
         [((4, devices * head_dim, model), BF16)],
         bundles,
         10**9,
     )
 
-    state, kept, blocks, done = None, [], {}, 0
+    kept, blocks, done = [], {}, 1
     bounds = stages(devices)
     for low, high in zip(bounds[:-1], bounds[1:]):
         while done < high - 1 and done < devices - 2:
-            ins = [came] + ([] if state is None else [state]) + [total, local]
-            kernel = functools.partial(first_merge_kernel if state is None else merge_kernel, done)
+            kernel = functools.partial(merge_kernel, done)
+            ins = [came, state, total, local]
             state, sent = call(kernel, [((states, width), BF16)] * 2, ins, 10**8)
             done += 1
             came = link(sent, done)
@@ -395,16 +435,29 @@
             2 * 10**9,
         )
         if high < devices:
-            for mask in range(devices // 2 if low == 0 else 1, devices):
-                if mask not in blocks:
-                    blocks[mask] = swap(kept[1], "seq", mask)
-
-    known = [kept[1]] + [blocks[mask] for mask in range(1, devices)]
+            for mask in range(1, devices):
+                pairs = [(i, i ^ mask) for i in range(low, high) if i < i ^ mask]
+                if pairs:
+                    blocks.setdefault(mask, []).append(lax.ppermute(kept[1], "seq", pairs))
+
+    inner_width = devices * head_dim
+    sides = [((inner_width, most), BF16), ((most, inner_width), BF16)]
+    query, key, value, bias = call(
+        functools.partial(own_kernel, devices, length),
+        [((most, inner_width), BF16)] + sides + [((most, devices * most), F32)],
+        [kept[1], weights, groups],
+        10**9,
+    )
+    keys, values = [key], [value]
+    for mask in range(1, devices):
+        key, value = call(project_kernel, sides, blocks[mask] + [weights], 5 * 10**8)
+        keys.append(key)
+        values.append(value)
     (result,) = call(
-        functools.partial(attend_kernel, devices, length),
+        functools.partial(attend_kernel, devices),
         [((length, model), BF16)],
-        known + [kept[0], weights, placing, groups],
-        3 * 10**9,
+        keys + values + [query, bias, weights, kept[0], placing],
+        2 * 10**9,
     )
     return result
 

time: 46.1 us -> 49.3 us (1.069)
  the two profiles are of different devices: /device:TPU:0 before, /device:TPU:24 now
where the time goes in v3:
time: 49.3 us; the launch traced here: 49.1 us
  waiting for transfers between devices  23.7 us (48%)
  starting transfers between devices  13.8 us (28%)
  Pallas kernels  11.3 us (23%)
    ppermute x9, waiting for transfers between devices, swap(): return lax.ppermute(value, axis, pairs)  14.1 us
    pallas_call x13, Pallas kernels, call(): return kernel(*ins)  11.3 us
    ppermute x4, waiting for transfers between devices, shards(): blocks.setdefault(mask, []).append(lax.ppermute(kept[1], 'seq', pairs))  8.12 us
    ppermute x9, starting transfers between devices, swap(): return lax.ppermute(value, axis, pairs)  7.3 us
    ppermute x4, starting transfers between devices, shards(): blocks.setdefault(mask, []).append(lax.ppermute(kept[1], 'seq', pairs))  4.55 us
    ppermute x2, starting transfers between devices, link(): return lax.ppermute(sent, 'seq', pairs)  1.96 us
    ppermute x2, waiting for transfers between devices, link(): return lax.ppermute(sent, 'seq', pairs)  1.54 us
  transfers between devices with their start and end apart: 15, of which 8 were waited for; matrix products, arithmetic and copies ran while one was open for 0% of the time, Pallas kernels for 11%

profile of v3, /device:TPU:24, one launch (start us, length us, event | category | flops | bytes accessed | tf_op | source)
XLA Modules:
  0.0 49.1 jit_solution(1449448213696931680)
XLA Ops:
  0.0 2.8 %shard_map.91 = (bf16[256,1024]{1,0:T(8,128)(2,1)S(1)}, bf16[256,128]{1,0:T(8,128)(2,1)S(1)}, f32[64,1024]{1,0:T(8,128)S(1)}, bf16[80,1024]{1,0:T(8,128)(2,1)S(1...) custom-call(bf16[256,512]{1,0:T(8,128)(2,1)} %tokens.7, f32[16,256]{1,0:T(8,128)} %bitcast.5, bf16[512,2176]{1,0:T(8,128)(2,1)} %weight.3, ...), custom_call_target="tpu_custom_call" | custom-call | flops 3000000000 | tf_op jit(solution)/shard_map/pallas_call | solution.py:321
  2.8 0.5 %collective-permute-start = (bf16[80,1024]{1,0:T(8,128)(2,1)S(1)}, bf16[80,1024]{1,0:T(8,128)(2,1)S(1)}, u32[]{:S(2)}, u32[]{:S(2)}) collective-permute-start(bf16[80,1024]{1,0:T(8,128)(2,1)S(1)} %get-tuple-element.37.first), channel_id=1, source_target_pairs={{0,1},{1,0},{2,3},{3,2},{4,5},{5,4},{6,7},{7,6},{8,9},{9,8},{10,11... | collective-permute-start | bytes 491528 | tf_op jit(solution)/shard_map/ppermute | solution.py:304
  3.4 3.1 %shard_map.94 = (f32[256,1024]{1,0:T(8,128)S(1)}, f32[256,1024]{1,0:T(8,128)S(1)}, f32[256,1024]{1,0:T(8,128)S(1)}, bf16[256,128]{1,0:T(8,128)(2,1)S(1)}, bf16[256,64]{1,0:T(8,128)(2,1)S(1)}) custom-call(bf16[256,512]{1,0:T(8,128)(2,1)S(1)} %copy-done.1, f32[16,256]{1,0:T(8,128)S(1)} %bitcast.6, bf16[512,2176]{1,0:T(8,128)(2,1)} %weight.3, ...), custom_call_target="tpu_custom_call" | custom-call | flops 3000000000 | tf_op jit(solution)/shard_map/pallas_call | solution.py:321
  6.5 2.3 %collective-permute-done.came = bf16[80,1024]{1,0:T(8,128)(2,1)S(1)} collective-permute-done((bf16[80,1024]{1,0:T(8,128)(2,1)S(1)}, bf16[80,1024]{1,0:T(8,128)(2,1)S(1)}, u32[]{:S(2)}, u32[]{:S(2)}) %collective-permute-start) | collective-permute-done | bytes 163872 | tf_op jit(solution)/shard_map/ppermute | solution.py:304
  8.9 0.7 %collective-permute-start.1 = (bf16[64,1024]{1,0:T(8,128)(2,1)S(1)}, bf16[64,1024]{1,0:T(8,128)(2,1)S(1)}, u32[]{:S(2)}, u32[]{:S(2)}) collective-permute-start(bf16[64,1024]{1,0:T(8,128)(2,1)S(1)} %get-tuple-element.40), channel_id=1, source_target_pairs={{1,2},{5,6},{9,10},{13,14},{17,18},{21,22},{25,26},{29,30}} | collective-permute-start | bytes 393224 | tf_op jit(solution)/shard_map/ppermute | solution.py:377
  9.5 3.2 %collective-permute-start.3 = (bf16[256,128]{1,0:T(8,128)(2,1)S(1)}, bf16[256,128]{1,0:T(8,128)(2,1)S(1)}, u32[]{:S(2)}, u32[]{:S(2)}) collective-permute-start(bf16[256,128]{1,0:T(8,128)(2,1)S(1)} %get-tuple-element.57), channel_id=1, source_target_pairs={{0,2},{1,3},{2,0},{3,1},{4,6},{5,7},{6,4},{7,5},{8,10},{9,11},{10,... | collective-permute-start | bytes 196616 | tf_op jit(solution)/shard_map/ppermute | solution.py:304
  12.8 1.3 %collective-permute-start.13 = (bf16[128,512]{1,0:T(8,128)(2,1)S(1)}, bf16[128,512]{1,0:T(8,128)(2,1)S(1)}, u32[]{:S(2)}, u32[]{:S(2)}) collective-permute-start(bf16[128,512]{1,0:T(8,128)(2,1)S(1)} %get-tuple-element.53.refs_1_), channel_id=1, source_target_pairs={{0,2},{1,3},{4,6},{5,7},{8,10},{9,11},{12,14},{13,15},{16,18},{17,... | collective-permute-start | bytes 393224 | tf_op jit(solution)/shard_map/ppermute | solution.py:441
  14.1 7.8 %collective-permute-done.3 = bf16[256,128]{1,0:T(8,128)(2,1)S(1)} collective-permute-done((bf16[256,128]{1,0:T(8,128)(2,1)S(1)}, bf16[256,128]{1,0:T(8,128)(2,1)S(1)}, u32[]{:S(2)}, u32[]{:S(2)}) %collective-permute-start.3) | collective-permute-done | bytes 65568 | tf_op jit(solution)/shard_map/ppermute | solution.py:304
  21.9 1.6 %collective-permute-start.4 = (bf16[512,128]{1,0:T(8,128)(2,1)S(1)}, bf16[512,128]{1,0:T(8,128)(2,1)S(1)}, u32[]{:S(2)}, u32[]{:S(2)}) collective-permute-start(bf16[512,128]{1,0:T(8,128)(2,1)S(1)} %constant_dynamic-update-slice_fusion.refs_0_), channel_id=1, source_target_pairs={{0,8},{4,12},{8,0},{12,4},{16,24},{20,28},{24,16},{28,20},{1,9},{5... | collective-permute-start | bytes 393224 | tf_op jit(solution)/shard_map/ppermute | solution.py:304
  23.5 1.5 %collective-permute-start.5 = (bf16[512,128]{1,0:T(8,128)(2,1)S(1)}, bf16[512,128]{1,0:T(8,128)(2,1)S(1)}, u32[]{:S(2)}, u32[]{:S(2)}) collective-permute-start(bf16[512,128]{1,0:T(8,128)(2,1)S(1)} %constant_dynamic-update-slice_fusion.refs_0_), channel_id=1, source_target_pairs={{0,16},{4,20},{8,24},{12,28},{16,0},{20,4},{24,8},{28,12},{1,17},{... | collective-permute-start | bytes 393224 | tf_op jit(solution)/shard_map/ppermute | solution.py:304
  25.0 0.5 collective-permute-start.6
  25.6 1.3 %collective-permute-start.2 = (bf16[64,1024]{1,0:T(8,128)(2,1)S(1)}, bf16[64,1024]{1,0:T(8,128)(2,1)S(1)}, u32[]{:S(2)}, u32[]{:S(2)}) collective-permute-start(bf16[64,1024]{1,0:T(8,128)(2,1)S(1)} %get-tuple-element.42), channel_id=1, source_target_pairs={{2,3},{6,7},{10,11},{14,15},{18,19},{22,23},{26,27},{30,31}} | collective-permute-start | bytes 393224 | tf_op jit(solution)/shard_map/ppermute | solution.py:377
  27.1 1.4 %collective-permute-done.5.refs_2_ = bf16[512,128]{1,0:T(8,128)(2,1)S(1)} collective-permute-done((bf16[512,128]{1,0:T(8,128)(2,1)S(1)}, bf16[512,128]{1,0:T(8,128)(2,1)S(1)}, u32[]{:S(2)}, u32[]{:S(2)}) %collective-permute-start.5) | collective-permute-done | bytes 131104 | tf_op jit(solution)/shard_map/ppermute | solution.py:304
  28.5 2.4 %collective-permute-done.6.refs_3_ = bf16[512,128]{1,0:T(8,128)(2,1)S(1)} collective-permute-done((bf16[512,128]{1,0:T(8,128)(2,1)S(1)}, bf16[512,128]{1,0:T(8,128)(2,1)S(1)}, u32[]{:S(2)}, u32[]{:S(2)}) %collective-permute-start.6) | collective-permute-done | bytes 131104 | tf_op jit(solution)/shard_map/ppermute | solution.py:304
  30.9 1.5 %collective-permute-done.2.state = bf16[64,1024]{1,0:T(8,128)(2,1)S(1)} collective-permute-done((bf16[64,1024]{1,0:T(8,128)(2,1)S(1)}, bf16[64,1024]{1,0:T(8,128)(2,1)S(1)}, u32[]{:S(2)}, u32[]{:S(2)}) %collective-permute-start.2) | collective-permute-done | bytes 131104 | tf_op jit(solution)/shard_map/ppermute | solution.py:377
  32.4 1.1 %shard_map.97 = (bf16[256,512]{1,0:T(8,128)(2,1)S(1)}, bf16[128,512]{1,0:T(8,128)(2,1)S(1)}) custom-call(bf16[64,1024]{1,0:T(8,128)(2,1)S(1)} %collective-permute-done.2.state, f32[256,1024]{1,0:T(8,128)S(1)} %get-tuple-element.46.within, f32[256,1024]{1,0:T(8,128)S(1)} %get-tuple-element.47.silu, f32[256,1024]{1,0:T(8,128)S(1)} %get-tuple-element.48.grown, ...), custom_call_target="tpu_custom_call" | custom-call | flops 2000000000 | tf_op jit(solution)/shard_map/pallas_call | solution.py:321
  33.5 0.7 %collective-permute-start.11 = (bf16[128,512]{1,0:T(8,128)(2,1)S(1)}, bf16[128,512]{1,0:T(8,128)(2,1)S(1)}, u32[]{:S(2)}, u32[]{:S(2)}) collective-permute-start(bf16[128,512]{1,0:T(8,128)(2,1)S(1)} %get-tuple-element.53.refs_1_), channel_id=1, source_target_pairs={{0,1},{4,5},{8,9},{12,13},{16,17},{20,21},{24,25},{28,29}} | collective-permute-start | bytes 393224 | tf_op jit(solution)/shard_map/ppermute | solution.py:441
  34.2 1.3 %collective-permute-start.14 = (bf16[128,512]{1,0:T(8,128)(2,1)S(1)}, bf16[128,512]{1,0:T(8,128)(2,1)S(1)}, u32[]{:S(2)}, u32[]{:S(2)}) collective-permute-start(bf16[128,512]{1,0:T(8,128)(2,1)S(1)} %get-tuple-element.53.refs_1_), channel_id=1, source_target_pairs={{0,3},{1,2},{4,7},{5,6},{8,11},{9,10},{12,15},{13,14},{16,19},{17,... | collective-permute-start | bytes 393224 | tf_op jit(solution)/shard_map/ppermute | solution.py:441
  35.5 1.3 %collective-permute-start.12 = (bf16[128,512]{1,0:T(8,128)(2,1)S(1)}, bf16[128,512]{1,0:T(8,128)(2,1)S(1)}, u32[]{:S(2)}, u32[]{:S(2)}) collective-permute-start(bf16[128,512]{1,0:T(8,128)(2,1)S(1)} %get-tuple-element.55.refs_1_), channel_id=1, source_target_pairs={{2,3},{6,7},{10,11},{14,15},{18,19},{22,23},{26,27},{30,31}} | collective-permute-start | bytes 393224 | tf_op jit(solution)/shard_map/ppermute | solution.py:441
  37.1 0.3 shard_map.101
  37.4 6.6 %collective-permute-done.14.refs_0_ = bf16[128,512]{1,0:T(8,128)(2,1)S(1)} collective-permute-done((bf16[128,512]{1,0:T(8,128)(2,1)S(1)}, bf16[128,512]{1,0:T(8,128)(2,1)S(1)}, u32[]{:S(2)}, u32[]{:S(2)}) %collective-permute-start.14) | collective-permute-done | bytes 131104 | tf_op jit(solution)/shard_map/ppermute | solution.py:441
  44.2 0.4 shard_map.99
  44.6 1.5 %collective-permute-done.12.refs_1_ = bf16[128,512]{1,0:T(8,128)(2,1)S(1)} collective-permute-done((bf16[128,512]{1,0:T(8,128)(2,1)S(1)}, bf16[128,512]{1,0:T(8,128)(2,1)S(1)}, u32[]{:S(2)}, u32[]{:S(2)}) %collective-permute-start.12) | collective-permute-done | bytes 131104 | tf_op jit(solution)/shard_map/ppermute | solution.py:441
  46.5 2.7 %shard_map.103 = bf16[256,512]{1,0:T(8,128)(2,1)} custom-call(bf16[256,128]{1,0:T(8,128)(2,1)S(1)} %get-tuple-element.58.refs_0_, bf16[256,128]{1,0:T(8,128)(2,1)S(1)} %get-tuple-element.59.refs_1_, bf16[256,128]{1,0:T(8,128)(2,1)S(1)} %get-tuple-element.60.refs_2_, bf16[256,128]{1,0:T(8,128)(2,1)S(1)} %get-tuple-element.61.refs_3_, ...), custom_call_target="tpu_custom_call" | custom-call | flops 2000000000 | tf_op jit(solution)/shard_map/pallas_call | solution.py:321
  (33 shorter events, 1.2 us)
Async XLA Ops:
  0.0 3.3 %copy-start.1 = (bf16[256,512]{1,0:T(8,128)(2,1)S(1)}, bf16[256,512]{1,0:T(8,128)(2,1)}, u32[]{:S(2)}) copy-start(bf16[256,512]{1,0:T(8,128)(2,1)} %tokens.7) | copy-start | bytes 786436
  0.0 3.3 %copy-start.2 = (f32[256,16]{0,1:T(8,128)S(1)}, f32[256,16]{0,1:T(8,128)}, u32[]{:S(2)}) copy-start(f32[256,16]{0,1:T(8,128)} %param.11) | copy-start | bytes 49156
  0.0 3.3 %copy-start.5 = (s32[256]{0:T(256)S(1)}, s32[256]{0:T(256)}, u32[]{:S(2)}) copy-start(s32[256]{0:T(256)} %param.10) | copy-start | bytes 3076
  2.8 6.0 %collective-permute-start = (bf16[80,1024]{1,0:T(8,128)(2,1)S(1)}, bf16[80,1024]{1,0:T(8,128)(2,1)S(1)}, u32[]{:S(2)}, u32[]{:S(2)}) collective-permute-start(bf16[80,1024]{1,0:T(8,128)(2,1)S(1)} %get-tuple-element.37.first), channel_id=1, source_target_pairs={{0,1},{1,0},{2,3},{3,2},{4,5},{5,4},{6,7},{7,6},{8,9},{9,8},{10,11... | collective-permute-start | bytes 491528 | tf_op jit(solution)/shard_map/ppermute | solution.py:304
  3.3 9.4 %copy-start = (bf16[1024,512]{1,0:T(8,128)(2,1)S(1)}, bf16[1024,512]{1,0:T(8,128)(2,1)}, u32[]{:S(2)}) copy-start(bf16[1024,512]{1,0:T(8,128)(2,1)} %out_weight.5) | copy-start | bytes 3145732
  3.3 9.4 %copy-start.3 = (f32[1024]{0:T(1024)S(1)}, f32[1024]{0:T(1024)}, u32[]{:S(2)}) copy-start(f32[1024]{0:T(1024)} %param.13) | copy-start | bytes 12292
  3.3 9.4 %copy-start.4 = (f32[512]{0:T(512)S(1)}, f32[512]{0:T(512)}, u32[]{:S(2)}) copy-start(f32[512]{0:T(512)} %param.15) | copy-start | bytes 6148
  8.9 16.6 %collective-permute-start.1 = (bf16[64,1024]{1,0:T(8,128)(2,1)S(1)}, bf16[64,1024]{1,0:T(8,128)(2,1)S(1)}, u32[]{:S(2)}, u32[]{:S(2)}) collective-permute-start(bf16[64,1024]{1,0:T(8,128)(2,1)S(1)} %get-tuple-element.40), channel_id=1, source_target_pairs={{1,2},{5,6},{9,10},{13,14},{17,18},{21,22},{25,26},{29,30}} | collective-permute-start | bytes 393224 | tf_op jit(solution)/shard_map/ppermute | solution.py:377
  9.5 12.4 %collective-permute-start.3 = (bf16[256,128]{1,0:T(8,128)(2,1)S(1)}, bf16[256,128]{1,0:T(8,128)(2,1)S(1)}, u32[]{:S(2)}, u32[]{:S(2)}) collective-permute-start(bf16[256,128]{1,0:T(8,128)(2,1)S(1)} %get-tuple-element.57), channel_id=1, source_target_pairs={{0,2},{1,3},{2,0},{3,1},{4,6},{5,7},{6,4},{7,5},{8,10},{9,11},{10,... | collective-permute-start | bytes 196616 | tf_op jit(solution)/shard_map/ppermute | solution.py:304
  12.8 24.2 %collective-permute-start.13 = (bf16[128,512]{1,0:T(8,128)(2,1)S(1)}, bf16[128,512]{1,0:T(8,128)(2,1)S(1)}, u32[]{:S(2)}, u32[]{:S(2)}) collective-permute-start(bf16[128,512]{1,0:T(8,128)(2,1)S(1)} %get-tuple-element.53.refs_1_), channel_id=1, source_target_pairs={{0,2},{1,3},{4,6},{5,7},{8,10},{9,11},{12,14},{13,15},{16,18},{17,... | collective-permute-start | bytes 393224 | tf_op jit(solution)/shard_map/ppermute | solution.py:441
  21.9 5.1 %collective-permute-start.4 = (bf16[512,128]{1,0:T(8,128)(2,1)S(1)}, bf16[512,128]{1,0:T(8,128)(2,1)S(1)}, u32[]{:S(2)}, u32[]{:S(2)}) collective-permute-start(bf16[512,128]{1,0:T(8,128)(2,1)S(1)} %constant_dynamic-update-slice_fusion.refs_0_), channel_id=1, source_target_pairs={{0,8},{4,12},{8,0},{12,4},{16,24},{20,28},{24,16},{28,20},{1,9},{5... | collective-permute-start | bytes 393224 | tf_op jit(solution)/shard_map/ppermute | solution.py:304
  23.5 5.0 %collective-permute-start.5 = (bf16[512,128]{1,0:T(8,128)(2,1)S(1)}, bf16[512,128]{1,0:T(8,128)(2,1)S(1)}, u32[]{:S(2)}, u32[]{:S(2)}) collective-permute-start(bf16[512,128]{1,0:T(8,128)(2,1)S(1)} %constant_dynamic-update-slice_fusion.refs_0_), channel_id=1, source_target_pairs={{0,16},{4,20},{8,24},{12,28},{16,0},{20,4},{24,8},{28,12},{1,17},{... | collective-permute-start | bytes 393224 | tf_op jit(solution)/shard_map/ppermute | solution.py:304
  25.0 5.9 %collective-permute-start.6 = (bf16[512,128]{1,0:T(8,128)(2,1)S(1)}, bf16[512,128]{1,0:T(8,128)(2,1)S(1)}, u32[]{:S(2)}, u32[]{:S(2)}) collective-permute-start(bf16[512,128]{1,0:T(8,128)(2,1)S(1)} %constant_dynamic-update-slice_fusion.refs_0_), channel_id=1, source_target_pairs={{0,24},{4,28},{8,16},{12,20},{16,8},{20,12},{24,0},{28,4},{1,25},{... | collective-permute-start | bytes 393224 | tf_op jit(solution)/shard_map/ppermute | solution.py:304
  25.6 6.9 %collective-permute-start.2 = (bf16[64,1024]{1,0:T(8,128)(2,1)S(1)}, bf16[64,1024]{1,0:T(8,128)(2,1)S(1)}, u32[]{:S(2)}, u32[]{:S(2)}) collective-permute-start(bf16[64,1024]{1,0:T(8,128)(2,1)S(1)} %get-tuple-element.42), channel_id=1, source_target_pairs={{2,3},{6,7},{10,11},{14,15},{18,19},{22,23},{26,27},{30,31}} | collective-permute-start | bytes 393224 | tf_op jit(solution)/shard_map/ppermute | solution.py:377
  27.1 6.5 %collective-permute-start.7 = (bf16[512,128]{1,0:T(8,128)(2,1)S(1)}, bf16[512,128]{1,0:T(8,128)(2,1)S(1)}, u32[]{:S(2)}, u32[]{:S(2)}) collective-permute-start(bf16[512,128]{1,0:T(8,128)(2,1)S(1)} %constant_dynamic-update-slice_fusion.refs_0_), channel_id=1, source_target_pairs={{0,4},{4,0},{8,12},{12,8},{16,20},{20,16},{24,28},{28,24},{1,5},{5... | collective-permute-start | bytes 393224 | tf_op jit(solution)/shard_map/ppermute | solution.py:304
  28.5 5.8 %collective-permute-start.8 = (bf16[512,128]{1,0:T(8,128)(2,1)S(1)}, bf16[512,128]{1,0:T(8,128)(2,1)S(1)}, u32[]{:S(2)}, u32[]{:S(2)}) collective-permute-start(bf16[512,128]{1,0:T(8,128)(2,1)S(1)} %collective-permute-done.4.refs_1_), channel_id=1, source_target_pairs={{0,4},{4,0},{8,12},{12,8},{16,20},{20,16},{24,28},{28,24},{1,5},{5... | collective-permute-start | bytes 393224 | tf_op jit(solution)/shard_map/ppermute | solution.py:304
  30.9 4.6 %collective-permute-start.9 = (bf16[512,128]{1,0:T(8,128)(2,1)S(1)}, bf16[512,128]{1,0:T(8,128)(2,1)S(1)}, u32[]{:S(2)}, u32[]{:S(2)}) collective-permute-start(bf16[512,128]{1,0:T(8,128)(2,1)S(1)} %collective-permute-done.5.refs_2_), channel_id=1, source_target_pairs={{0,4},{4,0},{8,12},{12,8},{16,20},{20,16},{24,28},{28,24},{1,5},{5... | collective-permute-start | bytes 393224 | tf_op jit(solution)/shard_map/ppermute | solution.py:304
  32.4 4.4 %collective-permute-start.10 = (bf16[512,128]{1,0:T(8,128)(2,1)S(1)}, bf16[512,128]{1,0:T(8,128)(2,1)S(1)}, u32[]{:S(2)}, u32[]{:S(2)}) collective-permute-start(bf16[512,128]{1,0:T(8,128)(2,1)S(1)} %collective-permute-done.6.refs_3_), channel_id=1, source_target_pairs={{0,4},{4,0},{8,12},{12,8},{16,20},{20,16},{24,28},{28,24},{1,5},{5... | collective-permute-start | bytes 393224 | tf_op jit(solution)/shard_map/ppermute | solution.py:304
  33.5 11.1 %collective-permute-start.11 = (bf16[128,512]{1,0:T(8,128)(2,1)S(1)}, bf16[128,512]{1,0:T(8,128)(2,1)S(1)}, u32[]{:S(2)}, u32[]{:S(2)}) collective-permute-start(bf16[128,512]{1,0:T(8,128)(2,1)S(1)} %get-tuple-element.53.refs_1_), channel_id=1, source_target_pairs={{0,1},{4,5},{8,9},{12,13},{16,17},{20,21},{24,25},{28,29}} | collective-permute-start | bytes 393224 | tf_op jit(solution)/shard_map/ppermute | solution.py:441
  34.2 9.7 %collective-permute-start.14 = (bf16[128,512]{1,0:T(8,128)(2,1)S(1)}, bf16[128,512]{1,0:T(8,128)(2,1)S(1)}, u32[]{:S(2)}, u32[]{:S(2)}) collective-permute-start(bf16[128,512]{1,0:T(8,128)(2,1)S(1)} %get-tuple-element.53.refs_1_), channel_id=1, source_target_pairs={{0,3},{1,2},{4,7},{5,6},{8,11},{9,10},{12,15},{13,14},{16,19},{17,... | collective-permute-start | bytes 393224 | tf_op jit(solution)/shard_map/ppermute | solution.py:441
  35.5 10.6 %collective-permute-start.12 = (bf16[128,512]{1,0:T(8,128)(2,1)S(1)}, bf16[128,512]{1,0:T(8,128)(2,1)S(1)}, u32[]{:S(2)}, u32[]{:S(2)}) collective-permute-start(bf16[128,512]{1,0:T(8,128)(2,1)S(1)} %get-tuple-element.55.refs_1_), channel_id=1, source_target_pairs={{2,3},{6,7},{10,11},{14,15},{18,19},{22,23},{26,27},{30,31}} | collective-permute-start | bytes 393224 | tf_op jit(solution)/shard_map/ppermute | solution.py:441

commit v4 on v3

--- a/solution.py
+++ b/solution.py
@@ -268,11 +268,21 @@
         bias[:, back * most : (back + 1) * most] = jnp.where(seen, 0.0, -jnp.inf)
 
 
-def project_kernel(*refs):
+def project_kernel(mask, *refs):
     rows, (weights, keys, values) = refs[:-3], refs[-3:]
-    block = sum(some[...] for some in rows)
-    keys[...] = dot_lanes(weights[1], block).astype(BF16)
-    values[...] = dot_lanes(block, weights[2]).astype(BF16)
+    me = lax.axis_index("seq")
+    earlier = (me ^ mask) < me
+
+    @pl.when(earlier)
+    def _():
+        block = sum(some[...] for some in rows)
+        keys[...] = dot_lanes(weights[1], block).astype(BF16)
+        values[...] = dot_lanes(block, weights[2]).astype(BF16)
+
+    @pl.when(jnp.logical_not(earlier))
+    def _():
+        keys[...] = jnp.zeros_like(keys)
+        values[...] = jnp.zeros_like(values)
 
 
 def attend_kernel(devices, *refs):
@@ -419,7 +429,7 @@
 
     kept, blocks, done = [], {}, 1
     bounds = stages(devices)
-    for low, high in zip(bounds[:-1], bounds[1:]):
+    for at, (low, high) in enumerate(zip(bounds[:-1], bounds[1:])):
         while done < high - 1 and done < devices - 2:
             kernel = functools.partial(merge_kernel, done)
             ins = [came, state, total, local]
@@ -436,8 +446,10 @@
         )
         if high < devices:
             for mask in range(1, devices):
-                pairs = [(i, i ^ mask) for i in range(low, high) if i < i ^ mask]
-                if pairs:
+                far = mask >= devices // 2
+                first_source = 0 if far and at == 1 else low
+                pairs = [(i, i ^ mask) for i in range(first_source, high) if i < i ^ mask]
+                if pairs and not (far and low == 0):
                     blocks.setdefault(mask, []).append(lax.ppermute(kept[1], "seq", pairs))
 
     inner_width = devices * head_dim
@@ -450,7 +462,8 @@
     )
     keys, values = [key], [value]
     for mask in range(1, devices):
-        key, value = call(project_kernel, sides, blocks[mask] + [weights], 5 * 10**8)
+        kernel = functools.partial(project_kernel, mask)
+        key, value = call(kernel, sides, blocks[mask] + [weights], 5 * 10**8)
         keys.append(key)
         values.append(value)
     (result,) = call(
@@ -463,7 +476,7 @@
 
 
 def stages(devices):
-    return sorted({0, devices // 2, devices - 1, devices})
+    return sorted({0, 1, devices // 2, devices - 1, devices})
 
 
 def solution(mesh):

time: 49.3 us -> 49.4 us (level)
    pallas_call x13 -> x14, Pallas kernels: 11.3 us -> 11.4 us  [call(): return kernel(*ins)]
where the time goes in v4:
time: 49.4 us; the launch traced here: 49.1 us
  waiting for transfers between devices  23.7 us (48%)
  starting transfers between devices  13.8 us (28%)
  Pallas kernels  11.4 us (23%)
    ppermute x9, waiting for transfers between devices, swap(): return lax.ppermute(value, axis, pairs)  14 us
    pallas_call x14, Pallas kernels, call(): return kernel(*ins)  11.4 us
    ppermute x4, waiting for transfers between devices, shards(): blocks.setdefault(mask, []).append(lax.ppermute(kept[1], 'seq', pairs))  8.1 us
    ppermute x9, starting transfers between devices, swap(): return lax.ppermute(value, axis, pairs)  7.3 us
    ppermute x4, starting transfers between devices, shards(): blocks.setdefault(mask, []).append(lax.ppermute(kept[1], 'seq', pairs))  4.55 us
    ppermute x2, starting transfers between devices, link(): return lax.ppermute(sent, 'seq', pairs)  1.96 us
    ppermute x2, waiting for transfers between devices, link(): return lax.ppermute(sent, 'seq', pairs)  1.54 us
  transfers between devices with their start and end apart: 15, of which 8 were waited for; matrix products, arithmetic and copies ran while one was open for 0% of the time, Pallas kernels for 11%

profile of v4, /device:TPU:24, one launch (start us, length us, event | category | flops | bytes accessed | tf_op | source)
XLA Modules:
  0.0 49.1 jit_solution(12185555512981678035)
XLA Ops:
  0.0 2.8 %shard_map.91 = (bf16[256,1024]{1,0:T(8,128)(2,1)S(1)}, bf16[256,128]{1,0:T(8,128)(2,1)S(1)}, f32[64,1024]{1,0:T(8,128)S(1)}, bf16[80,1024]{1,0:T(8,128)(2,1)S(1...) custom-call(bf16[256,512]{1,0:T(8,128)(2,1)} %tokens.9, f32[16,256]{1,0:T(8,128)} %bitcast.5, bf16[512,2176]{1,0:T(8,128)(2,1)} %weight.3, ...), custom_call_target="tpu_custom_call" | custom-call | flops 3000000000 | tf_op jit(solution)/shard_map/pallas_call | solution.py:331
  2.8 0.5 %collective-permute-start = (bf16[80,1024]{1,0:T(8,128)(2,1)S(1)}, bf16[80,1024]{1,0:T(8,128)(2,1)S(1)}, u32[]{:S(2)}, u32[]{:S(2)}) collective-permute-start(bf16[80,1024]{1,0:T(8,128)(2,1)S(1)} %get-tuple-element.39.first), channel_id=1, source_target_pairs={{0,1},{1,0},{2,3},{3,2},{4,5},{5,4},{6,7},{7,6},{8,9},{9,8},{10,11... | collective-permute-start | bytes 491528 | tf_op jit(solution)/shard_map/ppermute | solution.py:314
  3.4 3.1 %shard_map.94 = (f32[256,1024]{1,0:T(8,128)S(1)}, f32[256,1024]{1,0:T(8,128)S(1)}, f32[256,1024]{1,0:T(8,128)S(1)}, bf16[256,128]{1,0:T(8,128)(2,1)S(1)}, bf16[256,64]{1,0:T(8,128)(2,1)S(1)}) custom-call(bf16[256,512]{1,0:T(8,128)(2,1)S(1)} %copy-done.1, f32[16,256]{1,0:T(8,128)S(1)} %bitcast.6, bf16[512,2176]{1,0:T(8,128)(2,1)} %weight.3, ...), custom_call_target="tpu_custom_call" | custom-call | flops 3000000000 | tf_op jit(solution)/shard_map/pallas_call | solution.py:331
  6.5 2.3 %collective-permute-done.came = bf16[80,1024]{1,0:T(8,128)(2,1)S(1)} collective-permute-done((bf16[80,1024]{1,0:T(8,128)(2,1)S(1)}, bf16[80,1024]{1,0:T(8,128)(2,1)S(1)}, u32[]{:S(2)}, u32[]{:S(2)}) %collective-permute-start) | collective-permute-done | bytes 163872 | tf_op jit(solution)/shard_map/ppermute | solution.py:314
  8.9 0.7 %collective-permute-start.1 = (bf16[64,1024]{1,0:T(8,128)(2,1)S(1)}, bf16[64,1024]{1,0:T(8,128)(2,1)S(1)}, u32[]{:S(2)}, u32[]{:S(2)}) collective-permute-start(bf16[64,1024]{1,0:T(8,128)(2,1)S(1)} %get-tuple-element.42), channel_id=1, source_target_pairs={{1,2},{5,6},{9,10},{13,14},{17,18},{21,22},{25,26},{29,30}} | collective-permute-start | bytes 393224 | tf_op jit(solution)/shard_map/ppermute | solution.py:387
  9.5 3.2 %collective-permute-start.3 = (bf16[256,128]{1,0:T(8,128)(2,1)S(1)}, bf16[256,128]{1,0:T(8,128)(2,1)S(1)}, u32[]{:S(2)}, u32[]{:S(2)}) collective-permute-start(bf16[256,128]{1,0:T(8,128)(2,1)S(1)} %get-tuple-element.61), channel_id=1, source_target_pairs={{0,2},{1,3},{2,0},{3,1},{4,6},{5,7},{6,4},{7,5},{8,10},{9,11},{10,... | collective-permute-start | bytes 196616 | tf_op jit(solution)/shard_map/ppermute | solution.py:314
  12.9 1.3 %collective-permute-start.13 = (bf16[128,512]{1,0:T(8,128)(2,1)S(1)}, bf16[128,512]{1,0:T(8,128)(2,1)S(1)}, u32[]{:S(2)}, u32[]{:S(2)}) collective-permute-start(bf16[128,512]{1,0:T(8,128)(2,1)S(1)} %get-tuple-element.57.refs_1_), channel_id=1, source_target_pairs={{0,2},{1,3},{4,6},{5,7},{8,10},{9,11},{12,14},{13,15},{16,18},{17,... | collective-permute-start | bytes 393224 | tf_op jit(solution)/shard_map/ppermute | solution.py:453
  14.2 7.7 %collective-permute-done.3 = bf16[256,128]{1,0:T(8,128)(2,1)S(1)} collective-permute-done((bf16[256,128]{1,0:T(8,128)(2,1)S(1)}, bf16[256,128]{1,0:T(8,128)(2,1)S(1)}, u32[]{:S(2)}, u32[]{:S(2)}) %collective-permute-start.3) | collective-permute-done | bytes 65568 | tf_op jit(solution)/shard_map/ppermute | solution.py:314
  21.9 1.6 %collective-permute-start.4 = (bf16[512,128]{1,0:T(8,128)(2,1)S(1)}, bf16[512,128]{1,0:T(8,128)(2,1)S(1)}, u32[]{:S(2)}, u32[]{:S(2)}) collective-permute-start(bf16[512,128]{1,0:T(8,128)(2,1)S(1)} %constant_dynamic-update-slice_fusion.refs_0_), channel_id=1, source_target_pairs={{0,8},{4,12},{8,0},{12,4},{16,24},{20,28},{24,16},{28,20},{1,9},{5... | collective-permute-start | bytes 393224 | tf_op jit(solution)/shard_map/ppermute | solution.py:314
  23.5 1.5 %collective-permute-start.5 = (bf16[512,128]{1,0:T(8,128)(2,1)S(1)}, bf16[512,128]{1,0:T(8,128)(2,1)S(1)}, u32[]{:S(2)}, u32[]{:S(2)}) collective-permute-start(bf16[512,128]{1,0:T(8,128)(2,1)S(1)} %constant_dynamic-update-slice_fusion.refs_0_), channel_id=1, source_target_pairs={{0,16},{4,20},{8,24},{12,28},{16,0},{20,4},{24,8},{28,12},{1,17},{... | collective-permute-start | bytes 393224 | tf_op jit(solution)/shard_map/ppermute | solution.py:314
  25.0 0.5 collective-permute-start.6
  25.6 1.3 %collective-permute-start.2 = (bf16[64,1024]{1,0:T(8,128)(2,1)S(1)}, bf16[64,1024]{1,0:T(8,128)(2,1)S(1)}, u32[]{:S(2)}, u32[]{:S(2)}) collective-permute-start(bf16[64,1024]{1,0:T(8,128)(2,1)S(1)} %get-tuple-element.44), channel_id=1, source_target_pairs={{2,3},{6,7},{10,11},{14,15},{18,19},{22,23},{26,27},{30,31}} | collective-permute-start | bytes 393224 | tf_op jit(solution)/shard_map/ppermute | solution.py:387
  27.1 1.4 %collective-permute-done.5.refs_2_ = bf16[512,128]{1,0:T(8,128)(2,1)S(1)} collective-permute-done((bf16[512,128]{1,0:T(8,128)(2,1)S(1)}, bf16[512,128]{1,0:T(8,128)(2,1)S(1)}, u32[]{:S(2)}, u32[]{:S(2)}) %collective-permute-start.5) | collective-permute-done | bytes 131104 | tf_op jit(solution)/shard_map/ppermute | solution.py:314
  28.5 2.4 %collective-permute-done.6.refs_3_ = bf16[512,128]{1,0:T(8,128)(2,1)S(1)} collective-permute-done((bf16[512,128]{1,0:T(8,128)(2,1)S(1)}, bf16[512,128]{1,0:T(8,128)(2,1)S(1)}, u32[]{:S(2)}, u32[]{:S(2)}) %collective-permute-start.6) | collective-permute-done | bytes 131104 | tf_op jit(solution)/shard_map/ppermute | solution.py:314
  30.9 1.5 %collective-permute-done.2.state = bf16[64,1024]{1,0:T(8,128)(2,1)S(1)} collective-permute-done((bf16[64,1024]{1,0:T(8,128)(2,1)S(1)}, bf16[64,1024]{1,0:T(8,128)(2,1)S(1)}, u32[]{:S(2)}, u32[]{:S(2)}) %collective-permute-start.2) | collective-permute-done | bytes 131104 | tf_op jit(solution)/shard_map/ppermute | solution.py:387
  32.4 1.1 %shard_map.98 = (bf16[256,512]{1,0:T(8,128)(2,1)S(1)}, bf16[128,512]{1,0:T(8,128)(2,1)S(1)}) custom-call(bf16[64,1024]{1,0:T(8,128)(2,1)S(1)} %collective-permute-done.2.state, f32[256,1024]{1,0:T(8,128)S(1)} %get-tuple-element.48.within, f32[256,1024]{1,0:T(8,128)S(1)} %get-tuple-element.49.silu, f32[256,1024]{1,0:T(8,128)S(1)} %get-tuple-element.50.grown, ...), custom_call_target="tpu_custom_call" | custom-call | flops 2000000000 | tf_op jit(solution)/shard_map/pallas_call | solution.py:331
  33.5 0.7 %collective-permute-start.11 = (bf16[128,512]{1,0:T(8,128)(2,1)S(1)}, bf16[128,512]{1,0:T(8,128)(2,1)S(1)}, u32[]{:S(2)}, u32[]{:S(2)}) collective-permute-start(bf16[128,512]{1,0:T(8,128)(2,1)S(1)} %get-tuple-element.55.refs_1_), channel_id=1, source_target_pairs={{0,1},{4,5},{8,9},{12,13},{16,17},{20,21},{24,25},{28,29}} | collective-permute-start | bytes 393224 | tf_op jit(solution)/shard_map/ppermute | solution.py:453
  34.2 1.3 %collective-permute-start.14 = (bf16[128,512]{1,0:T(8,128)(2,1)S(1)}, bf16[128,512]{1,0:T(8,128)(2,1)S(1)}, u32[]{:S(2)}, u32[]{:S(2)}) collective-permute-start(bf16[128,512]{1,0:T(8,128)(2,1)S(1)} %get-tuple-element.57.refs_1_), channel_id=1, source_target_pairs={{0,3},{1,2},{4,7},{5,6},{8,11},{9,10},{12,15},{13,14},{16,19},{17,... | collective-permute-start | bytes 393224 | tf_op jit(solution)/shard_map/ppermute | solution.py:453
  35.5 1.3 %collective-permute-start.12 = (bf16[128,512]{1,0:T(8,128)(2,1)S(1)}, bf16[128,512]{1,0:T(8,128)(2,1)S(1)}, u32[]{:S(2)}, u32[]{:S(2)}) collective-permute-start(bf16[128,512]{1,0:T(8,128)(2,1)S(1)} %get-tuple-element.59.refs_1_), channel_id=1, source_target_pairs={{2,3},{6,7},{10,11},{14,15},{18,19},{22,23},{26,27},{30,31}} | collective-permute-start | bytes 393224 | tf_op jit(solution)/shard_map/ppermute | solution.py:453
  37.1 0.3 shard_map.102
  37.4 6.6 %collective-permute-done.14.refs_0_ = bf16[128,512]{1,0:T(8,128)(2,1)S(1)} collective-permute-done((bf16[128,512]{1,0:T(8,128)(2,1)S(1)}, bf16[128,512]{1,0:T(8,128)(2,1)S(1)}, u32[]{:S(2)}, u32[]{:S(2)}) %collective-permute-start.14) | collective-permute-done | bytes 131104 | tf_op jit(solution)/shard_map/ppermute | solution.py:453
  44.2 0.4 shard_map.100
  44.6 1.5 %collective-permute-done.12.refs_1_ = bf16[128,512]{1,0:T(8,128)(2,1)S(1)} collective-permute-done((bf16[128,512]{1,0:T(8,128)(2,1)S(1)}, bf16[128,512]{1,0:T(8,128)(2,1)S(1)}, u32[]{:S(2)}, u32[]{:S(2)}) %collective-permute-start.12) | collective-permute-done | bytes 131104 | tf_op jit(solution)/shard_map/ppermute | solution.py:453
  46.5 2.7 %shard_map.104 = bf16[256,512]{1,0:T(8,128)(2,1)} custom-call(bf16[256,128]{1,0:T(8,128)(2,1)S(1)} %get-tuple-element.62.refs_0_, bf16[256,128]{1,0:T(8,128)(2,1)S(1)} %get-tuple-element.63.refs_1_, bf16[256,128]{1,0:T(8,128)(2,1)S(1)} %get-tuple-element.64.refs_2_, bf16[256,128]{1,0:T(8,128)(2,1)S(1)} %get-tuple-element.65.refs_3_, ...), custom_call_target="tpu_custom_call" | custom-call | flops 2000000000 | tf_op jit(solution)/shard_map/pallas_call | solution.py:331
  (34 shorter events, 1.3 us)
Async XLA Ops:
  0.0 3.3 %copy-start.1 = (bf16[256,512]{1,0:T(8,128)(2,1)S(1)}, bf16[256,512]{1,0:T(8,128)(2,1)}, u32[]{:S(2)}) copy-start(bf16[256,512]{1,0:T(8,128)(2,1)} %tokens.9) | copy-start | bytes 786436
  0.0 3.3 %copy-start.2 = (f32[256,16]{0,1:T(8,128)S(1)}, f32[256,16]{0,1:T(8,128)}, u32[]{:S(2)}) copy-start(f32[256,16]{0,1:T(8,128)} %param.11) | copy-start | bytes 49156
  0.0 3.3 %copy-start.5 = (s32[256]{0:T(256)S(1)}, s32[256]{0:T(256)}, u32[]{:S(2)}) copy-start(s32[256]{0:T(256)} %param.10) | copy-start | bytes 3076
  2.8 6.0 %collective-permute-start = (bf16[80,1024]{1,0:T(8,128)(2,1)S(1)}, bf16[80,1024]{1,0:T(8,128)(2,1)S(1)}, u32[]{:S(2)}, u32[]{:S(2)}) collective-permute-start(bf16[80,1024]{1,0:T(8,128)(2,1)S(1)} %get-tuple-element.39.first), channel_id=1, source_target_pairs={{0,1},{1,0},{2,3},{3,2},{4,5},{5,4},{6,7},{7,6},{8,9},{9,8},{10,11... | collective-permute-start | bytes 491528 | tf_op jit(solution)/shard_map/ppermute | solution.py:314
  3.3 9.4 %copy-start = (bf16[1024,512]{1,0:T(8,128)(2,1)S(1)}, bf16[1024,512]{1,0:T(8,128)(2,1)}, u32[]{:S(2)}) copy-start(bf16[1024,512]{1,0:T(8,128)(2,1)} %out_weight.7) | copy-start | bytes 3145732
  3.3 9.4 %copy-start.3 = (f32[1024]{0:T(1024)S(1)}, f32[1024]{0:T(1024)}, u32[]{:S(2)}) copy-start(f32[1024]{0:T(1024)} %param.13) | copy-start | bytes 12292
  3.3 9.4 %copy-start.4 = (f32[512]{0:T(512)S(1)}, f32[512]{0:T(512)}, u32[]{:S(2)}) copy-start(f32[512]{0:T(512)} %param.15) | copy-start | bytes 6148
  8.9 16.6 %collective-permute-start.1 = (bf16[64,1024]{1,0:T(8,128)(2,1)S(1)}, bf16[64,1024]{1,0:T(8,128)(2,1)S(1)}, u32[]{:S(2)}, u32[]{:S(2)}) collective-permute-start(bf16[64,1024]{1,0:T(8,128)(2,1)S(1)} %get-tuple-element.42), channel_id=1, source_target_pairs={{1,2},{5,6},{9,10},{13,14},{17,18},{21,22},{25,26},{29,30}} | collective-permute-start | bytes 393224 | tf_op jit(solution)/shard_map/ppermute | solution.py:387
  9.5 12.4 %collective-permute-start.3 = (bf16[256,128]{1,0:T(8,128)(2,1)S(1)}, bf16[256,128]{1,0:T(8,128)(2,1)S(1)}, u32[]{:S(2)}, u32[]{:S(2)}) collective-permute-start(bf16[256,128]{1,0:T(8,128)(2,1)S(1)} %get-tuple-element.61), channel_id=1, source_target_pairs={{0,2},{1,3},{2,0},{3,1},{4,6},{5,7},{6,4},{7,5},{8,10},{9,11},{10,... | collective-permute-start | bytes 196616 | tf_op jit(solution)/shard_map/ppermute | solution.py:314
  12.9 24.2 %collective-permute-start.13 = (bf16[128,512]{1,0:T(8,128)(2,1)S(1)}, bf16[128,512]{1,0:T(8,128)(2,1)S(1)}, u32[]{:S(2)}, u32[]{:S(2)}) collective-permute-start(bf16[128,512]{1,0:T(8,128)(2,1)S(1)} %get-tuple-element.57.refs_1_), channel_id=1, source_target_pairs={{0,2},{1,3},{4,6},{5,7},{8,10},{9,11},{12,14},{13,15},{16,18},{17,... | collective-permute-start | bytes 393224 | tf_op jit(solution)/shard_map/ppermute | solution.py:453
  21.9 5.1 %collective-permute-start.4 = (bf16[512,128]{1,0:T(8,128)(2,1)S(1)}, bf16[512,128]{1,0:T(8,128)(2,1)S(1)}, u32[]{:S(2)}, u32[]{:S(2)}) collective-permute-start(bf16[512,128]{1,0:T(8,128)(2,1)S(1)} %constant_dynamic-update-slice_fusion.refs_0_), channel_id=1, source_target_pairs={{0,8},{4,12},{8,0},{12,4},{16,24},{20,28},{24,16},{28,20},{1,9},{5... | collective-permute-start | bytes 393224 | tf_op jit(solution)/shard_map/ppermute | solution.py:314
  23.5 5.0 %collective-permute-start.5 = (bf16[512,128]{1,0:T(8,128)(2,1)S(1)}, bf16[512,128]{1,0:T(8,128)(2,1)S(1)}, u32[]{:S(2)}, u32[]{:S(2)}) collective-permute-start(bf16[512,128]{1,0:T(8,128)(2,1)S(1)} %constant_dynamic-update-slice_fusion.refs_0_), channel_id=1, source_target_pairs={{0,16},{4,20},{8,24},{12,28},{16,0},{20,4},{24,8},{28,12},{1,17},{... | collective-permute-start | bytes 393224 | tf_op jit(solution)/shard_map/ppermute | solution.py:314
  25.0 5.9 %collective-permute-start.6 = (bf16[512,128]{1,0:T(8,128)(2,1)S(1)}, bf16[512,128]{1,0:T(8,128)(2,1)S(1)}, u32[]{:S(2)}, u32[]{:S(2)}) collective-permute-start(bf16[512,128]{1,0:T(8,128)(2,1)S(1)} %constant_dynamic-update-slice_fusion.refs_0_), channel_id=1, source_target_pairs={{0,24},{4,28},{8,16},{12,20},{16,8},{20,12},{24,0},{28,4},{1,25},{... | collective-permute-start | bytes 393224 | tf_op jit(solution)/shard_map/ppermute | solution.py:314
  25.6 6.9 %collective-permute-start.2 = (bf16[64,1024]{1,0:T(8,128)(2,1)S(1)}, bf16[64,1024]{1,0:T(8,128)(2,1)S(1)}, u32[]{:S(2)}, u32[]{:S(2)}) collective-permute-start(bf16[64,1024]{1,0:T(8,128)(2,1)S(1)} %get-tuple-element.44), channel_id=1, source_target_pairs={{2,3},{6,7},{10,11},{14,15},{18,19},{22,23},{26,27},{30,31}} | collective-permute-start | bytes 393224 | tf_op jit(solution)/shard_map/ppermute | solution.py:387
  27.1 6.5 %collective-permute-start.7 = (bf16[512,128]{1,0:T(8,128)(2,1)S(1)}, bf16[512,128]{1,0:T(8,128)(2,1)S(1)}, u32[]{:S(2)}, u32[]{:S(2)}) collective-permute-start(bf16[512,128]{1,0:T(8,128)(2,1)S(1)} %constant_dynamic-update-slice_fusion.refs_0_), channel_id=1, source_target_pairs={{0,4},{4,0},{8,12},{12,8},{16,20},{20,16},{24,28},{28,24},{1,5},{5... | collective-permute-start | bytes 393224 | tf_op jit(solution)/shard_map/ppermute | solution.py:314
  28.5 5.8 %collective-permute-start.8 = (bf16[512,128]{1,0:T(8,128)(2,1)S(1)}, bf16[512,128]{1,0:T(8,128)(2,1)S(1)}, u32[]{:S(2)}, u32[]{:S(2)}) collective-permute-start(bf16[512,128]{1,0:T(8,128)(2,1)S(1)} %collective-permute-done.4.refs_1_), channel_id=1, source_target_pairs={{0,4},{4,0},{8,12},{12,8},{16,20},{20,16},{24,28},{28,24},{1,5},{5... | collective-permute-start | bytes 393224 | tf_op jit(solution)/shard_map/ppermute | solution.py:314
  30.9 4.6 %collective-permute-start.9 = (bf16[512,128]{1,0:T(8,128)(2,1)S(1)}, bf16[512,128]{1,0:T(8,128)(2,1)S(1)}, u32[]{:S(2)}, u32[]{:S(2)}) collective-permute-start(bf16[512,128]{1,0:T(8,128)(2,1)S(1)} %collective-permute-done.5.refs_2_), channel_id=1, source_target_pairs={{0,4},{4,0},{8,12},{12,8},{16,20},{20,16},{24,28},{28,24},{1,5},{5... | collective-permute-start | bytes 393224 | tf_op jit(solution)/shard_map/ppermute | solution.py:314
  32.4 4.4 %collective-permute-start.10 = (bf16[512,128]{1,0:T(8,128)(2,1)S(1)}, bf16[512,128]{1,0:T(8,128)(2,1)S(1)}, u32[]{:S(2)}, u32[]{:S(2)}) collective-permute-start(bf16[512,128]{1,0:T(8,128)(2,1)S(1)} %collective-permute-done.6.refs_3_), channel_id=1, source_target_pairs={{0,4},{4,0},{8,12},{12,8},{16,20},{20,16},{24,28},{28,24},{1,5},{5... | collective-permute-start | bytes 393224 | tf_op jit(solution)/shard_map/ppermute | solution.py:314
  33.5 11.1 %collective-permute-start.11 = (bf16[128,512]{1,0:T(8,128)(2,1)S(1)}, bf16[128,512]{1,0:T(8,128)(2,1)S(1)}, u32[]{:S(2)}, u32[]{:S(2)}) collective-permute-start(bf16[128,512]{1,0:T(8,128)(2,1)S(1)} %get-tuple-element.55.refs_1_), channel_id=1, source_target_pairs={{0,1},{4,5},{8,9},{12,13},{16,17},{20,21},{24,25},{28,29}} | collective-permute-start | bytes 393224 | tf_op jit(solution)/shard_map/ppermute | solution.py:453
  34.2 9.7 %collective-permute-start.14 = (bf16[128,512]{1,0:T(8,128)(2,1)S(1)}, bf16[128,512]{1,0:T(8,128)(2,1)S(1)}, u32[]{:S(2)}, u32[]{:S(2)}) collective-permute-start(bf16[128,512]{1,0:T(8,128)(2,1)S(1)} %get-tuple-element.57.refs_1_), channel_id=1, source_target_pairs={{0,3},{1,2},{4,7},{5,6},{8,11},{9,10},{12,15},{13,14},{16,19},{17,... | collective-permute-start | bytes 393224 | tf_op jit(solution)/shard_map/ppermute | solution.py:453
  35.5 10.6 %collective-permute-start.12 = (bf16[128,512]{1,0:T(8,128)(2,1)S(1)}, bf16[128,512]{1,0:T(8,128)(2,1)S(1)}, u32[]{:S(2)}, u32[]{:S(2)}) collective-permute-start(bf16[128,512]{1,0:T(8,128)(2,1)S(1)} %get-tuple-element.59.refs_1_), channel_id=1, source_target_pairs={{2,3},{6,7},{10,11},{14,15},{18,19},{22,23},{26,27},{30,31}} | collective-permute-start | bytes 393224 | tf_op jit(solution)/shard_map/ppermute | solution.py:453

commit v5 on v4

--- a/solution.py
+++ b/solution.py
@@ -1,4 +1,5 @@
 import functools
+import math
 
 import jax
 import jax.numpy as jnp
@@ -250,10 +251,20 @@
                 ]
 
 
+def exact_scale(size):
+    return size ** (-0.5) == 2.0 ** round(math.log2(size ** (-0.5)))
+
+
 def own_kernel(devices, length, rows, weights, groups, query, keys, values, bias):
     most = rows.shape[0]
     own = rows[...]
-    query[...] = dot_lanes(own, weights[0]).astype(BF16)
+    size = weights.shape[1] // devices
+    wanted = dot_lanes(own, weights[0]).astype(BF16).astype(F32)
+    if exact_scale(size):
+        wanted = wanted * size ** (-0.5)
+    even = lax.rem(iota(wanted.shape, 1), 2 * size) < size
+    query[0] = jnp.where(even, wanted, 0.0).astype(BF16)
+    query[1] = jnp.where(even, 0.0, wanted).astype(BF16)
     keys[...] = dot_lanes(weights[1], own).astype(BF16)
     values[...] = dot_lanes(own, weights[2]).astype(BF16)
     me = lax.axis_index("seq")
@@ -289,19 +300,27 @@
     keys, refs = refs[:devices], refs[devices:]
     values, refs = refs[:devices], refs[devices:]
     query, bias, weights, hidden, placing, result = refs
+    most = query.shape[1]
     heads = devices
-    head_dim = query.shape[1] // heads
+    size = query.shape[2] // heads
     known = jnp.concatenate([block[...] for block in keys], axis=1)
     worth = jnp.concatenate([block[...] for block in values], axis=0)
     hide = bias[...]
+    left = iota((most, 2 * size), 1) < size
     outs = []
-    for head in range(heads):
-        lanes = slice(head * head_dim, (head + 1) * head_dim)
-        scores = dot(query[:, lanes], known[lanes, :]) * head_dim ** (-0.5) + hide
-        top = jnp.max(scores, axis=1, keepdims=True)
-        expo = jnp.exp(scores - top)
-        share = 1.0 / jnp.sum(expo, axis=1, keepdims=True)
-        outs.append(dot((expo * share).astype(BF16), worth[:, lanes]).astype(BF16))
+    for at in range(0, heads, 2):
+        lanes = slice(at * size, (at + 2) * size)
+        both = []
+        for side in range(2):
+            scores = dot(query[side, :, lanes], known[lanes, :])
+            if not exact_scale(size):
+                scores = scores * size ** (-0.5)
+            scores = scores + hide
+            top = jnp.max(scores, axis=1, keepdims=True)
+            expo = jnp.exp(scores - top)
+            share = 1.0 / jnp.sum(expo, axis=1, keepdims=True)
+            both.append(dot((expo * share).astype(BF16), worth[:, lanes]))
+        outs.append(jnp.where(left, both[0], both[1]).astype(BF16))
     joined = jnp.concatenate(outs, axis=1)
     back = jnp.concatenate(terms(dot(joined, weights[3]), 2), axis=0)
     place = placing[...]
@@ -456,7 +475,7 @@
     sides = [((inner_width, most), BF16), ((most, inner_width), BF16)]
     query, key, value, bias = call(
         functools.partial(own_kernel, devices, length),
-        [((most, inner_width), BF16)] + sides + [((most, devices * most), F32)],
+        [((2, most, inner_width), BF16)] + sides + [((most, devices * most), F32)],
         [kept[1], weights, groups],
         10**9,
     )

time: 49.4 us -> 49.3 us (level)
  no operation moved by 1% of the time
where the time goes in v5:
time: 49.3 us; the launch traced here: 49 us
  waiting for transfers between devices  23.7 us (48%)
  starting transfers between devices  13.8 us (28%)
  Pallas kernels  11.3 us (23%)
    ppermute x9, waiting for transfers between devices, swap(): return lax.ppermute(value, axis, pairs)  14 us
    pallas_call x14, Pallas kernels, call(): return kernel(*ins)  11.3 us
    ppermute x4, waiting for transfers between devices, shards(): blocks.setdefault(mask, []).append(lax.ppermute(kept[1], 'seq', pairs))  8.09 us
    ppermute x9, starting transfers between devices, swap(): return lax.ppermute(value, axis, pairs)  7.3 us
    ppermute x4, starting transfers between devices, shards(): blocks.setdefault(mask, []).append(lax.ppermute(kept[1], 'seq', pairs))  4.55 us
    ppermute x2, starting transfers between devices, link(): return lax.ppermute(sent, 'seq', pairs)  1.96 us
    ppermute x2, waiting for transfers between devices, link(): return lax.ppermute(sent, 'seq', pairs)  1.54 us
  transfers between devices with their start and end apart: 15, of which 8 were waited for; matrix products, arithmetic and copies ran while one was open for 0% of the time, Pallas kernels for 11%

profile of v5, /device:TPU:24, one launch (start us, length us, event | category | flops | bytes accessed | tf_op | source)
XLA Modules:
  0.0 49.0 jit_solution(17988147725451107453)
XLA Ops:
  0.0 2.8 %shard_map.91 = (bf16[256,1024]{1,0:T(8,128)(2,1)S(1)}, bf16[256,128]{1,0:T(8,128)(2,1)S(1)}, f32[64,1024]{1,0:T(8,128)S(1)}, bf16[80,1024]{1,0:T(8,128)(2,1)S(1...) custom-call(bf16[256,512]{1,0:T(8,128)(2,1)} %tokens.9, f32[16,256]{1,0:T(8,128)} %bitcast.5, bf16[512,2176]{1,0:T(8,128)(2,1)} %weight.3, ...), custom_call_target="tpu_custom_call" | custom-call | flops 3000000000 | tf_op jit(solution)/shard_map/pallas_call | solution.py:350
  2.8 0.5 %collective-permute-start = (bf16[80,1024]{1,0:T(8,128)(2,1)S(1)}, bf16[80,1024]{1,0:T(8,128)(2,1)S(1)}, u32[]{:S(2)}, u32[]{:S(2)}) collective-permute-start(bf16[80,1024]{1,0:T(8,128)(2,1)S(1)} %get-tuple-element.39.first), channel_id=1, source_target_pairs={{0,1},{1,0},{2,3},{3,2},{4,5},{5,4},{6,7},{7,6},{8,9},{9,8},{10,11... | collective-permute-start | bytes 491528 | tf_op jit(solution)/shard_map/ppermute | solution.py:333
  3.4 3.1 %shard_map.94 = (f32[256,1024]{1,0:T(8,128)S(1)}, f32[256,1024]{1,0:T(8,128)S(1)}, f32[256,1024]{1,0:T(8,128)S(1)}, bf16[256,128]{1,0:T(8,128)(2,1)S(1)}, bf16[256,64]{1,0:T(8,128)(2,1)S(1)}) custom-call(bf16[256,512]{1,0:T(8,128)(2,1)S(1)} %copy-done.1, f32[16,256]{1,0:T(8,128)S(1)} %bitcast.6, bf16[512,2176]{1,0:T(8,128)(2,1)} %weight.3, ...), custom_call_target="tpu_custom_call" | custom-call | flops 3000000000 | tf_op jit(solution)/shard_map/pallas_call | solution.py:350
  6.5 2.3 %collective-permute-done.came = bf16[80,1024]{1,0:T(8,128)(2,1)S(1)} collective-permute-done((bf16[80,1024]{1,0:T(8,128)(2,1)S(1)}, bf16[80,1024]{1,0:T(8,128)(2,1)S(1)}, u32[]{:S(2)}, u32[]{:S(2)}) %collective-permute-start) | collective-permute-done | bytes 163872 | tf_op jit(solution)/shard_map/ppermute | solution.py:333
  8.9 0.7 %collective-permute-start.1 = (bf16[64,1024]{1,0:T(8,128)(2,1)S(1)}, bf16[64,1024]{1,0:T(8,128)(2,1)S(1)}, u32[]{:S(2)}, u32[]{:S(2)}) collective-permute-start(bf16[64,1024]{1,0:T(8,128)(2,1)S(1)} %get-tuple-element.42), channel_id=1, source_target_pairs={{1,2},{5,6},{9,10},{13,14},{17,18},{21,22},{25,26},{29,30}} | collective-permute-start | bytes 393224 | tf_op jit(solution)/shard_map/ppermute | solution.py:406
  9.5 3.2 %collective-permute-start.3 = (bf16[256,128]{1,0:T(8,128)(2,1)S(1)}, bf16[256,128]{1,0:T(8,128)(2,1)S(1)}, u32[]{:S(2)}, u32[]{:S(2)}) collective-permute-start(bf16[256,128]{1,0:T(8,128)(2,1)S(1)} %get-tuple-element.61), channel_id=1, source_target_pairs={{0,2},{1,3},{2,0},{3,1},{4,6},{5,7},{6,4},{7,5},{8,10},{9,11},{10,... | collective-permute-start | bytes 196616 | tf_op jit(solution)/shard_map/ppermute | solution.py:333
  12.9 1.3 %collective-permute-start.13 = (bf16[128,512]{1,0:T(8,128)(2,1)S(1)}, bf16[128,512]{1,0:T(8,128)(2,1)S(1)}, u32[]{:S(2)}, u32[]{:S(2)}) collective-permute-start(bf16[128,512]{1,0:T(8,128)(2,1)S(1)} %get-tuple-element.57.refs_1_), channel_id=1, source_target_pairs={{0,2},{1,3},{4,6},{5,7},{8,10},{9,11},{12,14},{13,15},{16,18},{17,... | collective-permute-start | bytes 393224 | tf_op jit(solution)/shard_map/ppermute | solution.py:472
  14.2 7.7 %collective-permute-done.3 = bf16[256,128]{1,0:T(8,128)(2,1)S(1)} collective-permute-done((bf16[256,128]{1,0:T(8,128)(2,1)S(1)}, bf16[256,128]{1,0:T(8,128)(2,1)S(1)}, u32[]{:S(2)}, u32[]{:S(2)}) %collective-permute-start.3) | collective-permute-done | bytes 65568 | tf_op jit(solution)/shard_map/ppermute | solution.py:333
  21.9 1.6 %collective-permute-start.4 = (bf16[512,128]{1,0:T(8,128)(2,1)S(1)}, bf16[512,128]{1,0:T(8,128)(2,1)S(1)}, u32[]{:S(2)}, u32[]{:S(2)}) collective-permute-start(bf16[512,128]{1,0:T(8,128)(2,1)S(1)} %constant_dynamic-update-slice_fusion.refs_0_), channel_id=1, source_target_pairs={{0,8},{4,12},{8,0},{12,4},{16,24},{20,28},{24,16},{28,20},{1,9},{5... | collective-permute-start | bytes 393224 | tf_op jit(solution)/shard_map/ppermute | solution.py:333
  23.5 1.5 %collective-permute-start.5 = (bf16[512,128]{1,0:T(8,128)(2,1)S(1)}, bf16[512,128]{1,0:T(8,128)(2,1)S(1)}, u32[]{:S(2)}, u32[]{:S(2)}) collective-permute-start(bf16[512,128]{1,0:T(8,128)(2,1)S(1)} %constant_dynamic-update-slice_fusion.refs_0_), channel_id=1, source_target_pairs={{0,16},{4,20},{8,24},{12,28},{16,0},{20,4},{24,8},{28,12},{1,17},{... | collective-permute-start | bytes 393224 | tf_op jit(solution)/shard_map/ppermute | solution.py:333
  25.0 0.5 collective-permute-start.6
  25.6 1.3 %collective-permute-start.2 = (bf16[64,1024]{1,0:T(8,128)(2,1)S(1)}, bf16[64,1024]{1,0:T(8,128)(2,1)S(1)}, u32[]{:S(2)}, u32[]{:S(2)}) collective-permute-start(bf16[64,1024]{1,0:T(8,128)(2,1)S(1)} %get-tuple-element.44), channel_id=1, source_target_pairs={{2,3},{6,7},{10,11},{14,15},{18,19},{22,23},{26,27},{30,31}} | collective-permute-start | bytes 393224 | tf_op jit(solution)/shard_map/ppermute | solution.py:406
  27.1 1.4 %collective-permute-done.5.refs_2_ = bf16[512,128]{1,0:T(8,128)(2,1)S(1)} collective-permute-done((bf16[512,128]{1,0:T(8,128)(2,1)S(1)}, bf16[512,128]{1,0:T(8,128)(2,1)S(1)}, u32[]{:S(2)}, u32[]{:S(2)}) %collective-permute-start.5) | collective-permute-done | bytes 131104 | tf_op jit(solution)/shard_map/ppermute | solution.py:333
  28.5 2.4 %collective-permute-done.6.refs_3_ = bf16[512,128]{1,0:T(8,128)(2,1)S(1)} collective-permute-done((bf16[512,128]{1,0:T(8,128)(2,1)S(1)}, bf16[512,128]{1,0:T(8,128)(2,1)S(1)}, u32[]{:S(2)}, u32[]{:S(2)}) %collective-permute-start.6) | collective-permute-done | bytes 131104 | tf_op jit(solution)/shard_map/ppermute | solution.py:333
  30.9 1.5 %collective-permute-done.2.state = bf16[64,1024]{1,0:T(8,128)(2,1)S(1)} collective-permute-done((bf16[64,1024]{1,0:T(8,128)(2,1)S(1)}, bf16[64,1024]{1,0:T(8,128)(2,1)S(1)}, u32[]{:S(2)}, u32[]{:S(2)}) %collective-permute-start.2) | collective-permute-done | bytes 131104 | tf_op jit(solution)/shard_map/ppermute | solution.py:406
  32.4 1.1 %shard_map.98 = (bf16[256,512]{1,0:T(8,128)(2,1)S(1)}, bf16[128,512]{1,0:T(8,128)(2,1)S(1)}) custom-call(bf16[64,1024]{1,0:T(8,128)(2,1)S(1)} %collective-permute-done.2.state, f32[256,1024]{1,0:T(8,128)S(1)} %get-tuple-element.48.within, f32[256,1024]{1,0:T(8,128)S(1)} %get-tuple-element.49.silu, f32[256,1024]{1,0:T(8,128)S(1)} %get-tuple-element.50.grown, ...), custom_call_target="tpu_custom_call" | custom-call | flops 2000000000 | tf_op jit(solution)/shard_map/pallas_call | solution.py:350
  33.5 0.7 %collective-permute-start.11 = (bf16[128,512]{1,0:T(8,128)(2,1)S(1)}, bf16[128,512]{1,0:T(8,128)(2,1)S(1)}, u32[]{:S(2)}, u32[]{:S(2)}) collective-permute-start(bf16[128,512]{1,0:T(8,128)(2,1)S(1)} %get-tuple-element.55.refs_1_), channel_id=1, source_target_pairs={{0,1},{4,5},{8,9},{12,13},{16,17},{20,21},{24,25},{28,29}} | collective-permute-start | bytes 393224 | tf_op jit(solution)/shard_map/ppermute | solution.py:472
  34.2 1.3 %collective-permute-start.14 = (bf16[128,512]{1,0:T(8,128)(2,1)S(1)}, bf16[128,512]{1,0:T(8,128)(2,1)S(1)}, u32[]{:S(2)}, u32[]{:S(2)}) collective-permute-start(bf16[128,512]{1,0:T(8,128)(2,1)S(1)} %get-tuple-element.57.refs_1_), channel_id=1, source_target_pairs={{0,3},{1,2},{4,7},{5,6},{8,11},{9,10},{12,15},{13,14},{16,19},{17,... | collective-permute-start | bytes 393224 | tf_op jit(solution)/shard_map/ppermute | solution.py:472
  35.5 1.3 %collective-permute-start.12 = (bf16[128,512]{1,0:T(8,128)(2,1)S(1)}, bf16[128,512]{1,0:T(8,128)(2,1)S(1)}, u32[]{:S(2)}, u32[]{:S(2)}) collective-permute-start(bf16[128,512]{1,0:T(8,128)(2,1)S(1)} %get-tuple-element.59.refs_1_), channel_id=1, source_target_pairs={{2,3},{6,7},{10,11},{14,15},{18,19},{22,23},{26,27},{30,31}} | collective-permute-start | bytes 393224 | tf_op jit(solution)/shard_map/ppermute | solution.py:472
  37.1 0.3 shard_map.102
  37.4 6.6 %collective-permute-done.14.refs_0_ = bf16[128,512]{1,0:T(8,128)(2,1)S(1)} collective-permute-done((bf16[128,512]{1,0:T(8,128)(2,1)S(1)}, bf16[128,512]{1,0:T(8,128)(2,1)S(1)}, u32[]{:S(2)}, u32[]{:S(2)}) %collective-permute-start.14) | collective-permute-done | bytes 131104 | tf_op jit(solution)/shard_map/ppermute | solution.py:472
  44.2 0.4 shard_map.100
  44.6 1.5 %collective-permute-done.12.refs_1_ = bf16[128,512]{1,0:T(8,128)(2,1)S(1)} collective-permute-done((bf16[128,512]{1,0:T(8,128)(2,1)S(1)}, bf16[128,512]{1,0:T(8,128)(2,1)S(1)}, u32[]{:S(2)}, u32[]{:S(2)}) %collective-permute-start.12) | collective-permute-done | bytes 131104 | tf_op jit(solution)/shard_map/ppermute | solution.py:472
  46.5 2.6 %shard_map.104 = bf16[256,512]{1,0:T(8,128)(2,1)} custom-call(bf16[256,128]{1,0:T(8,128)(2,1)S(1)} %get-tuple-element.62.refs_0_, bf16[256,128]{1,0:T(8,128)(2,1)S(1)} %get-tuple-element.63.refs_1_, bf16[256,128]{1,0:T(8,128)(2,1)S(1)} %get-tuple-element.64.refs_2_, bf16[256,128]{1,0:T(8,128)(2,1)S(1)} %get-tuple-element.65.refs_3_, ...), custom_call_target="tpu_custom_call" | custom-call | flops 2000000000 | tf_op jit(solution)/shard_map/pallas_call | solution.py:350
  (34 shorter events, 1.3 us)
Async XLA Ops:
  0.0 3.3 %copy-start.1 = (bf16[256,512]{1,0:T(8,128)(2,1)S(1)}, bf16[256,512]{1,0:T(8,128)(2,1)}, u32[]{:S(2)}) copy-start(bf16[256,512]{1,0:T(8,128)(2,1)} %tokens.9) | copy-start | bytes 786436
  0.0 3.3 %copy-start.2 = (f32[256,16]{0,1:T(8,128)S(1)}, f32[256,16]{0,1:T(8,128)}, u32[]{:S(2)}) copy-start(f32[256,16]{0,1:T(8,128)} %param.11) | copy-start | bytes 49156
  0.0 3.3 %copy-start.5 = (s32[256]{0:T(256)S(1)}, s32[256]{0:T(256)}, u32[]{:S(2)}) copy-start(s32[256]{0:T(256)} %param.10) | copy-start | bytes 3076
  2.8 6.0 %collective-permute-start = (bf16[80,1024]{1,0:T(8,128)(2,1)S(1)}, bf16[80,1024]{1,0:T(8,128)(2,1)S(1)}, u32[]{:S(2)}, u32[]{:S(2)}) collective-permute-start(bf16[80,1024]{1,0:T(8,128)(2,1)S(1)} %get-tuple-element.39.first), channel_id=1, source_target_pairs={{0,1},{1,0},{2,3},{3,2},{4,5},{5,4},{6,7},{7,6},{8,9},{9,8},{10,11... | collective-permute-start | bytes 491528 | tf_op jit(solution)/shard_map/ppermute | solution.py:333
  3.3 9.4 %copy-start = (bf16[1024,512]{1,0:T(8,128)(2,1)S(1)}, bf16[1024,512]{1,0:T(8,128)(2,1)}, u32[]{:S(2)}) copy-start(bf16[1024,512]{1,0:T(8,128)(2,1)} %out_weight.7) | copy-start | bytes 3145732
  3.3 9.4 %copy-start.3 = (f32[1024]{0:T(1024)S(1)}, f32[1024]{0:T(1024)}, u32[]{:S(2)}) copy-start(f32[1024]{0:T(1024)} %param.13) | copy-start | bytes 12292
  3.3 9.4 %copy-start.4 = (f32[512]{0:T(512)S(1)}, f32[512]{0:T(512)}, u32[]{:S(2)}) copy-start(f32[512]{0:T(512)} %param.15) | copy-start | bytes 6148
  8.9 16.6 %collective-permute-start.1 = (bf16[64,1024]{1,0:T(8,128)(2,1)S(1)}, bf16[64,1024]{1,0:T(8,128)(2,1)S(1)}, u32[]{:S(2)}, u32[]{:S(2)}) collective-permute-start(bf16[64,1024]{1,0:T(8,128)(2,1)S(1)} %get-tuple-element.42), channel_id=1, source_target_pairs={{1,2},{5,6},{9,10},{13,14},{17,18},{21,22},{25,26},{29,30}} | collective-permute-start | bytes 393224 | tf_op jit(solution)/shard_map/ppermute | solution.py:406
  9.5 12.4 %collective-permute-start.3 = (bf16[256,128]{1,0:T(8,128)(2,1)S(1)}, bf16[256,128]{1,0:T(8,128)(2,1)S(1)}, u32[]{:S(2)}, u32[]{:S(2)}) collective-permute-start(bf16[256,128]{1,0:T(8,128)(2,1)S(1)} %get-tuple-element.61), channel_id=1, source_target_pairs={{0,2},{1,3},{2,0},{3,1},{4,6},{5,7},{6,4},{7,5},{8,10},{9,11},{10,... | collective-permute-start | bytes 196616 | tf_op jit(solution)/shard_map/ppermute | solution.py:333
  12.9 24.2 %collective-permute-start.13 = (bf16[128,512]{1,0:T(8,128)(2,1)S(1)}, bf16[128,512]{1,0:T(8,128)(2,1)S(1)}, u32[]{:S(2)}, u32[]{:S(2)}) collective-permute-start(bf16[128,512]{1,0:T(8,128)(2,1)S(1)} %get-tuple-element.57.refs_1_), channel_id=1, source_target_pairs={{0,2},{1,3},{4,6},{5,7},{8,10},{9,11},{12,14},{13,15},{16,18},{17,... | collective-permute-start | bytes 393224 | tf_op jit(solution)/shard_map/ppermute | solution.py:472
  21.9 5.1 %collective-permute-start.4 = (bf16[512,128]{1,0:T(8,128)(2,1)S(1)}, bf16[512,128]{1,0:T(8,128)(2,1)S(1)}, u32[]{:S(2)}, u32[]{:S(2)}) collective-permute-start(bf16[512,128]{1,0:T(8,128)(2,1)S(1)} %constant_dynamic-update-slice_fusion.refs_0_), channel_id=1, source_target_pairs={{0,8},{4,12},{8,0},{12,4},{16,24},{20,28},{24,16},{28,20},{1,9},{5... | collective-permute-start | bytes 393224 | tf_op jit(solution)/shard_map/ppermute | solution.py:333
  23.5 5.0 %collective-permute-start.5 = (bf16[512,128]{1,0:T(8,128)(2,1)S(1)}, bf16[512,128]{1,0:T(8,128)(2,1)S(1)}, u32[]{:S(2)}, u32[]{:S(2)}) collective-permute-start(bf16[512,128]{1,0:T(8,128)(2,1)S(1)} %constant_dynamic-update-slice_fusion.refs_0_), channel_id=1, source_target_pairs={{0,16},{4,20},{8,24},{12,28},{16,0},{20,4},{24,8},{28,12},{1,17},{... | collective-permute-start | bytes 393224 | tf_op jit(solution)/shard_map/ppermute | solution.py:333
  25.0 5.9 %collective-permute-start.6 = (bf16[512,128]{1,0:T(8,128)(2,1)S(1)}, bf16[512,128]{1,0:T(8,128)(2,1)S(1)}, u32[]{:S(2)}, u32[]{:S(2)}) collective-permute-start(bf16[512,128]{1,0:T(8,128)(2,1)S(1)} %constant_dynamic-update-slice_fusion.refs_0_), channel_id=1, source_target_pairs={{0,24},{4,28},{8,16},{12,20},{16,8},{20,12},{24,0},{28,4},{1,25},{... | collective-permute-start | bytes 393224 | tf_op jit(solution)/shard_map/ppermute | solution.py:333
  25.6 6.9 %collective-permute-start.2 = (bf16[64,1024]{1,0:T(8,128)(2,1)S(1)}, bf16[64,1024]{1,0:T(8,128)(2,1)S(1)}, u32[]{:S(2)}, u32[]{:S(2)}) collective-permute-start(bf16[64,1024]{1,0:T(8,128)(2,1)S(1)} %get-tuple-element.44), channel_id=1, source_target_pairs={{2,3},{6,7},{10,11},{14,15},{18,19},{22,23},{26,27},{30,31}} | collective-permute-start | bytes 393224 | tf_op jit(solution)/shard_map/ppermute | solution.py:406
  27.1 6.5 %collective-permute-start.7 = (bf16[512,128]{1,0:T(8,128)(2,1)S(1)}, bf16[512,128]{1,0:T(8,128)(2,1)S(1)}, u32[]{:S(2)}, u32[]{:S(2)}) collective-permute-start(bf16[512,128]{1,0:T(8,128)(2,1)S(1)} %constant_dynamic-update-slice_fusion.refs_0_), channel_id=1, source_target_pairs={{0,4},{4,0},{8,12},{12,8},{16,20},{20,16},{24,28},{28,24},{1,5},{5... | collective-permute-start | bytes 393224 | tf_op jit(solution)/shard_map/ppermute | solution.py:333
  28.5 5.8 %collective-permute-start.8 = (bf16[512,128]{1,0:T(8,128)(2,1)S(1)}, bf16[512,128]{1,0:T(8,128)(2,1)S(1)}, u32[]{:S(2)}, u32[]{:S(2)}) collective-permute-start(bf16[512,128]{1,0:T(8,128)(2,1)S(1)} %collective-permute-done.4.refs_1_), channel_id=1, source_target_pairs={{0,4},{4,0},{8,12},{12,8},{16,20},{20,16},{24,28},{28,24},{1,5},{5... | collective-permute-start | bytes 393224 | tf_op jit(solution)/shard_map/ppermute | solution.py:333
  30.9 4.6 %collective-permute-start.9 = (bf16[512,128]{1,0:T(8,128)(2,1)S(1)}, bf16[512,128]{1,0:T(8,128)(2,1)S(1)}, u32[]{:S(2)}, u32[]{:S(2)}) collective-permute-start(bf16[512,128]{1,0:T(8,128)(2,1)S(1)} %collective-permute-done.5.refs_2_), channel_id=1, source_target_pairs={{0,4},{4,0},{8,12},{12,8},{16,20},{20,16},{24,28},{28,24},{1,5},{5... | collective-permute-start | bytes 393224 | tf_op jit(solution)/shard_map/ppermute | solution.py:333
  32.4 4.4 %collective-permute-start.10 = (bf16[512,128]{1,0:T(8,128)(2,1)S(1)}, bf16[512,128]{1,0:T(8,128)(2,1)S(1)}, u32[]{:S(2)}, u32[]{:S(2)}) collective-permute-start(bf16[512,128]{1,0:T(8,128)(2,1)S(1)} %collective-permute-done.6.refs_3_), channel_id=1, source_target_pairs={{0,4},{4,0},{8,12},{12,8},{16,20},{20,16},{24,28},{28,24},{1,5},{5... | collective-permute-start | bytes 393224 | tf_op jit(solution)/shard_map/ppermute | solution.py:333
  33.5 11.1 %collective-permute-start.11 = (bf16[128,512]{1,0:T(8,128)(2,1)S(1)}, bf16[128,512]{1,0:T(8,128)(2,1)S(1)}, u32[]{:S(2)}, u32[]{:S(2)}) collective-permute-start(bf16[128,512]{1,0:T(8,128)(2,1)S(1)} %get-tuple-element.55.refs_1_), channel_id=1, source_target_pairs={{0,1},{4,5},{8,9},{12,13},{16,17},{20,21},{24,25},{28,29}} | collective-permute-start | bytes 393224 | tf_op jit(solution)/shard_map/ppermute | solution.py:472
  34.2 9.7 %collective-permute-start.14 = (bf16[128,512]{1,0:T(8,128)(2,1)S(1)}, bf16[128,512]{1,0:T(8,128)(2,1)S(1)}, u32[]{:S(2)}, u32[]{:S(2)}) collective-permute-start(bf16[128,512]{1,0:T(8,128)(2,1)S(1)} %get-tuple-element.57.refs_1_), channel_id=1, source_target_pairs={{0,3},{1,2},{4,7},{5,6},{8,11},{9,10},{12,15},{13,14},{16,19},{17,... | collective-permute-start | bytes 393224 | tf_op jit(solution)/shard_map/ppermute | solution.py:472
  35.5 10.6 %collective-permute-start.12 = (bf16[128,512]{1,0:T(8,128)(2,1)S(1)}, bf16[128,512]{1,0:T(8,128)(2,1)S(1)}, u32[]{:S(2)}, u32[]{:S(2)}) collective-permute-start(bf16[128,512]{1,0:T(8,128)(2,1)S(1)} %get-tuple-element.59.refs_1_), channel_id=1, source_target_pairs={{2,3},{6,7},{10,11},{14,15},{18,19},{22,23},{26,27},{30,31}} | collective-permute-start | bytes 393224 | tf_op jit(solution)/shard_map/ppermute | solution.py:472
